TPU v7x, 32 devices: a whole 2x2x4 slice. The times are simulated.
32 devices in a mesh: row: 4 (over y, x), col: 8 (over z, core).
Axes of the slice: x: 2, y: 2, z: 4, core: 2. Of those that a mesh axis runs over, the one named last changes fastest.
Arguments:
- pixels_tokens: bfloat16 [4, 2304, 5120], P(None, 'col', 'row'), may hold values from -12 to 12, as said below
- ln_gain: float32 [5120], replicated, may hold values from 0.1 to 1.9
- ln_bias: float32 [5120], replicated, may hold values from -3 to 3
- w_qkv: bfloat16 [5120, 6144], P('col', 'row'), may hold values from -1 to 1, as said below
- w_out: bfloat16 [2048, 5120], P('col', 'row'), may hold values from -0.125 to 0.125
Outputs:
- block_out: bfloat16 [4, 2304, 5120], P(None, 'col', 'row')
Inputs may be any that keep to these rules, and one draw needn't show every extreme that they name: `pixels_tokens`: activations of order one. `w_qkv`: projection entries scaled by the width.
All inputs are finite; a program needn't handle non-finite values.
Results may differ from a plain program's by a relative error of at most 0.012.
The roundings to bfloat16 on the way count: a program that leaves them out, or rounds other values in their place, can miss the bound.
Values may be sent and summed in bfloat16 or wider, within the bound.
No kernel may reach another device: no remote copies, remote signals or barrier semaphores. Data moves between devices by JAX's collectives and lax.ppermute only.
A program may use at most 128 MiB of HBM per device.

v0:
```python
import functools

import jax
import jax.numpy as jnp
from jax import lax
from jax.experimental import pallas as pl
from jax.experimental.pallas import tpu as pltpu
from jax.sharding import PartitionSpec as P

HDIM = 128
CHUNKS = 2
ANY = pl.BlockSpec(memory_space=pl.ANY)
VMEM = pl.BlockSpec(memory_space=pltpu.VMEM)


def ring(images, parts, step):
    return [
        (a * parts + b, ((a + step) % images) * parts + b)
        for a in range(images)
        for b in range(parts)
    ]


def group(images, parts, step):
    return [
        (a * parts + b, a * parts + (b + step) % parts)
        for a in range(images)
        for b in range(parts)
    ]


def tile_of(rows, limit):
    return max(t for t in range(16, limit + 1, 16) if rows % t == 0)


def cost(flops, moved, exps=0):
    return pl.CostEstimate(flops=flops, bytes_accessed=moved, transcendentals=exps)


def spread(block, rows, dims):
    pieces, n = [(0, block)], 0
    for d in dims:
        perm = [(a, a ^ d) for a in range(rows)]
        for m, b in list(pieces):
            pieces.append((m ^ d, lax.ppermute(b, "row", perm)))
            n += 1
    return pieces


def norm_kernel(masks, images, parts, gain_ref, bias_ref, *refs):
    pieces, out_ref = refs[: len(masks)], refs[-1]
    me = lax.axis_index("row")
    image = lax.axis_index("col") // parts
    width = pieces[0].shape[1]
    span = out_ref.shape[3]
    grain = min(width, span)
    total = width * len(pieces)
    floats = [ref[...].astype(jnp.float32) for ref in pieces]
    center = sum(jnp.sum(f, axis=-1, keepdims=True) for f in floats) / total
    floats = [f - center for f in floats]
    scatter = sum(jnp.sum(f * f, axis=-1, keepdims=True) for f in floats) / total
    scale = lax.rsqrt(scatter + 1e-06)
    for mask, f in zip(masks, floats):
        for part in range(width // grain):
            first = (me ^ mask) * width + part * grain
            at = pl.ds(pl.multiple_of(first, 128), grain)
            step = (image + images - first // span) % images
            to = pl.ds(pl.multiple_of(first % span, 128), grain)
            value = f[:, part * grain : (part + 1) * grain] * scale
            out_ref[0, step, :, to] = (value * gain_ref[:, at] + bias_ref[:, at]).astype(
                out_ref.dtype
            )


def normalize(k, held, pieces, gain, bias, images, parts):
    masks = [m for m, _ in pieces]
    rows, width = pieces[0][1].shape
    total = width * len(pieces)
    tile = tile_of(rows, 48)
    shape = (images, images, rows, total // images)
    whole = pl.BlockSpec((1, total), lambda t: (0, 0))
    extra = [] if held is None else [held]
    return pl.pallas_call(
        functools.partial(norm_kernel, masks, images, parts),
        grid=(rows // tile,),
        in_specs=[whole, whole]
        + [pl.BlockSpec((tile, width), lambda t: (t, 0))] * len(pieces)
        + [ANY] * len(extra),
        out_specs=pl.BlockSpec((1, images, tile, total // images), lambda t: (k, 0, t, 0)),
        out_shape=jax.ShapeDtypeStruct(shape, jnp.bfloat16),
        input_output_aliases={2 + len(pieces): 0} if extra else {},
        cost_estimate=cost(8 * rows * total, 4 * rows * total, rows),
        name="norm",
    )(gain[None], bias[None], *[b for _, b in pieces], *extra)


def piece_copies(w_refs, tags, parts, w_v, sems):
    part = lax.axis_index("col") % parts
    copies = []
    for n, (step, turn) in enumerate(tags):
        depth = w_refs[n].shape[0]
        at = pl.multiple_of(((part + parts - turn) % parts) * depth, 16)
        copies.append(
            pltpu.make_async_copy(w_refs[n], w_v.at[pl.ds(step * parts * depth + at, depth)], sems.at[n])
        )
    return copies


def early_kernel(steps, parts, tags, x_ref, *refs):
    w_refs = refs[: len(tags)]
    out_ref, x_v, w_v, o_v, x_sem, w_sem, o_sem = refs[len(tags) :]
    images, _, _, span = x_ref.shape
    half = w_v.shape[1] // CHUNKS
    copies = piece_copies(w_refs, tags, parts, w_v, w_sem)
    loads = [
        [
            pltpu.make_async_copy(
                x_ref.at[k, s], x_v.at[k, :, pl.ds(s * span, span)], x_sem.at[k, s]
            )
            for s in range(steps)
        ]
        for k in range(images)
    ]
    for copy in copies:
        copy.start()
    for block in loads:
        for load in block:
            load.start()
    for copy in copies:
        copy.wait()
    stores = []
    for k in range(images):
        for load in loads[k]:
            load.wait()
        for n in range(CHUNKS):
            m = k * CHUNKS + n
            slot = m % 2
            if m >= 2:
                stores[m - 2].wait()
            o_v[slot] = jnp.dot(
                x_v[k], w_v[:, n * half : (n + 1) * half], preferred_element_type=jnp.float32
            )
            store = pltpu.make_async_copy(o_v.at[slot], out_ref.at[n, k], o_sem.at[slot])
            store.start()
            stores.append(store)
    for store in stores[-2:]:
        store.wait()


def project_early(normed, pieces, parts):
    images, _, rows, span = normed.shape
    columns = pieces[0][2].shape[1]
    tags = [(s, t) for s, t, _ in pieces]
    steps = images - 1
    half = columns // CHUNKS
    tokens = images * rows
    return pl.pallas_call(
        functools.partial(early_kernel, steps, parts, tags),
        in_specs=[ANY] * (1 + len(pieces)),
        out_specs=ANY,
        out_shape=jax.ShapeDtypeStruct((CHUNKS, images, rows, half), jnp.float32),
        scratch_shapes=[
            pltpu.VMEM((images, rows, steps * span), jnp.bfloat16),
            pltpu.VMEM((steps * span, columns), jnp.bfloat16),
            pltpu.VMEM((2, rows, half), jnp.float32),
            pltpu.SemaphoreType.DMA((images, steps)),
            pltpu.SemaphoreType.DMA((len(pieces),)),
            pltpu.SemaphoreType.DMA((2,)),
        ],
        cost_estimate=cost(2 * tokens * steps * span * columns, 2 * tokens * span * steps),
        name="early",
    )(normed, *[w for _, _, w in pieces])


def late_kernel(chunk, parts, heads, tags, x_ref, acc_ref, *refs):
    w_refs = refs[: len(tags)]
    q_ref, kv_ref, x_v, a_v, w_v, x_sem, a_sem, w_sem = refs[len(tags) :]
    images, _, rows, _ = x_ref.shape
    copies = piece_copies(w_refs, [(0, t) for _, t in tags], parts, w_v, w_sem)
    loads = [
        (
            pltpu.make_async_copy(x_ref.at[k, images - 1], x_v.at[k], x_sem.at[k]),
            pltpu.make_async_copy(acc_ref.at[chunk, k], a_v.at[k], a_sem.at[k]),
        )
        for k in range(images)
    ]
    for copy in copies:
        copy.start()
    for pair in loads:
        for load in pair:
            load.start()
    for copy in copies:
        copy.wait()
    for k in range(images):
        for load in loads[k]:
            load.wait()
        got = a_v[k] + jnp.dot(x_v[k], w_v[...], preferred_element_type=jnp.float32)
        got = got.astype(jnp.bfloat16)
        own = pl.ds(k * rows, rows)
        for h in range(heads):
            at = 3 * HDIM * h
            q_ref[own, h * HDIM : (h + 1) * HDIM] = got[:, at : at + HDIM]
            kv_ref[own, 2 * h * HDIM : 2 * (h + 1) * HDIM] = got[:, at + HDIM : at + 3 * HDIM]


def project_late(chunk, normed, acc, pieces, parts):
    images, _, rows, span = normed.shape
    columns = pieces[0][2].shape[1]
    heads = columns // (3 * HDIM)
    tags = [(s, t) for s, t, _ in pieces]
    tokens = images * rows
    return pl.pallas_call(
        functools.partial(late_kernel, chunk, parts, heads, tags),
        in_specs=[ANY] * (2 + len(pieces)),
        out_specs=[VMEM, VMEM],
        out_shape=[
            jax.ShapeDtypeStruct((tokens, heads * HDIM), jnp.bfloat16),
            jax.ShapeDtypeStruct((tokens, 2 * heads * HDIM), jnp.bfloat16),
        ],
        scratch_shapes=[
            pltpu.VMEM((images, rows, span), jnp.bfloat16),
            pltpu.VMEM((images, rows, columns), jnp.float32),
            pltpu.VMEM((span, columns), jnp.bfloat16),
            pltpu.SemaphoreType.DMA((images,)),
            pltpu.SemaphoreType.DMA((images,)),
            pltpu.SemaphoreType.DMA((len(pieces),)),
        ],
        cost_estimate=cost(2 * tokens * span * columns, 8 * tokens * columns),
        name="late",
    )(normed, acc, *[w for _, _, w in pieces])


def attend_kernel(images, heads, q_ref, *refs):
    kv_refs, out_refs = refs[:-images], refs[-images:]
    rows = out_refs[0].shape[0]
    scale = HDIM ** (-0.5)

    def block(k, carry):
        own = pl.ds(pl.multiple_of(k * rows, 16), rows)
        for h in range(heads):
            query = q_ref[own, h * HDIM : (h + 1) * HDIM]
            scores = [
                lax.dot_general(
                    query,
                    ref[:, 2 * h * HDIM : (2 * h + 1) * HDIM],
                    (((1,), (1,)), ((), ())),
                    preferred_element_type=jnp.float32,
                )
                * scale
                for ref in kv_refs
            ]
            peak = functools.reduce(
                jnp.maximum, [jnp.max(s, axis=-1, keepdims=True) for s in scores]
            )
            expo = [jnp.exp(s - peak) for s in scores]
            inverse = 1.0 / sum(jnp.sum(e, axis=-1, keepdims=True) for e in expo)
            got = sum(
                jnp.dot(
                    (e * inverse).astype(jnp.bfloat16),
                    ref[:, (2 * h + 1) * HDIM : 2 * (h + 1) * HDIM],
                    preferred_element_type=jnp.float32,
                )
                for e, ref in zip(expo, kv_refs)
            ).astype(jnp.bfloat16)
            for n in range(images):

                @pl.when(k == n)
                def _(n=n, h=h, got=got):
                    out_refs[n][:, h * HDIM : (h + 1) * HDIM] = got

        return carry

    lax.fori_loop(0, images, block, 0)


def attend(query, pairs, images):
    tokens, wide = query.shape
    rows, heads = tokens // images, wide // HDIM
    keys = tokens * len(pairs)
    return pl.pallas_call(
        functools.partial(attend_kernel, images, heads),
        in_specs=[VMEM] * (1 + len(pairs)),
        out_specs=[VMEM] * images,
        out_shape=[jax.ShapeDtypeStruct((rows, wide), jnp.bfloat16)] * images,
        cost_estimate=cost(
            8 * heads * tokens * keys * HDIM,
            4 * heads * HDIM * (tokens + keys),
            heads * tokens * keys,
        ),
        name="attend",
    )(query, *pairs)


def out_kernel(images, parts, head_row, begin, count, o_tags, w_tags, *refs):
    o_refs = refs[: len(o_tags)]
    refs = refs[len(o_tags) :]
    w_refs = refs[: len(w_tags)]
    base_ref, out_ref, o_v, w_v, o_sem, w_sem = refs[len(w_tags) :]
    me = lax.axis_index("row")
    col = lax.axis_index("col")
    image, part = col // parts, col % parts
    depth = w_refs[0].shape[0]
    copies = []
    for n, (step, turn) in enumerate(w_tags):
        place = ((image + images - step) % images) * parts + (part + parts - turn) % parts
        at = pl.multiple_of(place * depth, 16)
        copies.append(pltpu.make_async_copy(w_refs[n], w_v.at[pl.ds(at, depth)], w_sem.at[n]))
    for n, (first, mask) in enumerate(o_tags):
        to = o_v.at[me ^ mask, pl.ds(first, o_refs[n].shape[0])]
        copies.append(pltpu.make_async_copy(o_refs[n], to, o_sem.at[n]))
    for copy in copies:
        copy.start()
    for copy in copies:
        copy.wait()
    rows = out_ref.shape[1]
    w_all = jnp.concatenate(
        [
            w_v[(r * head_row + begin) * HDIM : (r * head_row + begin + count) * HDIM, :]
            for r in range(o_v.shape[0])
        ],
        axis=0,
    )
    for k in range(images):
        at = (image + k) % images
        o_all = jnp.concatenate(
            [o_v[r, k * rows : (k + 1) * rows, :] for r in range(o_v.shape[0])], axis=1
        )
        got = jnp.dot(o_all, w_all, preferred_element_type=jnp.float32)
        out_ref[at] = (base_ref[at].astype(jnp.float32) + got).astype(out_ref.dtype)


def project_out(base, o_pieces, w_pieces, parts, head_row, row_count, begin, kind):
    o_tags = [(f, m) for f, m, _ in o_pieces]
    w_tags = [(s, t) for s, t, _ in w_pieces]
    images, rows, columns = base.shape
    width = o_pieces[0][2].shape[1]
    deep = len(w_pieces) * w_pieces[0][2].shape[0]
    return pl.pallas_call(
        functools.partial(
            out_kernel, images, parts, head_row, begin, width // HDIM, o_tags, w_tags
        ),
        in_specs=[ANY] * (len(o_tags) + len(w_tags)) + [VMEM],
        out_specs=VMEM,
        out_shape=jax.ShapeDtypeStruct(base.shape, kind),
        scratch_shapes=[
            pltpu.VMEM((row_count, images * rows, width), jnp.bfloat16),
            pltpu.VMEM((deep, columns), jnp.bfloat16),
            pltpu.SemaphoreType.DMA((len(o_tags),)),
            pltpu.SemaphoreType.DMA((len(w_tags),)),
        ],
        cost_estimate=cost(
            2 * images * rows * columns * width * row_count, 8 * images * rows * columns
        ),
        name="out",
    )(*[o for _, _, o in o_pieces], *[w for _, _, w in w_pieces], base)


def local(pixels_tokens, ln_gain, ln_bias, w_qkv, w_out):
    images, rows, _ = pixels_tokens.shape
    row_count = lax.axis_size("row")
    col_count = lax.axis_size("col")
    parts = col_count // images
    head_row = w_qkv.shape[1] // (3 * HDIM)
    heads = head_row // CHUNKS
    image = lax.axis_index("col") // parts
    dims = [1 << n for n in range(row_count.bit_length() - 1)]

    def around(value, step):
        if step % images == 0:
            return value
        return lax.ppermute(value, "col", ring(images, parts, step))

    def swaps(step, shard):
        return [(step, 0, shard)] + [
            (step, t, lax.ppermute(shard, "col", group(images, parts, t)))
            for t in range(1, parts)
        ]

    blocks = []
    for k in range(images):
        block = lax.dynamic_index_in_dim(pixels_tokens, (image + k) % images, 0, keepdims=False)
        blocks.append(around(block, k))
    normed = None
    for k in ORDER(images):
        turned = dims[k % len(dims) :] + dims[: k % len(dims)]
        pieces = spread(blocks[k], row_count, turned)
        normed = normalize(k, normed, pieces, ln_gain, ln_bias, images, parts)

    shard, early = w_qkv, []
    for step in range(images - 1):
        early += swaps(step, shard)
        if step + 2 < images:
            shard = around(shard, 1)
    acc = project_early(normed, early, parts)
    chunk_columns = heads * 3 * HDIM
    results = []
    for j in range(CHUNKS):
        last = shard[:, j * chunk_columns : (j + 1) * chunk_columns]
        last = around(last, 1)
        query, pair = project_late(j, normed, acc, swaps(images - 1, last), parts)
        pairs = [pair] + [
            lax.ppermute(pair, "col", group(images, parts, t)) for t in range(1, parts)
        ]
        outs = attend(query, pairs, images)
        outs = [around(o, -k) for k, o in enumerate(outs)]
        half = images // 2
        pieces = []
        for n in range(2):
            joined = jnp.concatenate(outs[n * half : (n + 1) * half], axis=0)
            turned = dims[n:] + dims[:n]
            pieces += [(n * half * rows, m, b) for m, b in spread(joined, row_count, turned)]
        results.append(pieces)

    shard, out_pieces = w_out, []
    for step in range(images):
        out_pieces += swaps(step, shard)
        if step + 1 < images:
            shard = around(shard, 1)
    total = pixels_tokens
    for j, pieces in enumerate(results):
        kind = jnp.float32 if j + 1 < CHUNKS else jnp.bfloat16
        total = project_out(total, pieces, out_pieces, parts, head_row, row_count, j * heads, kind)
    return total


def ORDER(images):
    return sorted(range(images), key=lambda k: (min(k, images - k), k))


def solution(mesh):
    in_specs = (P(None, "col", "row"), P(), P(), P("col", "row"), P("col", "row"))
    out_specs = P(None, "col", "row")

    def whole(pixels_tokens, *rest):
        step = jax.shard_map(
            local, mesh=mesh, in_specs=in_specs, out_specs=out_specs, check_vma=False
        )
        return step(pixels_tokens, *rest)

    return whole
```

profile of v0, /device:TPU:0, one launch (start us, length us, event | category | flops | bytes accessed | tf_op | source)
XLA Modules:
  0.0 456.7 jit_solution(18421342010862708910)
XLA Ops:
  0.0 3.1 collective-permute-start.16
  3.1 2.0 dynamic-slice_bitcast_fusion
  5.0 2.7 collective-permute-start
  7.7 1.3 collective-permute-start.4
  9.0 0.7 collective-permute-start.8
  9.7 1.5 collective-permute-start.12
  11.2 69.5 %collective-permute-done.refs_0_ = bf16[288,1280]{1,0:T(8,128)(2,1)S(1)} collective-permute-done((bf16[288,1280]{1,0:T(8,128)(2,1)S(1)}, bf16[288,1280]{1,0:T(8,128)(2,1)S(1)}, u32[]{:S(2)}, u32[]{:S(2)}) %collective-permute-start) | collective-permute-done | bytes 737312 | tf_op jit(solution)/shard_map/ppermute | solution.py:371
  80.7 1.7 collective-permute-start.13
  82.4 14.6 %collective-permute-start.18 = (bf16[640,1536]{1,0:T(8,128)(2,1)}, bf16[640,1536]{1,0:T(8,128)(2,1)S(1)}, u32[]{:S(2)}, u32[]{:S(2)}) collective-permute-start(bf16[640,1536]{1,0:T(8,128)(2,1)} %collective-permute-done.16.refs_2_), channel_id=1, source_target_pairs={{0,2},{1,3},{2,4},{3,5},{4,6},{5,7},{6,0},{7,1},{8,10},{9,11},{10,... | collective-permute-start | bytes 5898248 | tf_op jit(solution)/shard_map/ppermute | solution.py:371
  97.0 1.5 collective-permute-start.1
  99.0 1.5 collective-permute-start.5
  100.6 1.2 collective-permute-start.6
  101.8 14.6 %collective-permute-done.1.refs_1_ = bf16[288,1280]{1,0:T(8,128)(2,1)S(1)} collective-permute-done((bf16[288,1280]{1,0:T(8,128)(2,1)S(1)}, bf16[288,1280]{1,0:T(8,128)(2,1)S(1)}, u32[]{:S(2)}, u32[]{:S(2)}) %collective-permute-start.1) | collective-permute-done | bytes 737312 | tf_op jit(solution)/shard_map/ppermute | solution.py:45
  116.9 1.0 collective-permute-done.2.refs_2_
  117.9 0.5 collective-permute-start.10
  118.4 15.3 %collective-permute-done.5.refs_1_ = bf16[288,1280]{1,0:T(8,128)(2,1)S(1)} collective-permute-done((bf16[288,1280]{1,0:T(8,128)(2,1)S(1)}, bf16[288,1280]{1,0:T(8,128)(2,1)S(1)}, u32[]{:S(2)}, u32[]{:S(2)}) %collective-permute-start.5) | collective-permute-done | bytes 737312 | tf_op jit(solution)/shard_map/ppermute | solution.py:45
  134.2 1.5 collective-permute-start.3
  135.7 13.8 %collective-permute-done.9.refs_1_ = bf16[288,1280]{1,0:T(8,128)(2,1)S(1)} collective-permute-done((bf16[288,1280]{1,0:T(8,128)(2,1)S(1)}, bf16[288,1280]{1,0:T(8,128)(2,1)S(1)}, u32[]{:S(2)}, u32[]{:S(2)}) %collective-permute-start.9) | collective-permute-done | bytes 737312 | tf_op jit(solution)/shard_map/ppermute | solution.py:45
  150.2 15.1 %collective-permute-done.14.refs_3_ = bf16[288,1280]{1,0:T(8,128)(2,1)S(1)} collective-permute-done((bf16[288,1280]{1,0:T(8,128)(2,1)S(1)}, bf16[288,1280]{1,0:T(8,128)(2,1)S(1)}, u32[]{:S(2)}, u32[]{:S(2)}) %collective-permute-start.14) | collective-permute-done | bytes 737312 | tf_op jit(solution)/shard_map/ppermute | solution.py:45
  165.3 0.5 collective-permute-start.7
  165.8 12.0 %collective-permute-done.3.refs_3_ = bf16[288,1280]{1,0:T(8,128)(2,1)S(1)} collective-permute-done((bf16[288,1280]{1,0:T(8,128)(2,1)S(1)}, bf16[288,1280]{1,0:T(8,128)(2,1)S(1)}, u32[]{:S(2)}, u32[]{:S(2)}) %collective-permute-start.3) | collective-permute-done | bytes 737312 | tf_op jit(solution)/shard_map/ppermute | solution.py:45
  177.9 0.9 copy-done.19
  178.8 1.7 collective-permute-start.11
  180.5 1.4 fusion
  181.9 57.9 %collective-permute-start.20 = (bf16[640,768]{1,0:T(8,128)(2,1)}, bf16[640,768]{1,0:T(8,128)(2,1)}, u32[]{:S(2)}, u32[]{:S(2)}) collective-permute-start(bf16[640,768]{1,0:T(8,128)(2,1)} %get-tuple-element.34), channel_id=1, source_target_pairs={{0,2},{1,3},{2,4},{3,5},{4,6},{5,7},{6,0},{7,1},{8,10},{9,11},{10,... | collective-permute-start | bytes 2949128 | tf_op jit(solution)/shard_map/ppermute | solution.py:371
  239.8 0.9 copy-done.22
  240.7 15.2 %collective-permute-start.39 = (bf16[640,768]{1,0:T(8,128)(2,1)}, bf16[640,768]{1,0:T(8,128)(2,1)}, u32[]{:S(2)}, u32[]{:S(2)}) collective-permute-start(bf16[640,768]{1,0:T(8,128)(2,1)} %get-tuple-element.33), channel_id=1, source_target_pairs={{0,2},{1,3},{2,4},{3,5},{4,6},{5,7},{6,0},{7,1},{8,10},{9,11},{10,... | collective-permute-start | bytes 2949128 | tf_op jit(solution)/shard_map/ppermute | solution.py:371
  255.9 6.6 %norm.4.refs_4_ = bf16[4,4,288,1280]{3,2,1,0:T(8,128)(2,1)} custom-call(f32[1,5120]{1,0:T(1,128)} %bitcast.10, f32[1,5120]{1,0:T(1,128)} %bitcast.14, bf16[288,1280]{1,0:T(8,128)(2,1)} %copy-done, bf16[288,1280]{1,0:T(8,128)(2,1)} %copy-done.11, bf16[288,1280]{1,0:T(8,128)(2,1)} %copy-done.13, bf16[288,1280]{1,0:T(8,128)(2,1)} %copy-done.20), custom_call_target="tpu_custom_call" | custom-call | flops 11796480 | bytes 5898240 | tf_op jit(solution)/shard_map/norm/pallas_call | solution.py:83
  262.5 6.6 %norm.5.refs_4_ = bf16[4,4,288,1280]{3,2,1,0:T(8,128)(2,1)} custom-call(f32[1,5120]{1,0:T(1,128)} %bitcast.11, f32[1,5120]{1,0:T(1,128)} %bitcast.15, bf16[288,1280]{1,0:T(8,128)(2,1)} %copy-done.10, bf16[288,1280]{1,0:T(8,128)(2,1)} %copy-done.17, bf16[288,1280]{1,0:T(8,128)(2,1)} %copy-done.18, ...), custom_call_target="tpu_custom_call", output_to_operand_aliasing={{}: (6, {})} | custom-call | flops 11796480 | bytes 5898240 | tf_op jit(solution)/shard_map/norm/pallas_call | solution.py:83
  269.1 6.6 %norm.6.refs_4_ = bf16[4,4,288,1280]{3,2,1,0:T(8,128)(2,1)} custom-call(f32[1,5120]{1,0:T(1,128)} %bitcast.12, f32[1,5120]{1,0:T(1,128)} %bitcast.16, bf16[288,1280]{1,0:T(8,128)(2,1)} %copy-done.9, bf16[288,1280]{1,0:T(8,128)(2,1)} %copy-done.15, bf16[288,1280]{1,0:T(8,128)(2,1)} %copy-done.16, ...), custom_call_target="tpu_custom_call", output_to_operand_aliasing={{}: (6, {})} | custom-call | flops 11796480 | bytes 5898240 | tf_op jit(solution)/shard_map/norm/pallas_call | solution.py:83
  275.7 6.7 %norm.7.x_ref = bf16[4,4,288,1280]{3,2,1,0:T(8,128)(2,1)} custom-call(f32[1,5120]{1,0:T(1,128)} %bitcast.13, f32[1,5120]{1,0:T(1,128)} %bitcast.17, bf16[288,1280]{1,0:T(8,128)(2,1)} %copy-done.8, bf16[288,1280]{1,0:T(8,128)(2,1)} %copy-done.12, bf16[288,1280]{1,0:T(8,128)(2,1)} %copy-done.14, ...), custom_call_target="tpu_custom_call", output_to_operand_aliasing={{}: (6, {})} | custom-call | flops 11796480 | bytes 5898240 | tf_op jit(solution)/shard_map/norm/pallas_call | solution.py:83
  283.2 26.1 %early.1.acc_ref = f32[2,4,288,768]{3,2,1,0:T(8,128)} custom-call(bf16[4,4,288,1280]{3,2,1,0:T(8,128)(2,1)} %norm.7.x_ref, bf16[640,1536]{1,0:T(8,128)(2,1)} %refs_0_.1, bf16[640,1536]{1,0:T(8,128)(2,1)} %collective-permute-done.15.refs_1_, bf16[640,1536]{1,0:T(8,128)(2,1)} %collective-permute-done.16.refs_2_, ...), custom_call_target="tpu_custom_call" | custom-call | flops 13589544960 | bytes 8847360 | tf_op jit(solution)/shard_map/early/pallas_call | solution.py:157
  309.4 8.5 %late.3 = (bf16[1152,256]{1,0:T(8,128)(2,1)}, bf16[1152,512]{1,0:T(8,128)(2,1)}) custom-call(bf16[4,4,288,1280]{3,2,1,0:T(8,128)(2,1)} %norm.7.x_ref, f32[2,4,288,768]{3,2,1,0:T(8,128)} %early.1.acc_ref, bf16[640,768]{1,0:T(8,128)(2,1)} %collective-permute-done.39.refs_0_, bf16[640,768]{1,0:T(8,128)(2,1)} %collective-permute-done.40.refs_1_), custom_call_target="tpu_custom_call" | custom-call | flops 2264924160 | bytes 7077888 | tf_op jit(solution)/shard_map/late/pallas_call | solution.py:212
  318.1 8.3 %late.2 = (bf16[1152,256]{1,0:T(8,128)(2,1)}, bf16[1152,512]{1,0:T(8,128)(2,1)}) custom-call(bf16[4,4,288,1280]{3,2,1,0:T(8,128)(2,1)} %norm.7.x_ref, f32[2,4,288,768]{3,2,1,0:T(8,128)} %early.1.acc_ref, bf16[640,768]{1,0:T(8,128)(2,1)} %collective-permute-done.20.refs_0_, bf16[640,768]{1,0:T(8,128)(2,1)} %collective-permute-done.21.refs_1_), custom_call_target="tpu_custom_call" | custom-call | flops 2264924160 | bytes 7077888 | tf_op jit(solution)/shard_map/late/pallas_call | solution.py:212
  327.7 17.9 %collective-permute-done.35.refs_12_ = bf16[256,1280]{1,0:T(8,128)(2,1)S(1)} collective-permute-done((bf16[256,1280]{1,0:T(8,128)(2,1)S(1)}, bf16[256,1280]{1,0:T(8,128)(2,1)S(1)}, u32[]{:S(2)}, u32[]{:S(2)}) %collective-permute-start.35) | collective-permute-done | bytes 655392 | tf_op jit(solution)/shard_map/ppermute | solution.py:371
  345.6 15.6 %attend.3 = (bf16[288,256]{1,0:T(8,128)(2,1)}, bf16[288,256]{1,0:T(8,128)(2,1)}, bf16[288,256]{1,0:T(8,128)(2,1)}, bf16[288,256]{1,0:T(8,128)(2,1)}) custom-call(bf16[1152,256]{1,0:T(8,128)(2,1)} %get-tuple-element.23.q_ref, bf16[1152,512]{1,0:T(8,128)(2,1)} %get-tuple-element.24.refs_0_, bf16[1152,512]{1,0:T(8,128)(2,1)} %collective-permute-done.41.refs_1_), custom_call_target="tpu_custom_call" | custom-call | flops 5435817984 | bytes 3538944 | tf_op jit(solution)/shard_map/attend/pallas_call | solution.py:280
  361.2 2.1 collective-permute-start.46
  363.3 15.4 %attend.2 = (bf16[288,256]{1,0:T(8,128)(2,1)}, bf16[288,256]{1,0:T(8,128)(2,1)}, bf16[288,256]{1,0:T(8,128)(2,1)}, bf16[288,256]{1,0:T(8,128)(2,1)}) custom-call(bf16[1152,256]{1,0:T(8,128)(2,1)} %get-tuple-element.17.q_ref, bf16[1152,512]{1,0:T(8,128)(2,1)} %get-tuple-element.18.refs_0_, bf16[1152,512]{1,0:T(8,128)(2,1)} %collective-permute-done.22.refs_1_), custom_call_target="tpu_custom_call" | custom-call | flops 5435817984 | bytes 3538944 | tf_op jit(solution)/shard_map/attend/pallas_call | solution.py:280
  378.7 1.6 constant_dynamic-update-slice_fusion.1
  380.3 1.5 collective-permute-start.23
  381.8 0.9 constant_dynamic-update-slice_fusion.5
  383.3 0.8 collective-permute-start.42
  384.2 1.3 collective-permute-start.27
  385.7 2.7 collective-permute-start.47
  388.3 0.7 constant_dynamic-update-slice_fusion.refs_0_
  389.4 11.6 %collective-permute-start.28 = (bf16[288,256]{1,0:T(8,128)(2,1)}, bf16[288,256]{1,0:T(8,128)(2,1)S(1)}, u32[]{:S(2)}, u32[]{:S(2)}) collective-permute-start(bf16[288,256]{1,0:T(8,128)(2,1)} %get-tuple-element.22), channel_id=1, source_target_pairs={{0,2},{1,3},{2,4},{3,5},{4,6},{5,7},{6,0},{7,1},{8,10},{9,11},{10,... | collective-permute-start | bytes 442376 | tf_op jit(solution)/shard_map/ppermute | solution.py:371
  401.0 1.9 collective-permute-done.27
  402.9 0.5 collective-permute-start.24
  403.5 1.5 collective-permute-start.43
  405.0 1.6 collective-permute-start.48
  406.6 0.6 collective-permute-start.29
  407.2 1.5 collective-permute-start.44
  408.7 4.3 collective-permute-done.24.refs_1_
  413.0 0.5 collective-permute-start.49
  413.6 5.8 %collective-permute-done.43.refs_1_ = bf16[576,256]{1,0:T(8,128)(2,1)S(1)} collective-permute-done((bf16[576,256]{1,0:T(8,128)(2,1)S(1)}, bf16[576,256]{1,0:T(8,128)(2,1)S(1)}, u32[]{:S(2)}, u32[]{:S(2)}) %collective-permute-start.43) | collective-permute-done | bytes 294944 | tf_op jit(solution)/shard_map/ppermute | solution.py:45
  419.3 1.5 collective-permute-start.45
  421.4 1.4 collective-permute-start.25
  422.8 4.8 %collective-permute-done.44.refs_2_ = bf16[576,256]{1,0:T(8,128)(2,1)S(1)} collective-permute-done((bf16[576,256]{1,0:T(8,128)(2,1)S(1)}, bf16[576,256]{1,0:T(8,128)(2,1)S(1)}, u32[]{:S(2)}, u32[]{:S(2)}) %collective-permute-start.44) | collective-permute-done | bytes 294944 | tf_op jit(solution)/shard_map/ppermute | solution.py:45
  427.6 0.5 collective-permute-start.30
  428.1 1.5 collective-permute-start.26
  429.6 4.2 collective-permute-done.45.refs_3_
  433.9 0.5 collective-permute-start.31
  434.6 11.0 %out.2.refs_16_ = f32[4,288,1280]{2,1,0:T(8,128)} custom-call(bf16[576,256]{1,0:T(8,128)(2,1)} %copy-done.23, bf16[576,256]{1,0:T(8,128)(2,1)} %copy-done.28, bf16[576,256]{1,0:T(8,128)(2,1)} %copy-done.30, bf16[576,256]{1,0:T(8,128)(2,1)} %copy-done.32, bf16[576,256]{1,0:T(8,128)(2,1)} %copy-done.24, bf16[576,256]{1,0:T(8,128)(2,1)} %copy-done.29, ...), custom_call_target="tpu_custom_call" | custom-call | flops 3019898880 | bytes 11796480 | tf_op jit(solution)/shard_map/out/pallas_call | solution.py:338
  445.7 10.8 %out.3 = bf16[4,288,1280]{2,1,0:T(8,128)(2,1)} custom-call(bf16[576,256]{1,0:T(8,128)(2,1)} %constant_dynamic-update-slice_fusion.refs_0_, bf16[576,256]{1,0:T(8,128)(2,1)} %copy-done.26, bf16[576,256]{1,0:T(8,128)(2,1)} %collective-permute-done.25.refs_2_, bf16[576,256]{1,0:T(8,128)(2,1)} %collective-permute-done.26.refs_3_, bf16[576,256]{1,0:T(8,128)(2,1)} %copy-done.25, ...), custom_call_target="tpu_custom_call" | custom-call | flops 3019898880 | bytes 11796480 | tf_op jit(solution)/shard_map/out/pallas_call | solution.py:338
  (125 shorter events, 6.6 us)
Async XLA Ops:
  0.0 82.4 %collective-permute-start.16 = (bf16[640,1536]{1,0:T(8,128)(2,1)}, bf16[640,1536]{1,0:T(8,128)(2,1)}, u32[]{:S(2)}, u32[]{:S(2)}) collective-permute-start(bf16[640,1536]{1,0:T(8,128)(2,1)} %refs_0_.1), channel_id=1, source_target_pairs={{0,2},{1,3},{2,4},{3,5},{4,6},{5,7},{6,0},{7,1},{8,10},{9,11},{10,... | collective-permute-start | bytes 5898248 | tf_op jit(solution)/shard_map/ppermute | solution.py:371
  5.0 176.9 %copy-start = (bf16[288,1280]{1,0:T(8,128)(2,1)}, bf16[288,1280]{1,0:T(8,128)(2,1)S(1)}, u32[]{:S(2)}) copy-start(bf16[288,1280]{1,0:T(8,128)(2,1)S(1)} %get-tuple-element.29.refs_0_) | copy-start | bytes 2211844
  5.0 75.7 %collective-permute-start = (bf16[288,1280]{1,0:T(8,128)(2,1)S(1)}, bf16[288,1280]{1,0:T(8,128)(2,1)S(1)}, u32[]{:S(2)}, u32[]{:S(2)}) collective-permute-start(bf16[288,1280]{1,0:T(8,128)(2,1)S(1)} %get-tuple-element.32), channel_id=1, source_target_pairs={{0,4},{1,5},{2,6},{3,7},{4,0},{5,1},{6,2},{7,3},{8,12},{9,13},{10,... | collective-permute-start | bytes 2211848 | tf_op jit(solution)/shard_map/ppermute | solution.py:371
  7.7 89.3 %collective-permute-start.4 = (bf16[288,1280]{1,0:T(8,128)(2,1)S(1)}, bf16[288,1280]{1,0:T(8,128)(2,1)S(1)}, u32[]{:S(2)}, u32[]{:S(2)}) collective-permute-start(bf16[288,1280]{1,0:T(8,128)(2,1)S(1)} %get-tuple-element.31), channel_id=1, source_target_pairs={{0,6},{1,7},{2,0},{3,1},{4,2},{5,3},{6,4},{7,5},{8,14},{9,15},{10,... | collective-permute-start | bytes 2211848 | tf_op jit(solution)/shard_map/ppermute | solution.py:371
  9.0 89.5 %collective-permute-start.8 = (bf16[288,1280]{1,0:T(8,128)(2,1)S(1)}, bf16[288,1280]{1,0:T(8,128)(2,1)S(1)}, u32[]{:S(2)}, u32[]{:S(2)}) collective-permute-start(bf16[288,1280]{1,0:T(8,128)(2,1)S(1)} %get-tuple-element.30), channel_id=1, source_target_pairs={{0,2},{1,3},{2,4},{3,5},{4,6},{5,7},{6,0},{7,1},{8,10},{9,11},{10,... | collective-permute-start | bytes 2211848 | tf_op jit(solution)/shard_map/ppermute | solution.py:371
  9.7 89.3 %collective-permute-start.12 = (bf16[288,1280]{1,0:T(8,128)(2,1)S(1)}, bf16[288,1280]{1,0:T(8,128)(2,1)S(1)}, u32[]{:S(2)}, u32[]{:S(2)}) collective-permute-start(bf16[288,1280]{1,0:T(8,128)(2,1)S(1)} %get-tuple-element.29.refs_0_), channel_id=1, source_target_pairs={{0,8},{8,0},{16,24},{24,16},{1,9},{9,1},{17,25},{25,17},{2,10},{10... | collective-permute-start | bytes 2211848 | tf_op jit(solution)/shard_map/ppermute | solution.py:45
  80.7 69.3 %copy-start.8 = (bf16[288,1280]{1,0:T(8,128)(2,1)}, bf16[288,1280]{1,0:T(8,128)(2,1)S(1)}, u32[]{:S(2)}) copy-start(bf16[288,1280]{1,0:T(8,128)(2,1)S(1)} %collective-permute-done.refs_0_) | copy-start | bytes 2211844
  80.7 19.9 %collective-permute-start.13 = (bf16[288,1280]{1,0:T(8,128)(2,1)S(1)}, bf16[288,1280]{1,0:T(8,128)(2,1)S(1)}, u32[]{:S(2)}, u32[]{:S(2)}) collective-permute-start(bf16[288,1280]{1,0:T(8,128)(2,1)S(1)} %get-tuple-element.29.refs_0_), channel_id=1, source_target_pairs={{0,16},{8,24},{16,0},{24,8},{1,17},{9,25},{17,1},{25,9},{2,18},{10... | collective-permute-start | bytes 2211848 | tf_op jit(solution)/shard_map/ppermute | solution.py:45
  82.4 67.6 %collective-permute-start.18 = (bf16[640,1536]{1,0:T(8,128)(2,1)}, bf16[640,1536]{1,0:T(8,128)(2,1)S(1)}, u32[]{:S(2)}, u32[]{:S(2)}) collective-permute-start(bf16[640,1536]{1,0:T(8,128)(2,1)} %collective-permute-done.16.refs_2_), channel_id=1, source_target_pairs={{0,2},{1,3},{2,4},{3,5},{4,6},{5,7},{6,0},{7,1},{8,10},{9,11},{10,... | collective-permute-start | bytes 5898248 | tf_op jit(solution)/shard_map/ppermute | solution.py:371
  97.0 53.1 %copy-start.9 = (bf16[288,1280]{1,0:T(8,128)(2,1)}, bf16[288,1280]{1,0:T(8,128)(2,1)S(1)}, u32[]{:S(2)}) copy-start(bf16[288,1280]{1,0:T(8,128)(2,1)S(1)} %collective-permute-done.4.refs_0_) | copy-start | bytes 2211844
  97.0 19.4 %collective-permute-start.1 = (bf16[288,1280]{1,0:T(8,128)(2,1)S(1)}, bf16[288,1280]{1,0:T(8,128)(2,1)S(1)}, u32[]{:S(2)}, u32[]{:S(2)}) collective-permute-start(bf16[288,1280]{1,0:T(8,128)(2,1)S(1)} %collective-permute-done.refs_0_), channel_id=1, source_target_pairs={{0,8},{8,0},{16,24},{24,16},{1,9},{9,1},{17,25},{25,17},{2,10},{10... | collective-permute-start | bytes 2211848 | tf_op jit(solution)/shard_map/ppermute | solution.py:45
  98.5 66.8 %copy-start.10 = (bf16[288,1280]{1,0:T(8,128)(2,1)}, bf16[288,1280]{1,0:T(8,128)(2,1)S(1)}, u32[]{:S(2)}) copy-start(bf16[288,1280]{1,0:T(8,128)(2,1)S(1)} %collective-permute-done.8.refs_0_) | copy-start | bytes 2211844
  98.5 19.4 %collective-permute-start.2 = (bf16[288,1280]{1,0:T(8,128)(2,1)S(1)}, bf16[288,1280]{1,0:T(8,128)(2,1)S(1)}, u32[]{:S(2)}, u32[]{:S(2)}) collective-permute-start(bf16[288,1280]{1,0:T(8,128)(2,1)S(1)} %collective-permute-done.refs_0_), channel_id=1, source_target_pairs={{0,16},{8,24},{16,0},{24,8},{1,17},{9,25},{17,1},{25,9},{2,18},{10... | collective-permute-start | bytes 2211848 | tf_op jit(solution)/shard_map/ppermute | solution.py:45
  99.0 66.8 %copy-start.11 = (bf16[288,1280]{1,0:T(8,128)(2,1)}, bf16[288,1280]{1,0:T(8,128)(2,1)S(1)}, u32[]{:S(2)}) copy-start(bf16[288,1280]{1,0:T(8,128)(2,1)S(1)} %collective-permute-done.12.refs_1_) | copy-start | bytes 2211844
  99.0 34.6 %collective-permute-start.5 = (bf16[288,1280]{1,0:T(8,128)(2,1)S(1)}, bf16[288,1280]{1,0:T(8,128)(2,1)S(1)}, u32[]{:S(2)}, u32[]{:S(2)}) collective-permute-start(bf16[288,1280]{1,0:T(8,128)(2,1)S(1)} %collective-permute-done.4.refs_0_), channel_id=1, source_target_pairs={{0,16},{8,24},{16,0},{24,8},{1,17},{9,25},{17,1},{25,9},{2,18},{10... | collective-permute-start | bytes 2211848 | tf_op jit(solution)/shard_map/ppermute | solution.py:45
  100.6 77.3 %copy-start.13 = (bf16[288,1280]{1,0:T(8,128)(2,1)}, bf16[288,1280]{1,0:T(8,128)(2,1)S(1)}, u32[]{:S(2)}) copy-start(bf16[288,1280]{1,0:T(8,128)(2,1)S(1)} %collective-permute-done.13.refs_2_) | copy-start | bytes 2211844
  100.6 33.6 %collective-permute-start.6 = (bf16[288,1280]{1,0:T(8,128)(2,1)S(1)}, bf16[288,1280]{1,0:T(8,128)(2,1)S(1)}, u32[]{:S(2)}, u32[]{:S(2)}) collective-permute-start(bf16[288,1280]{1,0:T(8,128)(2,1)S(1)} %collective-permute-done.4.refs_0_), channel_id=1, source_target_pairs={{0,8},{8,0},{16,24},{24,16},{1,9},{9,1},{17,25},{25,17},{2,10},{10... | collective-permute-start | bytes 2211848 | tf_op jit(solution)/shard_map/ppermute | solution.py:45
  116.4 61.5 %copy-start.12 = (bf16[288,1280]{1,0:T(8,128)(2,1)}, bf16[288,1280]{1,0:T(8,128)(2,1)S(1)}, u32[]{:S(2)}) copy-start(bf16[288,1280]{1,0:T(8,128)(2,1)S(1)} %collective-permute-done.1.refs_1_) | copy-start | bytes 2211844
  116.4 33.1 %collective-permute-start.9 = (bf16[288,1280]{1,0:T(8,128)(2,1)S(1)}, bf16[288,1280]{1,0:T(8,128)(2,1)S(1)}, u32[]{:S(2)}, u32[]{:S(2)}) collective-permute-start(bf16[288,1280]{1,0:T(8,128)(2,1)S(1)} %collective-permute-done.8.refs_0_), channel_id=1, source_target_pairs={{0,16},{8,24},{16,0},{24,8},{1,17},{9,25},{17,1},{25,9},{2,18},{10... | collective-permute-start | bytes 2211848 | tf_op jit(solution)/shard_map/ppermute | solution.py:45
  117.9 60.0 %copy-start.14 = (bf16[288,1280]{1,0:T(8,128)(2,1)}, bf16[288,1280]{1,0:T(8,128)(2,1)S(1)}, u32[]{:S(2)}) copy-start(bf16[288,1280]{1,0:T(8,128)(2,1)S(1)} %collective-permute-done.2.refs_2_) | copy-start | bytes 2211844
  117.9 31.6 %collective-permute-start.10 = (bf16[288,1280]{1,0:T(8,128)(2,1)S(1)}, bf16[288,1280]{1,0:T(8,128)(2,1)S(1)}, u32[]{:S(2)}, u32[]{:S(2)}) collective-permute-start(bf16[288,1280]{1,0:T(8,128)(2,1)S(1)} %collective-permute-done.8.refs_0_), channel_id=1, source_target_pairs={{0,8},{8,0},{16,24},{24,16},{1,9},{9,1},{17,25},{25,17},{2,10},{10... | collective-permute-start | bytes 2211848 | tf_op jit(solution)/shard_map/ppermute | solution.py:45
  133.7 48.2 %copy-start.15 = (bf16[288,1280]{1,0:T(8,128)(2,1)}, bf16[288,1280]{1,0:T(8,128)(2,1)S(1)}, u32[]{:S(2)}) copy-start(bf16[288,1280]{1,0:T(8,128)(2,1)S(1)} %collective-permute-done.5.refs_1_) | copy-start | bytes 2211844
  133.7 31.6 %collective-permute-start.14 = (bf16[288,1280]{1,0:T(8,128)(2,1)S(1)}, bf16[288,1280]{1,0:T(8,128)(2,1)S(1)}, u32[]{:S(2)}, u32[]{:S(2)}) collective-permute-start(bf16[288,1280]{1,0:T(8,128)(2,1)S(1)} %collective-permute-done.12.refs_1_), channel_id=1, source_target_pairs={{0,16},{8,24},{16,0},{24,8},{1,17},{9,25},{17,1},{25,9},{2,18},{10... | collective-permute-start | bytes 2211848 | tf_op jit(solution)/shard_map/ppermute | solution.py:45
  134.2 43.7 %copy-start.16 = (bf16[288,1280]{1,0:T(8,128)(2,1)}, bf16[288,1280]{1,0:T(8,128)(2,1)S(1)}, u32[]{:S(2)}) copy-start(bf16[288,1280]{1,0:T(8,128)(2,1)S(1)} %collective-permute-done.6.refs_2_) | copy-start | bytes 2211844
  134.2 43.7 %collective-permute-start.3 = (bf16[288,1280]{1,0:T(8,128)(2,1)S(1)}, bf16[288,1280]{1,0:T(8,128)(2,1)S(1)}, u32[]{:S(2)}, u32[]{:S(2)}) collective-permute-start(bf16[288,1280]{1,0:T(8,128)(2,1)S(1)} %collective-permute-done.1.refs_1_), channel_id=1, source_target_pairs={{0,16},{8,24},{16,0},{24,8},{1,17},{9,25},{17,1},{25,9},{2,18},{10... | collective-permute-start | bytes 2211848 | tf_op jit(solution)/shard_map/ppermute | solution.py:45
  149.5 132.9 %collective-permute-start.15 = (bf16[640,1536]{1,0:T(8,128)(2,1)}, bf16[640,1536]{1,0:T(8,128)(2,1)}, u32[]{:S(2)}, u32[]{:S(2)}) collective-permute-start(bf16[640,1536]{1,0:T(8,128)(2,1)} %refs_0_.1), channel_id=1, source_target_pairs={{0,1},{1,0},{2,3},{3,2},{4,5},{5,4},{6,7},{7,6},{8,9},{9,8},{10,11... | collective-permute-start | bytes 5898248 | tf_op jit(solution)/shard_map/ppermute | solution.py:375
  149.5 133.7 %collective-permute-start.17 = (bf16[640,1536]{1,0:T(8,128)(2,1)}, bf16[640,1536]{1,0:T(8,128)(2,1)}, u32[]{:S(2)}, u32[]{:S(2)}) collective-permute-start(bf16[640,1536]{1,0:T(8,128)(2,1)} %collective-permute-done.16.refs_2_), channel_id=1, source_target_pairs={{0,1},{1,0},{2,3},{3,2},{4,5},{5,4},{6,7},{7,6},{8,9},{9,8},{10,11... | collective-permute-start | bytes 5898248 | tf_op jit(solution)/shard_map/ppermute | solution.py:375
  150.0 133.2 %collective-permute-start.19 = (bf16[640,1536]{1,0:T(8,128)(2,1)S(1)}, bf16[640,1536]{1,0:T(8,128)(2,1)}, u32[]{:S(2)}, u32[]{:S(2)}) collective-permute-start(bf16[640,1536]{1,0:T(8,128)(2,1)S(1)} %collective-permute-done.18.refs_4_), channel_id=1, source_target_pairs={{0,1},{1,0},{2,3},{3,2},{4,5},{5,4},{6,7},{7,6},{8,9},{9,8},{10,11... | collective-permute-start | bytes 5898248 | tf_op jit(solution)/shard_map/ppermute | solution.py:375
  165.3 16.6 %collective-permute-start.7 = (bf16[288,1280]{1,0:T(8,128)(2,1)S(1)}, bf16[288,1280]{1,0:T(8,128)(2,1)S(1)}, u32[]{:S(2)}, u32[]{:S(2)}) collective-permute-start(bf16[288,1280]{1,0:T(8,128)(2,1)S(1)} %collective-permute-done.5.refs_1_), channel_id=1, source_target_pairs={{0,8},{8,0},{16,24},{24,16},{1,9},{9,1},{17,25},{25,17},{2,10},{10... | collective-permute-start | bytes 2211848 | tf_op jit(solution)/shard_map/ppermute | solution.py:45
  178.8 61.0 %collective-permute-start.11 = (bf16[288,1280]{1,0:T(8,128)(2,1)S(1)}, bf16[288,1280]{1,0:T(8,128)(2,1)S(1)}, u32[]{:S(2)}, u32[]{:S(2)}) collective-permute-start(bf16[288,1280]{1,0:T(8,128)(2,1)S(1)} %collective-permute-done.9.refs_1_), channel_id=1, source_target_pairs={{0,8},{8,0},{16,24},{24,16},{1,9},{9,1},{17,25},{25,17},{2,10},{10... | collective-permute-start | bytes 2211848 | tf_op jit(solution)/shard_map/ppermute | solution.py:45
  181.9 57.9 %copy-start.21 = (bf16[288,1280]{1,0:T(8,128)(2,1)}, bf16[288,1280]{1,0:T(8,128)(2,1)S(1)}, u32[]{:S(2)}) copy-start(bf16[288,1280]{1,0:T(8,128)(2,1)S(1)} %collective-permute-done.7.refs_3_) | copy-start | bytes 2211844
  181.9 100.7 %collective-permute-start.20 = (bf16[640,768]{1,0:T(8,128)(2,1)}, bf16[640,768]{1,0:T(8,128)(2,1)}, u32[]{:S(2)}, u32[]{:S(2)}) collective-permute-start(bf16[640,768]{1,0:T(8,128)(2,1)} %get-tuple-element.34), channel_id=1, source_target_pairs={{0,2},{1,3},{2,4},{3,5},{4,6},{5,7},{6,0},{7,1},{8,10},{9,11},{10,... | collective-permute-start | bytes 2949128 | tf_op jit(solution)/shard_map/ppermute | solution.py:371
  240.7 42.1 %collective-permute-start.39 = (bf16[640,768]{1,0:T(8,128)(2,1)}, bf16[640,768]{1,0:T(8,128)(2,1)}, u32[]{:S(2)}, u32[]{:S(2)}) collective-permute-start(bf16[640,768]{1,0:T(8,128)(2,1)} %get-tuple-element.33), channel_id=1, source_target_pairs={{0,2},{1,3},{2,4},{3,5},{4,6},{5,7},{6,0},{7,1},{8,10},{9,11},{10,... | collective-permute-start | bytes 2949128 | tf_op jit(solution)/shard_map/ppermute | solution.py:371
  282.4 44.4 %collective-permute-start.33 = (bf16[256,1280]{1,0:T(8,128)(2,1)S(1)}, bf16[256,1280]{1,0:T(8,128)(2,1)S(1)}, u32[]{:S(2)}, u32[]{:S(2)}) collective-permute-start(bf16[256,1280]{1,0:T(8,128)(2,1)S(1)} %copy-done.1), channel_id=1, source_target_pairs={{0,2},{1,3},{2,4},{3,5},{4,6},{5,7},{6,0},{7,1},{8,10},{9,11},{10,... | collective-permute-start | bytes 1966088 | tf_op jit(solution)/shard_map/ppermute | solution.py:371
  282.6 35.4 %collective-permute-start.21 = (bf16[640,768]{1,0:T(8,128)(2,1)}, bf16[640,768]{1,0:T(8,128)(2,1)}, u32[]{:S(2)}, u32[]{:S(2)}) collective-permute-start(bf16[640,768]{1,0:T(8,128)(2,1)} %collective-permute-done.20.refs_0_), channel_id=1, source_target_pairs={{0,1},{1,0},{2,3},{3,2},{4,5},{5,4},{6,7},{7,6},{8,9},{9,8},{10,11... | collective-permute-start | bytes 2949128 | tf_op jit(solution)/shard_map/ppermute | solution.py:375
  282.7 26.6 %collective-permute-start.40 = (bf16[640,768]{1,0:T(8,128)(2,1)}, bf16[640,768]{1,0:T(8,128)(2,1)}, u32[]{:S(2)}, u32[]{:S(2)}) collective-permute-start(bf16[640,768]{1,0:T(8,128)(2,1)} %collective-permute-done.39.refs_0_), channel_id=1, source_target_pairs={{0,1},{1,0},{2,3},{3,2},{4,5},{5,4},{6,7},{7,6},{8,9},{9,8},{10,11... | collective-permute-start | bytes 2949128 | tf_op jit(solution)/shard_map/ppermute | solution.py:375
  317.9 27.7 %collective-permute-start.41 = (bf16[1152,512]{1,0:T(8,128)(2,1)}, bf16[1152,512]{1,0:T(8,128)(2,1)}, u32[]{:S(2)}, u32[]{:S(2)}) collective-permute-start(bf16[1152,512]{1,0:T(8,128)(2,1)} %get-tuple-element.24.refs_0_), channel_id=1, source_target_pairs={{0,1},{1,0},{2,3},{3,2},{4,5},{5,4},{6,7},{7,6},{8,9},{9,8},{10,11... | collective-permute-start | bytes 3538952 | tf_op jit(solution)/shard_map/ppermute | solution.py:402
  326.3 36.9 %collective-permute-start.22 = (bf16[1152,512]{1,0:T(8,128)(2,1)}, bf16[1152,512]{1,0:T(8,128)(2,1)}, u32[]{:S(2)}, u32[]{:S(2)}) collective-permute-start(bf16[1152,512]{1,0:T(8,128)(2,1)} %get-tuple-element.18.refs_0_), channel_id=1, source_target_pairs={{0,1},{1,0},{2,3},{3,2},{4,5},{5,4},{6,7},{7,6},{8,9},{9,8},{10,11... | collective-permute-start | bytes 3538952 | tf_op jit(solution)/shard_map/ppermute | solution.py:402
  326.8 18.7 %collective-permute-start.35 = (bf16[256,1280]{1,0:T(8,128)(2,1)S(1)}, bf16[256,1280]{1,0:T(8,128)(2,1)S(1)}, u32[]{:S(2)}, u32[]{:S(2)}) collective-permute-start(bf16[256,1280]{1,0:T(8,128)(2,1)S(1)} %collective-permute-done.33.refs_10_), channel_id=1, source_target_pairs={{0,2},{1,3},{2,4},{3,5},{4,6},{5,7},{6,0},{7,1},{8,10},{9,11},{10,... | collective-permute-start | bytes 1966088 | tf_op jit(solution)/shard_map/ppermute | solution.py:371
  327.1 55.6 %collective-permute-start.32 = (bf16[256,1280]{1,0:T(8,128)(2,1)S(1)}, bf16[256,1280]{1,0:T(8,128)(2,1)S(1)}, u32[]{:S(2)}, u32[]{:S(2)}) collective-permute-start(bf16[256,1280]{1,0:T(8,128)(2,1)S(1)} %copy-done.1), channel_id=1, source_target_pairs={{0,1},{1,0},{2,3},{3,2},{4,5},{5,4},{6,7},{7,6},{8,9},{9,8},{10,11... | collective-permute-start | bytes 1966088 | tf_op jit(solution)/shard_map/ppermute | solution.py:375
  327.3 56.8 %collective-permute-start.34 = (bf16[256,1280]{1,0:T(8,128)(2,1)S(1)}, bf16[256,1280]{1,0:T(8,128)(2,1)S(1)}, u32[]{:S(2)}, u32[]{:S(2)}) collective-permute-start(bf16[256,1280]{1,0:T(8,128)(2,1)S(1)} %collective-permute-done.33.refs_10_), channel_id=1, source_target_pairs={{0,1},{1,0},{2,3},{3,2},{4,5},{5,4},{6,7},{7,6},{8,9},{9,8},{10,11... | collective-permute-start | bytes 1966088 | tf_op jit(solution)/shard_map/ppermute | solution.py:375
  345.5 37.3 %collective-permute-start.37 = (bf16[256,1280]{1,0:T(8,128)(2,1)S(1)}, bf16[256,1280]{1,0:T(8,128)(2,1)}, u32[]{:S(2)}, u32[]{:S(2)}) collective-permute-start(bf16[256,1280]{1,0:T(8,128)(2,1)S(1)} %collective-permute-done.35.refs_12_), channel_id=1, source_target_pairs={{0,2},{1,3},{2,4},{3,5},{4,6},{5,7},{6,0},{7,1},{8,10},{9,11},{10,... | collective-permute-start | bytes 1966088 | tf_op jit(solution)/shard_map/ppermute | solution.py:371
  361.2 22.1 %collective-permute-start.46 = (bf16[288,256]{1,0:T(8,128)(2,1)}, bf16[288,256]{1,0:T(8,128)(2,1)S(1)}, u32[]{:S(2)}, u32[]{:S(2)}) collective-permute-start(bf16[288,256]{1,0:T(8,128)(2,1)} %get-tuple-element.27), channel_id=1, source_target_pairs={{0,4},{1,5},{2,6},{3,7},{4,0},{5,1},{6,2},{7,3},{8,12},{9,13},{10,... | collective-permute-start | bytes 442376 | tf_op jit(solution)/shard_map/ppermute | solution.py:371
  380.3 5.4 %collective-permute-start.23 = (bf16[288,256]{1,0:T(8,128)(2,1)}, bf16[288,256]{1,0:T(8,128)(2,1)S(1)}, u32[]{:S(2)}, u32[]{:S(2)}) collective-permute-start(bf16[288,256]{1,0:T(8,128)(2,1)} %get-tuple-element.20), channel_id=1, source_target_pairs={{0,6},{1,7},{2,0},{3,1},{4,2},{5,3},{6,4},{7,5},{8,14},{9,15},{10,... | collective-permute-start | bytes 442376 | tf_op jit(solution)/shard_map/ppermute | solution.py:371
  382.7 51.9 %copy-start.4 = (bf16[256,1280]{1,0:T(8,128)(2,1)}, bf16[256,1280]{1,0:T(8,128)(2,1)S(1)}, u32[]{:S(2)}) copy-start(bf16[256,1280]{1,0:T(8,128)(2,1)S(1)} %collective-permute-done.32.refs_9_) | copy-start | bytes 1966084
  382.7 23.9 %collective-permute-start.36 = (bf16[256,1280]{1,0:T(8,128)(2,1)S(1)}, bf16[256,1280]{1,0:T(8,128)(2,1)S(1)}, u32[]{:S(2)}, u32[]{:S(2)}) collective-permute-start(bf16[256,1280]{1,0:T(8,128)(2,1)S(1)} %collective-permute-done.35.refs_12_), channel_id=1, source_target_pairs={{0,1},{1,0},{2,3},{3,2},{4,5},{5,4},{6,7},{7,6},{8,9},{9,8},{10,11... | collective-permute-start | bytes 1966088 | tf_op jit(solution)/shard_map/ppermute | solution.py:375
  382.8 24.4 %collective-permute-start.38 = (bf16[256,1280]{1,0:T(8,128)(2,1)}, bf16[256,1280]{1,0:T(8,128)(2,1)}, u32[]{:S(2)}, u32[]{:S(2)}) collective-permute-start(bf16[256,1280]{1,0:T(8,128)(2,1)} %collective-permute-done.37.refs_14_), channel_id=1, source_target_pairs={{0,1},{1,0},{2,3},{3,2},{4,5},{5,4},{6,7},{7,6},{8,9},{9,8},{10,11... | collective-permute-start | bytes 1966088 | tf_op jit(solution)/shard_map/ppermute | solution.py:375
  383.3 6.0 %collective-permute-start.42 = (bf16[288,256]{1,0:T(8,128)(2,1)}, bf16[288,256]{1,0:T(8,128)(2,1)S(1)}, u32[]{:S(2)}, u32[]{:S(2)}) collective-permute-start(bf16[288,256]{1,0:T(8,128)(2,1)} %get-tuple-element.26), channel_id=1, source_target_pairs={{0,6},{1,7},{2,0},{3,1},{4,2},{5,3},{6,4},{7,5},{8,14},{9,15},{10,... | collective-permute-start | bytes 442376 | tf_op jit(solution)/shard_map/ppermute | solution.py:371
  384.1 50.5 %copy-start.5 = (bf16[256,1280]{1,0:T(8,128)(2,1)}, bf16[256,1280]{1,0:T(8,128)(2,1)S(1)}, u32[]{:S(2)}) copy-start(bf16[256,1280]{1,0:T(8,128)(2,1)S(1)} %collective-permute-done.34.refs_11_) | copy-start | bytes 1966084
  384.2 18.8 %collective-permute-start.27 = (bf16[288,256]{1,0:T(8,128)(2,1)}, bf16[288,256]{1,0:T(8,128)(2,1)S(1)}, u32[]{:S(2)}, u32[]{:S(2)}) collective-permute-start(bf16[288,256]{1,0:T(8,128)(2,1)} %get-tuple-element.21), channel_id=1, source_target_pairs={{0,4},{1,5},{2,6},{3,7},{4,0},{5,1},{6,2},{7,3},{8,12},{9,13},{10,... | collective-permute-start | bytes 442376 | tf_op jit(solution)/shard_map/ppermute | solution.py:371
  385.7 17.8 %collective-permute-start.47 = (bf16[288,256]{1,0:T(8,128)(2,1)}, bf16[288,256]{1,0:T(8,128)(2,1)S(1)}, u32[]{:S(2)}, u32[]{:S(2)}) collective-permute-start(bf16[288,256]{1,0:T(8,128)(2,1)} %get-tuple-element.28), channel_id=1, source_target_pairs={{0,2},{1,3},{2,4},{3,5},{4,6},{5,7},{6,0},{7,1},{8,10},{9,11},{10,... | collective-permute-start | bytes 442376 | tf_op jit(solution)/shard_map/ppermute | solution.py:371
  389.4 15.6 %collective-permute-start.28 = (bf16[288,256]{1,0:T(8,128)(2,1)}, bf16[288,256]{1,0:T(8,128)(2,1)S(1)}, u32[]{:S(2)}, u32[]{:S(2)}) collective-permute-start(bf16[288,256]{1,0:T(8,128)(2,1)} %get-tuple-element.22), channel_id=1, source_target_pairs={{0,2},{1,3},{2,4},{3,5},{4,6},{5,7},{6,0},{7,1},{8,10},{9,11},{10,... | collective-permute-start | bytes 442376 | tf_op jit(solution)/shard_map/ppermute | solution.py:371
  402.9 10.1 %collective-permute-start.24 = (bf16[576,256]{1,0:T(8,128)(2,1)}, bf16[576,256]{1,0:T(8,128)(2,1)S(1)}, u32[]{:S(2)}, u32[]{:S(2)}) collective-permute-start(bf16[576,256]{1,0:T(8,128)(2,1)} %constant_dynamic-update-slice_fusion.refs_0_), channel_id=1, source_target_pairs={{0,8},{8,0},{16,24},{24,16},{1,9},{9,1},{17,25},{25,17},{2,10},{10... | collective-permute-start | bytes 884744 | tf_op jit(solution)/shard_map/ppermute | solution.py:45
  403.5 15.9 %collective-permute-start.43 = (bf16[576,256]{1,0:T(8,128)(2,1)S(1)}, bf16[576,256]{1,0:T(8,128)(2,1)S(1)}, u32[]{:S(2)}, u32[]{:S(2)}) collective-permute-start(bf16[576,256]{1,0:T(8,128)(2,1)S(1)} %constant_dynamic-update-slice_fusion.4.refs_0_), channel_id=1, source_target_pairs={{0,8},{8,0},{16,24},{24,16},{1,9},{9,1},{17,25},{25,17},{2,10},{10... | collective-permute-start | bytes 884744 | tf_op jit(solution)/shard_map/ppermute | solution.py:45
  405.0 15.9 %collective-permute-start.48 = (bf16[576,256]{1,0:T(8,128)(2,1)S(1)}, bf16[576,256]{1,0:T(8,128)(2,1)S(1)}, u32[]{:S(2)}, u32[]{:S(2)}) collective-permute-start(bf16[576,256]{1,0:T(8,128)(2,1)S(1)} %constant_dynamic-update-slice_fusion.6.refs_4_), channel_id=1, source_target_pairs={{0,16},{8,24},{16,0},{24,8},{1,17},{9,25},{17,1},{25,9},{2,18},{10... | collective-permute-start | bytes 884744 | tf_op jit(solution)/shard_map/ppermute | solution.py:45
  406.6 14.8 %collective-permute-start.29 = (bf16[576,256]{1,0:T(8,128)(2,1)S(1)}, bf16[576,256]{1,0:T(8,128)(2,1)S(1)}, u32[]{:S(2)}, u32[]{:S(2)}) collective-permute-start(bf16[576,256]{1,0:T(8,128)(2,1)S(1)} %constant_dynamic-update-slice_fusion.2.refs_4_), channel_id=1, source_target_pairs={{0,16},{8,24},{16,0},{24,8},{1,17},{9,25},{17,1},{25,9},{2,18},{10... | collective-permute-start | bytes 884744 | tf_op jit(solution)/shard_map/ppermute | solution.py:45
  407.2 20.4 %collective-permute-start.44 = (bf16[576,256]{1,0:T(8,128)(2,1)S(1)}, bf16[576,256]{1,0:T(8,128)(2,1)S(1)}, u32[]{:S(2)}, u32[]{:S(2)}) collective-permute-start(bf16[576,256]{1,0:T(8,128)(2,1)S(1)} %constant_dynamic-update-slice_fusion.4.refs_0_), channel_id=1, source_target_pairs={{0,16},{8,24},{16,0},{24,8},{1,17},{9,25},{17,1},{25,9},{2,18},{10... | collective-permute-start | bytes 884744 | tf_op jit(solution)/shard_map/ppermute | solution.py:45
  413.0 15.1 %collective-permute-start.49 = (bf16[576,256]{1,0:T(8,128)(2,1)S(1)}, bf16[576,256]{1,0:T(8,128)(2,1)S(1)}, u32[]{:S(2)}, u32[]{:S(2)}) collective-permute-start(bf16[576,256]{1,0:T(8,128)(2,1)S(1)} %constant_dynamic-update-slice_fusion.6.refs_4_), channel_id=1, source_target_pairs={{0,8},{8,0},{16,24},{24,16},{1,9},{9,1},{17,25},{25,17},{2,10},{10... | collective-permute-start | bytes 884744 | tf_op jit(solution)/shard_map/ppermute | solution.py:45
  419.3 14.6 %collective-permute-start.45 = (bf16[576,256]{1,0:T(8,128)(2,1)S(1)}, bf16[576,256]{1,0:T(8,128)(2,1)S(1)}, u32[]{:S(2)}, u32[]{:S(2)}) collective-permute-start(bf16[576,256]{1,0:T(8,128)(2,1)S(1)} %collective-permute-done.43.refs_1_), channel_id=1, source_target_pairs={{0,16},{8,24},{16,0},{24,8},{1,17},{9,25},{17,1},{25,9},{2,18},{10... | collective-permute-start | bytes 884744 | tf_op jit(solution)/shard_map/ppermute | solution.py:45
  420.9 13.7 %collective-permute-start.50 = (bf16[576,256]{1,0:T(8,128)(2,1)S(1)}, bf16[576,256]{1,0:T(8,128)(2,1)}, u32[]{:S(2)}, u32[]{:S(2)}) collective-permute-start(bf16[576,256]{1,0:T(8,128)(2,1)S(1)} %collective-permute-done.48.refs_5_), channel_id=1, source_target_pairs={{0,8},{8,0},{16,24},{24,16},{1,9},{9,1},{17,25},{25,17},{2,10},{10... | collective-permute-start | bytes 884744 | tf_op jit(solution)/shard_map/ppermute | solution.py:45
  421.4 24.3 %collective-permute-start.25 = (bf16[576,256]{1,0:T(8,128)(2,1)}, bf16[576,256]{1,0:T(8,128)(2,1)}, u32[]{:S(2)}, u32[]{:S(2)}) collective-permute-start(bf16[576,256]{1,0:T(8,128)(2,1)} %constant_dynamic-update-slice_fusion.refs_0_), channel_id=1, source_target_pairs={{0,16},{8,24},{16,0},{24,8},{1,17},{9,25},{17,1},{25,9},{2,18},{10... | collective-permute-start | bytes 884744 | tf_op jit(solution)/shard_map/ppermute | solution.py:45
  427.6 18.1 %collective-permute-start.30 = (bf16[576,256]{1,0:T(8,128)(2,1)S(1)}, bf16[576,256]{1,0:T(8,128)(2,1)}, u32[]{:S(2)}, u32[]{:S(2)}) collective-permute-start(bf16[576,256]{1,0:T(8,128)(2,1)S(1)} %constant_dynamic-update-slice_fusion.2.refs_4_), channel_id=1, source_target_pairs={{0,8},{8,0},{16,24},{24,16},{1,9},{9,1},{17,25},{25,17},{2,10},{10... | collective-permute-start | bytes 884744 | tf_op jit(solution)/shard_map/ppermute | solution.py:45
  428.1 17.6 %collective-permute-start.26 = (bf16[576,256]{1,0:T(8,128)(2,1)S(1)}, bf16[576,256]{1,0:T(8,128)(2,1)}, u32[]{:S(2)}, u32[]{:S(2)}) collective-permute-start(bf16[576,256]{1,0:T(8,128)(2,1)S(1)} %collective-permute-done.24.refs_1_), channel_id=1, source_target_pairs={{0,16},{8,24},{16,0},{24,8},{1,17},{9,25},{17,1},{25,9},{2,18},{10... | collective-permute-start | bytes 884744 | tf_op jit(solution)/shard_map/ppermute | solution.py:45
  433.9 11.8 %collective-permute-start.31 = (bf16[576,256]{1,0:T(8,128)(2,1)S(1)}, bf16[576,256]{1,0:T(8,128)(2,1)}, u32[]{:S(2)}, u32[]{:S(2)}) collective-permute-start(bf16[576,256]{1,0:T(8,128)(2,1)S(1)} %collective-permute-done.29.refs_5_), channel_id=1, source_target_pairs={{0,8},{8,0},{16,24},{24,16},{1,9},{9,1},{17,25},{25,17},{2,10},{10... | collective-permute-start | bytes 884744 | tf_op jit(solution)/shard_map/ppermute | solution.py:45
  (20 other events, 375.4 us)
where the time goes:
time: 458 us; the launch traced here: 457 us
  waiting for transfers between devices  181 us (40%)
  starting transfers between devices  144 us (31%)
  Pallas kernels  122 us (27%)
  local copies, waits for them, and re-layouts  8.57 us (2%)
    ppermute x16, starting transfers between devices, around(): return lax.ppermute(value, 'col', ring(images, parts, step))  116 us
    ppermute x24, waiting for transfers between devices, spread(): pieces.append((m ^ d, lax.ppermute(b, 'row', perm)))  90.9 us
    ppermute x16, waiting for transfers between devices, around(): return lax.ppermute(value, 'col', ring(images, parts, step))  89.9 us
    pallas_call x2, Pallas kernels, attend(): pl.pallas_call(functools.partial(attend_kernel, images, heads), in_specs=...  31 us
    pallas_call x4, Pallas kernels, normalize(): pl.pallas_call(functools.partial(norm_kernel, masks, images, parts), grid...  26.5 us
    pallas_call x1, Pallas kernels, project_early(): pl.pallas_call(functools.partial(early_kernel, steps, parts, tags), in_sp...  26.1 us
    ppermute x24, starting transfers between devices, spread(): pieces.append((m ^ d, lax.ppermute(b, 'row', perm)))  25.6 us
    pallas_call x2, Pallas kernels, project_out(): pl.pallas_call(functools.partial(out_kernel, images, parts, head_row, beg...  21.8 us
  transfers between devices with their start and end apart: 51, of which 15 were waited for; matrix products, arithmetic and copies ran while one was open for 1% of the time, Pallas kernels for 24%

commit v1 on v0

v1 whole, which is shorter than its diff:
```python
import functools
import math

import jax
import jax.numpy as jnp
from jax import lax
from jax.experimental import pallas as pl
from jax.experimental.pallas import tpu as pltpu
from jax.sharding import PartitionSpec as P

HDIM = 128
CHUNKS = 2
ANY = pl.BlockSpec(memory_space=pl.ANY)
VMEM = pl.BlockSpec(memory_space=pltpu.VMEM)


def ring(images, parts, step):
    return [
        (a * parts + b, ((a + step) % images) * parts + b)
        for a in range(images)
        for b in range(parts)
    ]


def group(images, parts, step):
    return [
        (a * parts + b, a * parts + (b + step) % parts)
        for a in range(images)
        for b in range(parts)
    ]


def tile_of(rows, limit):
    return max(t for t in range(16, limit + 1, 16) if rows % t == 0)


def cost(flops, moved, exps=0):
    return pl.CostEstimate(flops=flops, bytes_accessed=moved, transcendentals=exps)


def spread(block, rows, dims):
    pieces, n = [(0, block)], 0
    for d in dims:
        perm = [(a, a ^ d) for a in range(rows)]
        for m, b in list(pieces):
            pieces.append((m ^ d, lax.ppermute(b, "row", perm)))
            n += 1
    return pieces


def source_of(image, slot):
    table = ((0, 1, 2, 3), (1, 0, 2, 3), (2, 3, 1, 0), (3, 2, 1, 0))
    return sum(jnp.where(image == a, row[slot], 0) for a, row in enumerate(table))


def slot_of(image, source):
    return sum(jnp.where(source_of(image, slot) == source, slot, 0) for slot in range(4))


PAIRS = ((0, 1), (1, 0), (2, 3), (3, 2))
MIDDLE = ((1, 2), (2, 1))
OUTWARD = ((1, 0), (2, 3))
MIDDLES, ENDS = (1, 2), (0, 3)


def hop(parts, moves):
    return [(a * parts + p, b * parts + p) for a, b in moves for p in range(parts)]


def norm_kernel(masks, parts, gain_ref, bias_ref, *refs):
    pieces, out_ref = refs[: len(masks)], refs[-1]
    me = lax.axis_index("row")
    image = lax.axis_index("col") // parts
    width = pieces[0].shape[1]
    span = out_ref.shape[3]
    grain = min(width, span)
    total = width * len(pieces)
    floats = [ref[...].astype(jnp.float32) for ref in pieces]
    center = sum(jnp.sum(f, axis=-1, keepdims=True) for f in floats) / total
    floats = [f - center for f in floats]
    scatter = sum(jnp.sum(f * f, axis=-1, keepdims=True) for f in floats) / total
    scale = lax.rsqrt(scatter + 1e-06)
    for mask, f in zip(masks, floats):
        for part in range(width // grain):
            first = (me ^ mask) * width + part * grain
            at = pl.ds(pl.multiple_of(first, 128), grain)
            slot = slot_of(image, first // span)
            to = pl.ds(pl.multiple_of(first % span, 128), grain)
            value = f[:, part * grain : (part + 1) * grain] * scale
            out_ref[0, slot, :, to] = (value * gain_ref[:, at] + bias_ref[:, at]).astype(
                out_ref.dtype
            )


def normalize(k, held, pieces, gain, bias, images, parts):
    masks = [m for m, _ in pieces]
    rows, width = pieces[0][1].shape
    total = width * len(pieces)
    tile = tile_of(rows, 48)
    shape = (images, images, rows, total // images)
    whole = pl.BlockSpec((1, total), lambda t: (0, 0))
    extra = [] if held is None else [held]
    return pl.pallas_call(
        functools.partial(norm_kernel, masks, parts),
        grid=(rows // tile,),
        in_specs=[whole, whole]
        + [pl.BlockSpec((tile, width), lambda t: (t, 0))] * len(pieces)
        + [ANY] * len(extra),
        out_specs=pl.BlockSpec((1, images, tile, total // images), lambda t: (k, 0, t, 0)),
        out_shape=jax.ShapeDtypeStruct(shape, jnp.bfloat16),
        input_output_aliases={2 + len(pieces): 0} if extra else {},
        cost_estimate=cost(8 * rows * total, 4 * rows * total, rows),
        name="norm",
        compiler_params=pltpu.CompilerParams(vmem_limit_bytes=16 << 20),
    )(gain[None], bias[None], *[b for _, b in pieces], *extra)


def piece_copies(w_refs, tags, parts, w_v, sems, first):
    image, part = lax.axis_index("col") // parts, lax.axis_index("col") % parts
    columns = w_v.shape[1]
    waits = {}
    for ref, (slot, turn, holders) in zip(w_refs, tags):
        depth, wide = ref.shape
        at = pl.multiple_of(((part + parts - turn) % parts) * depth, 16)
        source = ref.at[:, pl.ds(first, columns)] if wide > columns else ref
        to = w_v.at[pl.ds(slot * parts * depth + at, depth)]
        copy = pltpu.make_async_copy(source, to, sems.at[slot * parts + turn])
        waits[slot, turn] = copy
        if holders is None:
            copy.start()
        else:
            held = functools.reduce(jnp.logical_or, [image == a for a in holders])
            pl.when(held)(copy.start)
    return list(waits.values())


def early_kernel(steps, parts, tags, first, x_ref, *refs):
    w_refs = refs[: len(tags)]
    out_ref, x_v, w_v, o_v, x_sem, w_sem, o_sem = refs[len(tags) :]
    images, _, _, span = x_ref.shape

    def load(k, s):
        to = x_v.at[k, :, pl.ds(s * span, span)]
        return pltpu.make_async_copy(x_ref.at[k, s], to, x_sem.at[k, s])

    def store(k):
        return pltpu.make_async_copy(o_v.at[k], out_ref.at[k], o_sem.at[k])

    copies = piece_copies(w_refs, tags, parts, w_v, w_sem, first)
    for s in range(steps):
        load(0, s).start()
    for copy in copies:
        copy.wait()

    def block(k, carry):
        for s in range(steps):
            load(k, s).wait()

        @pl.when(k + 1 < images)
        def _():
            for s in range(steps):
                load(k + 1, s).start()

        o_v[k] = jnp.dot(x_v[k], w_v[...], preferred_element_type=jnp.float32)
        store(k).start()
        return carry

    lax.fori_loop(0, images, block, 0)
    for k in range(images):
        store(k).wait()


def project_early(normed, pieces, first, columns, parts):
    images, _, rows, span = normed.shape
    tags = [(s, t, a) for s, t, a, _ in pieces]
    steps = images - 1
    tokens = images * rows
    shape = (images, rows, columns)
    return pl.pallas_call(
        functools.partial(early_kernel, steps, parts, tags, first),
        in_specs=[ANY] * (1 + len(pieces)),
        out_specs=ANY,
        out_shape=jax.ShapeDtypeStruct(shape, jnp.float32),
        scratch_shapes=[
            pltpu.VMEM((images, rows, steps * span), jnp.bfloat16),
            pltpu.VMEM((steps * span, columns), jnp.bfloat16),
            pltpu.VMEM(shape, jnp.float32),
            pltpu.SemaphoreType.DMA((images, steps)),
            pltpu.SemaphoreType.DMA((steps * parts,)),
            pltpu.SemaphoreType.DMA((images,)),
        ],
        cost_estimate=cost(2 * tokens * steps * span * columns, 2 * tokens * span * steps),
        name="early",
        compiler_params=pltpu.CompilerParams(vmem_limit_bytes=30 << 20),
    )(normed, *[w for _, _, _, w in pieces])


def late_kernel(parts, heads, tags, x_ref, acc_ref, *refs):
    w_refs = refs[: len(tags)]
    q_ref, kv_ref, x_v, a_v, w_v, x_sem, a_sem, w_sem = refs[len(tags) :]
    images, _, rows, _ = x_ref.shape
    copies = piece_copies(w_refs, [(0, t, a) for _, t, a in tags], parts, w_v, w_sem, 0)

    half = images // 2

    def loads(n):
        return [
            pltpu.make_async_copy(
                x_ref.at[n * half + k, images - 1],
                x_v.at[n, pl.ds(k * rows, rows)],
                x_sem.at[n * half + k],
            )
            for k in range(half)
        ] + [
            pltpu.make_async_copy(
                acc_ref.at[n * half + k], a_v.at[n, pl.ds(k * rows, rows)], a_sem.at[n * half + k]
            )
            for k in range(half)
        ]

    for n in range(2):
        for load in loads(n):
            load.start()
    for copy in copies:
        copy.wait()

    def block(n, carry):
        for load in loads(n):
            load.wait()
        got = a_v[n] + jnp.dot(x_v[n], w_v[...], preferred_element_type=jnp.float32)
        got = got.astype(jnp.bfloat16)
        own = pl.ds(pl.multiple_of(n * half * rows, 16), half * rows)
        for h in range(heads):
            at = 3 * HDIM * h
            q_ref[own, h * HDIM : (h + 1) * HDIM] = got[:, at : at + HDIM]
            kv_ref[own, 2 * h * HDIM : 2 * (h + 1) * HDIM] = got[:, at + HDIM : at + 3 * HDIM]
        return carry

    lax.fori_loop(0, 2, block, 0)


def project_late(normed, acc, pieces, parts):
    images, _, rows, span = normed.shape
    columns = pieces[0][3].shape[1]
    heads = columns // (3 * HDIM)
    tags = [(s, t, a) for s, t, a, _ in pieces]
    tokens = images * rows
    return pl.pallas_call(
        functools.partial(late_kernel, parts, heads, tags),
        in_specs=[ANY] * (2 + len(pieces)),
        out_specs=[VMEM, VMEM],
        out_shape=[
            jax.ShapeDtypeStruct((tokens, heads * HDIM), jnp.bfloat16),
            jax.ShapeDtypeStruct((tokens, 2 * heads * HDIM), jnp.bfloat16),
        ],
        scratch_shapes=[
            pltpu.VMEM((2, tokens // 2, span), jnp.bfloat16),
            pltpu.VMEM((2, tokens // 2, columns), jnp.float32),
            pltpu.VMEM((span, columns), jnp.bfloat16),
            pltpu.SemaphoreType.DMA((images,)),
            pltpu.SemaphoreType.DMA((images,)),
            pltpu.SemaphoreType.DMA((parts,)),
        ],
        cost_estimate=cost(2 * tokens * span * columns, 8 * tokens * columns),
        name="late",
        compiler_params=pltpu.CompilerParams(vmem_limit_bytes=24 << 20),
    )(normed, acc, *[w for _, _, _, w in pieces])


def attend_kernel(first, slots, heads, q_ref, *refs):
    kv_refs, out_refs = refs[:-slots], refs[-slots:]
    rows = out_refs[0].shape[0]
    scale = HDIM ** (-0.5) * math.log2(math.e)
    own = slice(first * rows, (first + slots) * rows)
    for h in range(heads):
        query = q_ref[own, h * HDIM : (h + 1) * HDIM]
        scores = [
            lax.dot_general(
                query,
                ref[:, 2 * h * HDIM : (2 * h + 1) * HDIM],
                (((1,), (1,)), ((), ())),
                preferred_element_type=jnp.float32,
            )
            for ref in kv_refs
        ]
        peak = functools.reduce(jnp.maximum, [jnp.max(s, axis=-1, keepdims=True) for s in scores])
        peak = peak * scale
        both = 0.0
        for s, ref in zip(scores, kv_refs):
            expo = jnp.exp2(s * scale - peak).astype(jnp.bfloat16)
            value = ref[:, (2 * h + 1) * HDIM : 2 * (h + 1) * HDIM]
            value = jnp.concatenate([value, jnp.ones_like(value)], axis=1)
            both += jnp.dot(expo, value, preferred_element_type=jnp.float32)
        got = (both[:, :HDIM] / both[:, HDIM:]).astype(jnp.bfloat16)
        for m in range(slots):
            out_refs[m][:, h * HDIM : (h + 1) * HDIM] = got[m * rows : (m + 1) * rows]


def attend(query, pairs, images, first, slots):
    tokens, wide = query.shape
    rows, heads = tokens // images, wide // HDIM
    keys = tokens * len(pairs)
    return pl.pallas_call(
        functools.partial(attend_kernel, first, slots, heads),
        in_specs=[VMEM] * (1 + len(pairs)),
        out_specs=[VMEM] * slots,
        out_shape=[jax.ShapeDtypeStruct((rows, wide), jnp.bfloat16)] * slots,
        cost_estimate=cost(
            8 * heads * slots * rows * keys * HDIM,
            4 * heads * HDIM * (tokens + keys),
            heads * slots * rows * keys,
        ),
        name="attend",
        compiler_params=pltpu.CompilerParams(vmem_limit_bytes=32 << 20),
    )(query, *pairs)


def out_kernel(parts, turns, tags, w_tags, base_ref, *refs):
    w_refs, refs = refs[: len(w_tags)], refs[len(w_tags) :]
    o_refs = refs[: len(tags)]
    out_ref, o_v, w_v, b_v, r_v, o_sem, w_sem, b_sem, r_sem = refs[len(tags) :]
    me, col = lax.axis_index("row"), lax.axis_index("col")
    images, rows, columns = base_ref.shape
    image, part = col // parts, col % parts
    half = images // 2
    spots = [(image + k) % images for k in turns]
    cuts = column_cuts(columns)
    heads = [[], []]
    for n, (chunk, mask, block) in enumerate(tags):
        size, width = o_refs[n].shape
        at = pl.multiple_of(((me ^ mask) * CHUNKS + chunk) * width, 128)
        to = o_v.at[pl.ds(block * rows, size), pl.ds(at, width)]
        heads[block // half].append(pltpu.make_async_copy(o_refs[n], to, o_sem.at[n]))
    weights = []
    for m, (begin, size) in enumerate(cuts):
        for n, (step, turn) in enumerate(w_tags):
            depth = w_refs[n].shape[0]
            place = ((image + images - step) % images) * parts + (part + parts - turn) % parts
            at = pl.multiple_of(place * depth, 16)
            span = pl.ds(begin, size)
            weights.append(
                pltpu.make_async_copy(
                    w_refs[n].at[:, span], w_v.at[pl.ds(at, depth), span], w_sem.at[m, n]
                )
            )
    bases = [
        pltpu.make_async_copy(base_ref.at[spot], b_v.at[n], b_sem.at[n])
        for n, spot in enumerate(spots)
    ]
    per = len(w_tags)
    for copy in heads[0] + weights[:per] + heads[1] + bases + weights[per:]:
        copy.start()
    for copy in heads[0] + heads[1]:
        copy.wait()

    def store(m, n, spot):
        span = pl.ds(*cuts[m])
        return pltpu.make_async_copy(
            r_v.at[n, :, span], out_ref.at[spot, :, span], r_sem.at[m, n]
        )

    for m, (begin, size) in enumerate(cuts):
        for copy in weights[m * per : (m + 1) * per]:
            copy.wait()
        if m == 0:
            for copy in bases:
                copy.wait()

        def body(block, carry, m=m, begin=begin, size=size):
            at = pl.ds(pl.multiple_of(block * half * rows, 16), half * rows)
            got = jnp.dot(
                o_v[at, :], w_v[:, begin : begin + size], preferred_element_type=jnp.float32
            )
            for k in range(half):
                n = block * half + k
                mine = got[k * rows : (k + 1) * rows]
                r_v[n, :, begin : begin + size] = (
                    b_v[n, :, begin : begin + size].astype(jnp.float32) + mine
                ).astype(r_v.dtype)
                store(m, n, jnp.where(block == 0, spots[k], spots[half + k])).start()
            return carry

        lax.fori_loop(0, 2, body, 0)
    for m in range(len(cuts)):
        for n, spot in enumerate(spots):
            store(m, n, spot).wait()


def column_cuts(columns):
    first = -(-columns // 512) * 256
    return ((0, first), (first, columns - first))


def project_out(base, w_pieces, pieces, parts, row_count, turns):
    tags = [(chunk, m, block) for chunk, m, block, _ in pieces]
    w_tags = [(s, t) for s, t, _ in w_pieces]
    images, rows, columns = base.shape
    width = pieces[0][3].shape[1]
    deep = len(w_pieces) * w_pieces[0][2].shape[0]
    cuts = len(column_cuts(columns))
    return pl.pallas_call(
        functools.partial(out_kernel, parts, turns, tags, w_tags),
        in_specs=[ANY] * (1 + len(w_tags) + len(tags)),
        out_specs=ANY,
        out_shape=jax.ShapeDtypeStruct(base.shape, jnp.bfloat16),
        scratch_shapes=[
            pltpu.VMEM((images * rows, row_count * CHUNKS * width), jnp.bfloat16),
            pltpu.VMEM((deep, columns), jnp.bfloat16),
            pltpu.VMEM(base.shape, base.dtype),
            pltpu.VMEM(base.shape, jnp.bfloat16),
            pltpu.SemaphoreType.DMA((len(tags),)),
            pltpu.SemaphoreType.DMA((cuts, len(w_tags))),
            pltpu.SemaphoreType.DMA((images,)),
            pltpu.SemaphoreType.DMA((cuts, images)),
        ],
        cost_estimate=cost(2 * images * rows * columns * deep, 8 * images * rows * columns),
        name="out",
        compiler_params=pltpu.CompilerParams(vmem_limit_bytes=30 << 20),
    )(base, *[w for _, _, w in w_pieces], *[o for _, _, _, o in pieces])


def local(pixels_tokens, ln_gain, ln_bias, w_qkv, w_out):
    images, _, _ = pixels_tokens.shape
    row_count = lax.axis_size("row")
    col_count = lax.axis_size("col")
    parts = col_count // images
    head_row = w_qkv.shape[1] // (3 * HDIM)
    heads = head_row // CHUNKS
    image = lax.axis_index("col") // parts
    dims = [1 << n for n in range(row_count.bit_length() - 1)]

    def around(value, step):
        if step % images == 0:
            return value
        return lax.ppermute(value, "col", ring(images, parts, step))

    def swaps(step, shard):
        return [(step, 0, shard)] + [
            (step, t, lax.ppermute(shard, "col", group(images, parts, t)))
            for t in range(1, parts)
        ]

    shifts = SLOTS(images)
    blocks = []
    for k in shifts:
        block = lax.dynamic_index_in_dim(pixels_tokens, (image + k) % images, 0, keepdims=False)
        blocks.append(around(block, k))
    normed = None
    for slot in NORMS(images):
        k = shifts[slot]
        turned = dims[k % len(dims) :] + dims[: k % len(dims)]
        pieces = spread(blocks[slot], row_count, turned)
        normed = normalize(slot, normed, pieces, ln_gain, ln_bias, images, parts)

    columns = heads * 3 * HDIM
    own = [(0, t, None, w) for _, t, w in swaps(0, w_qkv)]

    def arrive(slot, holders, value, moves):
        got = lax.ppermute(value, "col", hop(parts, moves))
        there = [(a, a) for a in (holders or range(images))]
        turned = [(slot, 0, holders, got)]
        for t in range(1, parts):
            perm = [
                (a * parts + p, a * parts + (p + t) % parts) for a, _ in there for p in range(parts)
            ]
            turned.append((slot, t, holders, lax.ppermute(got, "col", perm)))
        return got, turned

    results = []
    for j in range(CHUNKS):
        shard = w_qkv[:, j * columns : (j + 1) * columns]
        near, one = arrive(1, None, shard, PAIRS)
        across, two = arrive(2, MIDDLES, shard, MIDDLE)
        _, three = arrive(2, ENDS, across, OUTWARD)
        far, four = arrive(3, MIDDLES, near, MIDDLE)
        _, five = arrive(3, ENDS, far, OUTWARD)
        first = own + one + two + three
        acc = project_early(normed, first, j * columns, columns, parts)
        query, pair = project_late(normed, acc, four + five, parts)
        pairs = [pair] + [
            lax.ppermute(pair, "col", group(images, parts, t)) for t in range(1, parts)
        ]
        half = images // 2
        outs = []
        for n in range(2):
            mine = shifts[n * half : (n + 1) * half]
            got = attend(query, pairs, images, n * half, half)
            outs += [around(o, -k) for k, o in zip(mine, got)]
        if j + 1 < CHUNKS:
            pieces = []
            for n in range(2):
                joined = jnp.concatenate(outs[n * half : (n + 1) * half], axis=0)
                turned = dims[n:] + dims[:n]
                pieces += [(n * half, spread(joined, row_count, turned))]
            results.append(pieces)
            continue
        pieces = []
        for n, (k, o) in enumerate(zip(shifts, outs)):
            turned = dims[n % len(dims) :] + dims[: n % len(dims)]
            pieces.append((n, spread(o, row_count, turned)))
        results.append(pieces)

    shard, out_pieces = w_out, []
    for step in range(images):
        out_pieces += swaps(step, shard)
        if step + 1 < images:
            shard = around(shard, 1)
    pieces = [
        (j, m, n, o) for j in range(CHUNKS) for n, got in results[j] for m, o in got
    ]
    return project_out(pixels_tokens, out_pieces, pieces, parts, row_count, shifts)


def SLOTS(images):
    return sorted(range(1, images), key=lambda k: (min(k, images - k), k)) + [0]


def NORMS(images):
    return [images - 1, 0] + list(range(images - 2, 0, -1))


def solution(mesh):
    in_specs = (P(None, "col", "row"), P(), P(), P("col", "row"), P("col", "row"))
    out_specs = P(None, "col", "row")

    def whole(pixels_tokens, *rest):
        step = jax.shard_map(
            local, mesh=mesh, in_specs=in_specs, out_specs=out_specs, check_vma=False
        )
        return step(pixels_tokens, *rest)

    return whole
```

time: 458 us -> 411 us (0.90)
  starting transfers between devices: 144 us -> 78.2 us
  waiting for transfers between devices: 181 us -> 243 us
  Pallas kernels: 122 us -> 75 us
  local copies, waits for them, and re-layouts: 8.57 us -> 13.4 us
    ppermute x16 -> x12, starting transfers between devices: 116 us -> 15.7 us  [around(): return lax.ppermute(value, 'col', ring(images, parts, step))]
    ppermute x0 -> x20, waiting for transfers between devices: none -> 69.5 us  [the longest x10 69.5 us: arrive(): got = lax.ppermute(value, 'col', hop(parts, moves))]
    pallas_call x11 -> x13, Pallas kernels: 122 us -> 75 us  [the longest x2 23.4 us: project_early(): pl.pallas_call(functools.partial(early_kernel, steps, parts, tags, first)...]
    ppermute x0 -> x20, starting transfers between devices: none -> 23.3 us  [the longest x10 12.8 us: arrive(): turned.append((slot, t, holders, lax.ppermute(got, 'col', perm)))]
    ppermute x24 -> x30, waiting for transfers between devices: 90.9 us -> 73.8 us  [spread(): pieces.append((m ^ d, lax.ppermute(b, 'row', perm)))]
    ppermute x24 -> x30, starting transfers between devices: 25.6 us -> 37.6 us  [spread(): pieces.append((m ^ d, lax.ppermute(b, 'row', perm)))]
    ppermute x16 -> x12, waiting for transfers between devices: 89.9 us -> 100 us  [around(): return lax.ppermute(value, 'col', ring(images, parts, step))]
    unnamed x70 -> x44, local copies, waits for them, and re-layouts: 4.51 us -> 11.2 us
  transfers between devices with their start and end apart: 51 -> 69, of which waited for: 15 -> 25; matrix products, arithmetic and copies ran while one was open for 1% -> 1% of each run, Pallas kernels for 24% -> 16%
where the time goes in v1:
time: 411 us
  waiting for transfers between devices  243 us (59%)
  starting transfers between devices  78.2 us (19%)
  Pallas kernels  75 us (18%)
  local copies, waits for them, and re-layouts  13.4 us (3%)
    ppermute x12, waiting for transfers between devices, around(): return lax.ppermute(value, 'col', ring(images, parts, step))  100 us
    ppermute x30, waiting for transfers between devices, spread(): pieces.append((m ^ d, lax.ppermute(b, 'row', perm)))  73.8 us
    ppermute x10, waiting for transfers between devices, arrive(): got = lax.ppermute(value, 'col', hop(parts, moves))  69.5 us
    ppermute x30, starting transfers between devices, spread(): pieces.append((m ^ d, lax.ppermute(b, 'row', perm)))  37.6 us
    pallas_call x2, Pallas kernels, project_early(): pl.pallas_call(functools.partial(early_kernel, steps, parts, tags, first)...  23.4 us
    pallas_call x4, Pallas kernels, attend(): pl.pallas_call(functools.partial(attend_kernel, first, slots, heads), in_...  16.5 us
    ppermute x12, starting transfers between devices, around(): return lax.ppermute(value, 'col', ring(images, parts, step))  15.7 us
    pallas_call x4, Pallas kernels, normalize(): pl.pallas_call(functools.partial(norm_kernel, masks, parts), grid=(rows /...  13.7 us
  transfers between devices with their start and end apart: 69, of which 25 were waited for; matrix products, arithmetic and copies ran while one was open for 1% of the time, Pallas kernels for 16%

profile of v1, /device:TPU:0, one launch (start us, length us, event | category | flops | bytes accessed | tf_op | source)
XLA Modules:
  0.0 410.7 jit_solution(8432007121699739283)
XLA Ops:
  0.0 3.1 collective-permute-start.1
  3.1 2.1 dynamic-slice_bitcast_fusion
  5.2 1.6 collective-permute-start.19
  6.8 1.5 collective-permute-start.20
  8.3 1.6 collective-permute-start.15
  11.2 9.9 %collective-permute-done.1.refs_2_ = bf16[256,1280]{1,0:T(8,128)(2,1)} collective-permute-done((bf16[256,1280]{1,0:T(8,128)(2,1)}, bf16[256,1280]{1,0:T(8,128)(2,1)}, u32[]{:S(2)}, u32[]{:S(2)}) %collective-permute-start.1) | collective-permute-done | bytes 655392 | tf_op jit(solution)/shard_map/ppermute | solution.py:435
  23.2 1.6 collective-permute-start.43
  24.8 2.5 collective-permute-start.7
  27.3 9.5 %collective-permute-done.15.refs_0_ = bf16[288,1280]{1,0:T(8,128)(2,1)S(1)} collective-permute-done((bf16[288,1280]{1,0:T(8,128)(2,1)S(1)}, bf16[288,1280]{1,0:T(8,128)(2,1)S(1)}, u32[]{:S(2)}, u32[]{:S(2)}) %collective-permute-start.15) | collective-permute-done | bytes 737312 | tf_op jit(solution)/shard_map/ppermute | solution.py:435
  37.5 30.1 %collective-permute-done.11.refs_0_ = bf16[288,1280]{1,0:T(8,128)(2,1)S(1)} collective-permute-done((bf16[288,1280]{1,0:T(8,128)(2,1)S(1)}, bf16[288,1280]{1,0:T(8,128)(2,1)S(1)}, u32[]{:S(2)}, u32[]{:S(2)}) %collective-permute-start.11) | collective-permute-done | bytes 737312 | tf_op jit(solution)/shard_map/ppermute | solution.py:435
  67.6 21.0 %collective-permute-done.7.refs_0_ = bf16[288,1280]{1,0:T(8,128)(2,1)S(1)} collective-permute-done((bf16[288,1280]{1,0:T(8,128)(2,1)S(1)}, bf16[288,1280]{1,0:T(8,128)(2,1)S(1)}, u32[]{:S(2)}, u32[]{:S(2)}) %collective-permute-start.7) | collective-permute-done | bytes 737312 | tf_op jit(solution)/shard_map/ppermute | solution.py:435
  88.6 1.5 collective-permute-start.21
  90.6 1.5 collective-permute-start.17
  92.6 17.0 %collective-permute-done.23.refs_2_ = bf16[640,768]{1,0:T(8,128)(2,1)} collective-permute-done((bf16[640,768]{1,0:T(8,128)(2,1)S(1)}, bf16[640,768]{1,0:T(8,128)(2,1)}, u32[]{:S(2)}, u32[]{:S(2)}) %collective-permute-start.23) | collective-permute-done | bytes 983072 | tf_op jit(solution)/shard_map/ppermute | solution.py:459
  109.7 1.5 collective-permute-start.13
  111.7 12.1 %collective-permute-done.16.refs_1_ = bf16[288,1280]{1,0:T(8,128)(2,1)S(1)} collective-permute-done((bf16[288,1280]{1,0:T(8,128)(2,1)S(1)}, bf16[288,1280]{1,0:T(8,128)(2,1)S(1)}, u32[]{:S(2)}, u32[]{:S(2)}) %collective-permute-start.16) | collective-permute-done | bytes 737312 | tf_op jit(solution)/shard_map/ppermute | solution.py:46
  123.7 1.5 collective-permute-start.9
  126.5 13.0 %collective-permute-done.13.refs_2_ = bf16[288,1280]{1,0:T(8,128)(2,1)S(1)} collective-permute-done((bf16[288,1280]{1,0:T(8,128)(2,1)S(1)}, bf16[288,1280]{1,0:T(8,128)(2,1)S(1)}, u32[]{:S(2)}, u32[]{:S(2)}) %collective-permute-start.13) | collective-permute-done | bytes 737312 | tf_op jit(solution)/shard_map/ppermute | solution.py:46
  139.5 14.8 %collective-permute-done.8.refs_1_ = bf16[288,1280]{1,0:T(8,128)(2,1)S(1)} collective-permute-done((bf16[288,1280]{1,0:T(8,128)(2,1)S(1)}, bf16[288,1280]{1,0:T(8,128)(2,1)S(1)}, u32[]{:S(2)}, u32[]{:S(2)}) %collective-permute-start.8) | collective-permute-done | bytes 737312 | tf_op jit(solution)/shard_map/ppermute | solution.py:46
  155.8 11.0 %collective-permute-done.47.refs_6_ = bf16[640,768]{1,0:T(8,128)(2,1)S(1)} collective-permute-done((bf16[640,768]{1,0:T(8,128)(2,1)S(1)}, bf16[640,768]{1,0:T(8,128)(2,1)S(1)}, u32[]{:S(2)}, u32[]{:S(2)}) %collective-permute-start.47) | collective-permute-done | bytes 983072 | tf_op jit(solution)/shard_map/ppermute | solution.py:459
  168.1 1.6 collective-permute-start.29
  171.0 1.6 collective-permute-start.18
  172.5 1.5 collective-permute-start.14
  174.1 24.5 %collective-permute-done.27.refs_6_ = bf16[640,768]{1,0:T(8,128)(2,1)S(1)} collective-permute-done((bf16[640,768]{1,0:T(8,128)(2,1)S(1)}, bf16[640,768]{1,0:T(8,128)(2,1)S(1)}, u32[]{:S(2)}, u32[]{:S(2)}) %collective-permute-start.27) | collective-permute-done | bytes 983072 | tf_op jit(solution)/shard_map/ppermute | solution.py:459
  198.6 1.9 collective-permute-start.48
  202.6 16.9 %collective-permute-done.51.refs_2_ = bf16[640,768]{1,0:T(8,128)(2,1)S(1)} collective-permute-done((bf16[640,768]{1,0:T(8,128)(2,1)S(1)}, bf16[640,768]{1,0:T(8,128)(2,1)S(1)}, u32[]{:S(2)}, u32[]{:S(2)}) %collective-permute-start.51) | collective-permute-done | bytes 983072 | tf_op jit(solution)/shard_map/ppermute | solution.py:459
  219.5 1.9 collective-permute-start.52
  221.4 1.6 collective-permute-start.10
  223.0 17.4 %collective-permute-done.10.refs_3_ = bf16[288,1280]{1,0:T(8,128)(2,1)S(1)} collective-permute-done((bf16[288,1280]{1,0:T(8,128)(2,1)S(1)}, bf16[288,1280]{1,0:T(8,128)(2,1)S(1)}, u32[]{:S(2)}, u32[]{:S(2)}) %collective-permute-start.10) | collective-permute-done | bytes 737312 | tf_op jit(solution)/shard_map/ppermute | solution.py:46
  240.4 1.6 collective-permute-start.26
  242.0 2.4 collective-permute-start.28
  244.4 3.4 norm.4.refs_4_
  247.8 3.4 norm.5.refs_4_
  251.3 3.4 norm.6.refs_4_
  254.7 3.4 norm.7.x_ref
  258.1 4.3 %copy-done = bf16[4,4,288,1280]{3,2,1,0:T(8,128)(2,1)} copy-done((bf16[4,4,288,1280]{3,2,1,0:T(8,128)(2,1)}, bf16[4,4,288,1280]{3,2,1,0:T(8,128)(2,1)S(1)}, u32[]{:S(2)}) %copy-start) | copy-done | bytes 11796504
  262.4 1.6 collective-permute-start.30
  265.1 1.9 collective-permute-start.32
  267.0 12.0 %early.3.acc_ref = f32[4,288,768]{2,1,0:T(8,128)S(1)} custom-call(bf16[4,4,288,1280]{3,2,1,0:T(8,128)(2,1)} %copy-done, bf16[640,1536]{1,0:T(8,128)(2,1)S(1)} %copy-done.2, bf16[640,1536]{1,0:T(8,128)(2,1)S(1)} %collective-permute-done.22.refs_1_, bf16[640,768]{1,0:T(8,128)(2,1)S(1)} %collective-permute-done.43.refs_2_, ...), custom_call_target="tpu_custom_call" | custom-call | flops 6794772480 | bytes 8847360 | tf_op jit(solution)/shard_map/early/pallas_call | solution.py:179
  279.0 1.7 copy-done.4
  280.8 2.0 copy-done.5
  284.0 6.4 %late.3 = (bf16[1152,256]{1,0:T(8,128)(2,1)S(1)}, bf16[1152,512]{1,0:T(8,128)(2,1)}) custom-call(bf16[4,4,288,1280]{3,2,1,0:T(8,128)(2,1)S(1)} %copy-done.1, f32[4,288,768]{2,1,0:T(8,128)S(1)} %copy-done.5, bf16[640,768]{1,0:T(8,128)(2,1)S(1)} %collective-permute-done.49.refs_0_, bf16[640,768]{1,0:T(8,128)(2,1)S(1)} %collective-permute-done.50.refs_1_, ...), custom_call_target="tpu_custom_call" | custom-call | flops 2264924160 | bytes 7077888 | tf_op jit(solution)/shard_map/late/pallas_call | solution.py:248
  291.8 11.4 %early.2.acc_ref = f32[4,288,768]{2,1,0:T(8,128)S(1)} custom-call(bf16[4,4,288,1280]{3,2,1,0:T(8,128)(2,1)} %copy-done, bf16[640,1536]{1,0:T(8,128)(2,1)S(1)} %copy-done.3, bf16[640,1536]{1,0:T(8,128)(2,1)S(1)} %copy-done.7, bf16[640,768]{1,0:T(8,128)(2,1)} %collective-permute-done.23.refs_2_, bf16[640,768]{1,0:T(8,128)(2,1)} %collective-permute-done.24.refs_3_, ...), custom_call_target="tpu_custom_call" | custom-call | flops 6794772480 | bytes 8847360 | tf_op jit(solution)/shard_map/early/pallas_call | solution.py:179
  303.3 4.7 %late.2 = (bf16[1152,256]{1,0:T(8,128)(2,1)S(1)}, bf16[1152,512]{1,0:T(8,128)(2,1)S(1)}) custom-call(bf16[4,4,288,1280]{3,2,1,0:T(8,128)(2,1)S(1)} %bitcast.11, f32[4,288,768]{2,1,0:T(8,128)S(1)} %early.2.acc_ref, bf16[640,768]{1,0:T(8,128)(2,1)} %collective-permute-done.29.refs_0_, bf16[640,768]{1,0:T(8,128)(2,1)} %collective-permute-done.30.refs_1_, ...), custom_call_target="tpu_custom_call" | custom-call | flops 2264924160 | bytes 7077888 | tf_op jit(solution)/shard_map/late/pallas_call | solution.py:248
  308.3 2.1 collective-permute-done.3.refs_4_
  310.9 17.6 %collective-permute-done.5.refs_6_ = bf16[256,1280]{1,0:T(8,128)(2,1)S(1)} collective-permute-done((bf16[256,1280]{1,0:T(8,128)(2,1)S(1)}, bf16[256,1280]{1,0:T(8,128)(2,1)S(1)}, u32[]{:S(2)}, u32[]{:S(2)}) %collective-permute-start.5) | collective-permute-done | bytes 655392 | tf_op jit(solution)/shard_map/ppermute | solution.py:435
  328.9 4.7 %attend.7 = (bf16[288,256]{1,0:T(8,128)(2,1)S(1)}, bf16[288,256]{1,0:T(8,128)(2,1)S(1)}) custom-call(bf16[1152,256]{1,0:T(8,128)(2,1)S(1)} %copy-done.17, bf16[1152,512]{1,0:T(8,128)(2,1)} %get-tuple-element.24.refs_0_, bf16[1152,512]{1,0:T(8,128)(2,1)S(1)} %collective-permute-done.53.refs_1_), custom_call_target="tpu_custom_call" | custom-call | flops 2717908992 | bytes 3538944 | tf_op jit(solution)/shard_map/attend/pallas_call | solution.py:303
  333.7 4.7 %attend.6 = (bf16[288,256]{1,0:T(8,128)(2,1)S(1)}, bf16[288,256]{1,0:T(8,128)(2,1)S(1)}) custom-call(bf16[1152,256]{1,0:T(8,128)(2,1)S(1)} %copy-done.17, bf16[1152,512]{1,0:T(8,128)(2,1)} %get-tuple-element.24.refs_0_, bf16[1152,512]{1,0:T(8,128)(2,1)S(1)} %collective-permute-done.53.refs_1_), custom_call_target="tpu_custom_call" | custom-call | flops 2717908992 | bytes 3538944 | tf_op jit(solution)/shard_map/attend/pallas_call | solution.py:303
  338.5 3.4 attend.5
  341.9 1.6 collective-permute-start.66
  343.5 2.9 collective-permute-start.39
  346.4 3.7 attend.4
  350.2 1.5 collective-permute-start.67
  353.0 1.8 collective-permute-start.34
  354.9 2.0 collective-permute-start.58
  357.2 1.5 collective-permute-start.63
  360.8 7.5 %collective-permute-done.54.refs_16_ = bf16[288,256]{1,0:T(8,128)(2,1)S(1)} collective-permute-done((bf16[288,256]{1,0:T(8,128)(2,1)S(1)}, bf16[288,256]{1,0:T(8,128)(2,1)S(1)}, u32[]{:S(2)}, u32[]{:S(2)}) %collective-permute-start.54) | collective-permute-done | bytes 147488 | tf_op jit(solution)/shard_map/ppermute | solution.py:435
  376.0 2.1 collective-permute-done.55.refs_17_
  378.1 1.5 collective-permute-start.60
  380.7 4.0 collective-permute-done.56.refs_18_
  384.7 1.5 collective-permute-start.41
  391.5 2.2 collective-permute-done.57.refs_19_
  395.1 3.7 collective-permute-done.61.refs_23_
  400.2 10.3 %out.1 = bf16[4,288,1280]{2,1,0:T(8,128)(2,1)} custom-call(bf16[4,288,1280]{2,1,0:T(8,128)(2,1)S(1)} %copy-done.8, bf16[256,1280]{1,0:T(8,128)(2,1)S(1)} %copy-done.15, bf16[256,1280]{1,0:T(8,128)(2,1)S(1)} %collective-permute-done.refs_1_, bf16[256,1280]{1,0:T(8,128)(2,1)} %collective-permute-done.1.refs_2_, ...), custom_call_target="tpu_custom_call" | custom-call | flops 6039797760 | bytes 11796480 | tf_op jit(solution)/shard_map/out/pallas_call | solution.py:401
  (136 shorter events, 39.0 us)
Async XLA Ops:
  0.0 21.1 %collective-permute-start.1 = (bf16[256,1280]{1,0:T(8,128)(2,1)}, bf16[256,1280]{1,0:T(8,128)(2,1)}, u32[]{:S(2)}, u32[]{:S(2)}) collective-permute-start(bf16[256,1280]{1,0:T(8,128)(2,1)} %refs_0_.5), channel_id=1, source_target_pairs={{0,2},{1,3},{2,4},{3,5},{4,6},{5,7},{6,0},{7,1},{8,10},{9,11},{10,... | collective-permute-start | bytes 1966088 | tf_op jit(solution)/shard_map/ppermute | solution.py:435
  5.2 18.0 %collective-permute-start.19 = (bf16[288,1280]{1,0:T(8,128)(2,1)S(1)}, bf16[288,1280]{1,0:T(8,128)(2,1)S(1)}, u32[]{:S(2)}, u32[]{:S(2)}) collective-permute-start(bf16[288,1280]{1,0:T(8,128)(2,1)S(1)} %get-tuple-element.29.refs_0_), channel_id=1, source_target_pairs={{0,8},{8,0},{16,24},{24,16},{1,9},{9,1},{17,25},{25,17},{2,10},{10... | collective-permute-start | bytes 2211848 | tf_op jit(solution)/shard_map/ppermute | solution.py:46
  6.8 18.0 %collective-permute-start.20 = (bf16[288,1280]{1,0:T(8,128)(2,1)S(1)}, bf16[288,1280]{1,0:T(8,128)(2,1)S(1)}, u32[]{:S(2)}, u32[]{:S(2)}) collective-permute-start(bf16[288,1280]{1,0:T(8,128)(2,1)S(1)} %get-tuple-element.29.refs_0_), channel_id=1, source_target_pairs={{0,16},{8,24},{16,0},{24,8},{1,17},{9,25},{17,1},{25,9},{2,18},{10... | collective-permute-start | bytes 2211848 | tf_op jit(solution)/shard_map/ppermute | solution.py:46
  8.3 28.5 %collective-permute-start.15 = (bf16[288,1280]{1,0:T(8,128)(2,1)S(1)}, bf16[288,1280]{1,0:T(8,128)(2,1)S(1)}, u32[]{:S(2)}, u32[]{:S(2)}) collective-permute-start(bf16[288,1280]{1,0:T(8,128)(2,1)S(1)} %get-tuple-element.30), channel_id=1, source_target_pairs={{0,2},{1,3},{2,4},{3,5},{4,6},{5,7},{6,0},{7,1},{8,10},{9,11},{10,... | collective-permute-start | bytes 2211848 | tf_op jit(solution)/shard_map/ppermute | solution.py:435
  9.8 57.7 %collective-permute-start.11 = (bf16[288,1280]{1,0:T(8,128)(2,1)S(1)}, bf16[288,1280]{1,0:T(8,128)(2,1)S(1)}, u32[]{:S(2)}, u32[]{:S(2)}) collective-permute-start(bf16[288,1280]{1,0:T(8,128)(2,1)S(1)} %get-tuple-element.31), channel_id=1, source_target_pairs={{0,4},{1,5},{2,6},{3,7},{4,0},{5,1},{6,2},{7,3},{8,12},{9,13},{10,... | collective-permute-start | bytes 2211848 | tf_op jit(solution)/shard_map/ppermute | solution.py:435
  21.1 69.0 %collective-permute-start.45 = (bf16[640,768]{1,0:T(8,128)(2,1)S(1)}, bf16[640,768]{1,0:T(8,128)(2,1)S(1)}, u32[]{:S(2)}, u32[]{:S(2)}) collective-permute-start(bf16[640,768]{1,0:T(8,128)(2,1)S(1)} %get-tuple-element.33), channel_id=1, source_target_pairs={{2,4},{3,5},{4,2},{5,3},{10,12},{11,13},{12,10},{13,11},{18,20},{1... | collective-permute-start | bytes 2949128 | tf_op jit(solution)/shard_map/ppermute | solution.py:459
  23.2 67.4 %collective-permute-start.43 = (bf16[640,768]{1,0:T(8,128)(2,1)S(1)}, bf16[640,768]{1,0:T(8,128)(2,1)S(1)}, u32[]{:S(2)}, u32[]{:S(2)}) collective-permute-start(bf16[640,768]{1,0:T(8,128)(2,1)S(1)} %get-tuple-element.33), channel_id=1, source_target_pairs={{0,2},{1,3},{2,0},{3,1},{4,6},{5,7},{6,4},{7,5},{8,10},{9,11},{10,... | collective-permute-start | bytes 2949128 | tf_op jit(solution)/shard_map/ppermute | solution.py:459
  24.8 63.8 %collective-permute-start.7 = (bf16[288,1280]{1,0:T(8,128)(2,1)S(1)}, bf16[288,1280]{1,0:T(8,128)(2,1)S(1)}, u32[]{:S(2)}, u32[]{:S(2)}) collective-permute-start(bf16[288,1280]{1,0:T(8,128)(2,1)S(1)} %get-tuple-element.32), channel_id=1, source_target_pairs={{0,6},{1,7},{2,0},{3,1},{4,2},{5,3},{6,4},{7,5},{8,14},{9,15},{10,... | collective-permute-start | bytes 2211848 | tf_op jit(solution)/shard_map/ppermute | solution.py:435
  36.8 55.3 %collective-permute-start.25 = (bf16[640,768]{1,0:T(8,128)(2,1)S(1)}, bf16[640,768]{1,0:T(8,128)(2,1)S(1)}, u32[]{:S(2)}, u32[]{:S(2)}) collective-permute-start(bf16[640,768]{1,0:T(8,128)(2,1)S(1)} %get-tuple-element.34), channel_id=1, source_target_pairs={{2,4},{3,5},{4,2},{5,3},{10,12},{11,13},{12,10},{13,11},{18,20},{1... | collective-permute-start | bytes 2949128 | tf_op jit(solution)/shard_map/ppermute | solution.py:459
  67.6 42.1 %collective-permute-start.23 = (bf16[640,768]{1,0:T(8,128)(2,1)S(1)}, bf16[640,768]{1,0:T(8,128)(2,1)}, u32[]{:S(2)}, u32[]{:S(2)}) collective-permute-start(bf16[640,768]{1,0:T(8,128)(2,1)S(1)} %get-tuple-element.34), channel_id=1, source_target_pairs={{0,2},{1,3},{2,0},{3,1},{4,6},{5,7},{6,4},{7,5},{8,10},{9,11},{10,... | collective-permute-start | bytes 2949128 | tf_op jit(solution)/shard_map/ppermute | solution.py:459
  88.6 22.6 %collective-permute-start.21 = (bf16[288,1280]{1,0:T(8,128)(2,1)S(1)}, bf16[288,1280]{1,0:T(8,128)(2,1)S(1)}, u32[]{:S(2)}, u32[]{:S(2)}) collective-permute-start(bf16[288,1280]{1,0:T(8,128)(2,1)S(1)} %collective-permute-done.19.refs_1_), channel_id=1, source_target_pairs={{0,16},{8,24},{16,0},{24,8},{1,17},{9,25},{17,1},{25,9},{2,18},{10... | collective-permute-start | bytes 2211848 | tf_op jit(solution)/shard_map/ppermute | solution.py:46
  90.1 33.6 %collective-permute-start.16 = (bf16[288,1280]{1,0:T(8,128)(2,1)S(1)}, bf16[288,1280]{1,0:T(8,128)(2,1)S(1)}, u32[]{:S(2)}, u32[]{:S(2)}) collective-permute-start(bf16[288,1280]{1,0:T(8,128)(2,1)S(1)} %collective-permute-done.15.refs_0_), channel_id=1, source_target_pairs={{0,16},{8,24},{16,0},{24,8},{1,17},{9,25},{17,1},{25,9},{2,18},{10... | collective-permute-start | bytes 2211848 | tf_op jit(solution)/shard_map/ppermute | solution.py:46
  90.6 33.1 %collective-permute-start.17 = (bf16[288,1280]{1,0:T(8,128)(2,1)S(1)}, bf16[288,1280]{1,0:T(8,128)(2,1)S(1)}, u32[]{:S(2)}, u32[]{:S(2)}) collective-permute-start(bf16[288,1280]{1,0:T(8,128)(2,1)S(1)} %collective-permute-done.15.refs_0_), channel_id=1, source_target_pairs={{0,8},{8,0},{16,24},{24,16},{1,9},{9,1},{17,25},{25,17},{2,10},{10... | collective-permute-start | bytes 2211848 | tf_op jit(solution)/shard_map/ppermute | solution.py:46
  92.1 33.1 %collective-permute-start.12 = (bf16[288,1280]{1,0:T(8,128)(2,1)S(1)}, bf16[288,1280]{1,0:T(8,128)(2,1)S(1)}, u32[]{:S(2)}, u32[]{:S(2)}) collective-permute-start(bf16[288,1280]{1,0:T(8,128)(2,1)S(1)} %collective-permute-done.11.refs_0_), channel_id=1, source_target_pairs={{0,8},{8,0},{16,24},{24,16},{1,9},{9,1},{17,25},{25,17},{2,10},{10... | collective-permute-start | bytes 2211848 | tf_op jit(solution)/shard_map/ppermute | solution.py:46
  109.7 29.9 %collective-permute-start.13 = (bf16[288,1280]{1,0:T(8,128)(2,1)S(1)}, bf16[288,1280]{1,0:T(8,128)(2,1)S(1)}, u32[]{:S(2)}, u32[]{:S(2)}) collective-permute-start(bf16[288,1280]{1,0:T(8,128)(2,1)S(1)} %collective-permute-done.11.refs_0_), channel_id=1, source_target_pairs={{0,16},{8,24},{16,0},{24,8},{1,17},{9,25},{17,1},{25,9},{2,18},{10... | collective-permute-start | bytes 2211848 | tf_op jit(solution)/shard_map/ppermute | solution.py:46
  111.2 43.1 %collective-permute-start.8 = (bf16[288,1280]{1,0:T(8,128)(2,1)S(1)}, bf16[288,1280]{1,0:T(8,128)(2,1)S(1)}, u32[]{:S(2)}, u32[]{:S(2)}) collective-permute-start(bf16[288,1280]{1,0:T(8,128)(2,1)S(1)} %collective-permute-done.7.refs_0_), channel_id=1, source_target_pairs={{0,16},{8,24},{16,0},{24,8},{1,17},{9,25},{17,1},{25,9},{2,18},{10... | collective-permute-start | bytes 2211848 | tf_op jit(solution)/shard_map/ppermute | solution.py:46
  123.7 48.8 %collective-permute-start.22 = (bf16[640,1536]{1,0:T(8,128)(2,1)S(1)}, bf16[640,1536]{1,0:T(8,128)(2,1)S(1)}, u32[]{:S(2)}, u32[]{:S(2)}) collective-permute-start(bf16[640,1536]{1,0:T(8,128)(2,1)S(1)} %copy-done.2), channel_id=1, source_target_pairs={{0,1},{1,0},{2,3},{3,2},{4,5},{5,4},{6,7},{7,6},{8,9},{9,8},{10,11... | collective-permute-start | bytes 5898248 | tf_op jit(solution)/shard_map/ppermute | solution.py:439
  123.7 31.3 %collective-permute-start.9 = (bf16[288,1280]{1,0:T(8,128)(2,1)S(1)}, bf16[288,1280]{1,0:T(8,128)(2,1)S(1)}, u32[]{:S(2)}, u32[]{:S(2)}) collective-permute-start(bf16[288,1280]{1,0:T(8,128)(2,1)S(1)} %collective-permute-done.7.refs_0_), channel_id=1, source_target_pairs={{0,8},{8,0},{16,24},{24,16},{1,9},{9,1},{17,25},{25,17},{2,10},{10... | collective-permute-start | bytes 2211848 | tf_op jit(solution)/shard_map/ppermute | solution.py:46
  125.2 41.5 %collective-permute-start.47 = (bf16[640,768]{1,0:T(8,128)(2,1)S(1)}, bf16[640,768]{1,0:T(8,128)(2,1)S(1)}, u32[]{:S(2)}, u32[]{:S(2)}) collective-permute-start(bf16[640,768]{1,0:T(8,128)(2,1)S(1)} %collective-permute-done.45.refs_4_), channel_id=1, source_target_pairs={{2,0},{3,1},{4,6},{5,7},{10,8},{11,9},{12,14},{13,15},{18,16},{19,... | collective-permute-start | bytes 2949128 | tf_op jit(solution)/shard_map/ppermute | solution.py:459
  139.5 28.5 %collective-permute-start.44 = (bf16[640,768]{1,0:T(8,128)(2,1)S(1)}, bf16[640,768]{1,0:T(8,128)(2,1)S(1)}, u32[]{:S(2)}, u32[]{:S(2)}) collective-permute-start(bf16[640,768]{1,0:T(8,128)(2,1)S(1)} %collective-permute-done.43.refs_2_), channel_id=1, source_target_pairs={{0,1},{1,0},{2,3},{3,2},{4,5},{5,4},{6,7},{7,6},{8,9},{9,8},{10,11... | collective-permute-start | bytes 2949128 | tf_op jit(solution)/shard_map/ppermute | solution.py:466
  154.3 15.4 %collective-permute-start.49 = (bf16[640,768]{1,0:T(8,128)(2,1)S(1)}, bf16[640,768]{1,0:T(8,128)(2,1)S(1)}, u32[]{:S(2)}, u32[]{:S(2)}) collective-permute-start(bf16[640,768]{1,0:T(8,128)(2,1)S(1)} %collective-permute-done.43.refs_2_), channel_id=1, source_target_pairs={{2,4},{3,5},{4,2},{5,3},{10,12},{11,13},{12,10},{13,11},{18,20},{1... | collective-permute-start | bytes 2949128 | tf_op jit(solution)/shard_map/ppermute | solution.py:459
  155.0 16.0 %collective-permute-start.46 = (bf16[640,768]{1,0:T(8,128)(2,1)S(1)}, bf16[640,768]{1,0:T(8,128)(2,1)S(1)}, u32[]{:S(2)}, u32[]{:S(2)}) collective-permute-start(bf16[640,768]{1,0:T(8,128)(2,1)S(1)} %collective-permute-done.45.refs_4_), channel_id=1, source_target_pairs={{2,3},{3,2},{4,5},{5,4},{10,11},{11,10},{12,13},{13,12},{18,19},{1... | collective-permute-start | bytes 2949128 | tf_op jit(solution)/shard_map/ppermute | solution.py:466
  166.8 31.8 %collective-permute-start.27 = (bf16[640,768]{1,0:T(8,128)(2,1)S(1)}, bf16[640,768]{1,0:T(8,128)(2,1)S(1)}, u32[]{:S(2)}, u32[]{:S(2)}) collective-permute-start(bf16[640,768]{1,0:T(8,128)(2,1)S(1)} %collective-permute-done.25.refs_4_), channel_id=1, source_target_pairs={{2,0},{3,1},{4,6},{5,7},{10,8},{11,9},{12,14},{13,15},{18,16},{19,... | collective-permute-start | bytes 2949128 | tf_op jit(solution)/shard_map/ppermute | solution.py:459
  168.1 32.5 %collective-permute-start.29 = (bf16[640,768]{1,0:T(8,128)(2,1)}, bf16[640,768]{1,0:T(8,128)(2,1)}, u32[]{:S(2)}, u32[]{:S(2)}) collective-permute-start(bf16[640,768]{1,0:T(8,128)(2,1)} %collective-permute-done.23.refs_2_), channel_id=1, source_target_pairs={{2,4},{3,5},{4,2},{5,3},{10,12},{11,13},{12,10},{13,11},{18,20},{1... | collective-permute-start | bytes 2949128 | tf_op jit(solution)/shard_map/ppermute | solution.py:459
  169.7 49.8 %collective-permute-start.51 = (bf16[640,768]{1,0:T(8,128)(2,1)S(1)}, bf16[640,768]{1,0:T(8,128)(2,1)S(1)}, u32[]{:S(2)}, u32[]{:S(2)}) collective-permute-start(bf16[640,768]{1,0:T(8,128)(2,1)S(1)} %collective-permute-done.49.refs_0_), channel_id=1, source_target_pairs={{2,0},{3,1},{4,6},{5,7},{10,8},{11,9},{12,14},{13,15},{18,16},{19,... | collective-permute-start | bytes 2949128 | tf_op jit(solution)/shard_map/ppermute | solution.py:459
  171.0 30.3 %collective-permute-start.18 = (bf16[288,1280]{1,0:T(8,128)(2,1)S(1)}, bf16[288,1280]{1,0:T(8,128)(2,1)S(1)}, u32[]{:S(2)}, u32[]{:S(2)}) collective-permute-start(bf16[288,1280]{1,0:T(8,128)(2,1)S(1)} %collective-permute-done.16.refs_1_), channel_id=1, source_target_pairs={{0,8},{8,0},{16,24},{24,16},{1,9},{9,1},{17,25},{25,17},{2,10},{10... | collective-permute-start | bytes 2211848 | tf_op jit(solution)/shard_map/ppermute | solution.py:46
  172.5 48.8 %collective-permute-start.14 = (bf16[288,1280]{1,0:T(8,128)(2,1)S(1)}, bf16[288,1280]{1,0:T(8,128)(2,1)S(1)}, u32[]{:S(2)}, u32[]{:S(2)}) collective-permute-start(bf16[288,1280]{1,0:T(8,128)(2,1)S(1)} %collective-permute-done.12.refs_1_), channel_id=1, source_target_pairs={{0,16},{8,24},{16,0},{24,8},{1,17},{9,25},{17,1},{25,9},{2,18},{10... | collective-permute-start | bytes 2211848 | tf_op jit(solution)/shard_map/ppermute | solution.py:46
  198.6 41.8 %collective-permute-start.48 = (bf16[640,768]{1,0:T(8,128)(2,1)S(1)}, bf16[640,768]{1,0:T(8,128)(2,1)S(1)}, u32[]{:S(2)}, u32[]{:S(2)}) collective-permute-start(bf16[640,768]{1,0:T(8,128)(2,1)S(1)} %collective-permute-done.47.refs_6_), channel_id=1, source_target_pairs={{0,1},{1,0},{6,7},{7,6},{8,9},{9,8},{14,15},{15,14},{16,17},{17,16... | collective-permute-start | bytes 2949128 | tf_op jit(solution)/shard_map/ppermute | solution.py:466
  200.5 41.4 %collective-permute-start.50 = (bf16[640,768]{1,0:T(8,128)(2,1)S(1)}, bf16[640,768]{1,0:T(8,128)(2,1)S(1)}, u32[]{:S(2)}, u32[]{:S(2)}) collective-permute-start(bf16[640,768]{1,0:T(8,128)(2,1)S(1)} %collective-permute-done.49.refs_0_), channel_id=1, source_target_pairs={{2,3},{3,2},{4,5},{5,4},{10,11},{11,10},{12,13},{13,12},{18,19},{1... | collective-permute-start | bytes 2949128 | tf_op jit(solution)/shard_map/ppermute | solution.py:466
  201.3 61.2 %collective-permute-start.31 = (bf16[640,768]{1,0:T(8,128)(2,1)}, bf16[640,768]{1,0:T(8,128)(2,1)}, u32[]{:S(2)}, u32[]{:S(2)}) collective-permute-start(bf16[640,768]{1,0:T(8,128)(2,1)} %collective-permute-done.29.refs_0_), channel_id=1, source_target_pairs={{2,0},{3,1},{4,6},{5,7},{10,8},{11,9},{12,14},{13,15},{18,16},{19,... | collective-permute-start | bytes 2949128 | tf_op jit(solution)/shard_map/ppermute | solution.py:459
  219.5 44.6 %collective-permute-start.52 = (bf16[640,768]{1,0:T(8,128)(2,1)S(1)}, bf16[640,768]{1,0:T(8,128)(2,1)S(1)}, u32[]{:S(2)}, u32[]{:S(2)}) collective-permute-start(bf16[640,768]{1,0:T(8,128)(2,1)S(1)} %collective-permute-done.51.refs_2_), channel_id=1, source_target_pairs={{0,1},{1,0},{6,7},{7,6},{8,9},{9,8},{14,15},{15,14},{16,17},{17,16... | collective-permute-start | bytes 2949128 | tf_op jit(solution)/shard_map/ppermute | solution.py:466
  221.4 19.0 %collective-permute-start.10 = (bf16[288,1280]{1,0:T(8,128)(2,1)S(1)}, bf16[288,1280]{1,0:T(8,128)(2,1)S(1)}, u32[]{:S(2)}, u32[]{:S(2)}) collective-permute-start(bf16[288,1280]{1,0:T(8,128)(2,1)S(1)} %collective-permute-done.8.refs_1_), channel_id=1, source_target_pairs={{0,8},{8,0},{16,24},{24,16},{1,9},{9,1},{17,25},{25,17},{2,10},{10... | collective-permute-start | bytes 2211848 | tf_op jit(solution)/shard_map/ppermute | solution.py:46
  240.4 50.9 %collective-permute-start.24 = (bf16[640,768]{1,0:T(8,128)(2,1)}, bf16[640,768]{1,0:T(8,128)(2,1)}, u32[]{:S(2)}, u32[]{:S(2)}) collective-permute-start(bf16[640,768]{1,0:T(8,128)(2,1)} %collective-permute-done.23.refs_2_), channel_id=1, source_target_pairs={{0,1},{1,0},{2,3},{3,2},{4,5},{5,4},{6,7},{7,6},{8,9},{9,8},{10,11... | collective-permute-start | bytes 2949128 | tf_op jit(solution)/shard_map/ppermute | solution.py:466
  240.4 51.1 %collective-permute-start.26 = (bf16[640,768]{1,0:T(8,128)(2,1)S(1)}, bf16[640,768]{1,0:T(8,128)(2,1)}, u32[]{:S(2)}, u32[]{:S(2)}) collective-permute-start(bf16[640,768]{1,0:T(8,128)(2,1)S(1)} %collective-permute-done.25.refs_4_), channel_id=1, source_target_pairs={{2,3},{3,2},{4,5},{5,4},{10,11},{11,10},{12,13},{13,12},{18,19},{1... | collective-permute-start | bytes 2949128 | tf_op jit(solution)/shard_map/ppermute | solution.py:466
  242.0 49.8 %collective-permute-start.28 = (bf16[640,768]{1,0:T(8,128)(2,1)S(1)}, bf16[640,768]{1,0:T(8,128)(2,1)}, u32[]{:S(2)}, u32[]{:S(2)}) collective-permute-start(bf16[640,768]{1,0:T(8,128)(2,1)S(1)} %collective-permute-done.27.refs_6_), channel_id=1, source_target_pairs={{0,1},{1,0},{6,7},{7,6},{8,9},{9,8},{14,15},{15,14},{16,17},{17,16... | collective-permute-start | bytes 2949128 | tf_op jit(solution)/shard_map/ppermute | solution.py:466
  262.4 40.8 %collective-permute-start.30 = (bf16[640,768]{1,0:T(8,128)(2,1)}, bf16[640,768]{1,0:T(8,128)(2,1)}, u32[]{:S(2)}, u32[]{:S(2)}) collective-permute-start(bf16[640,768]{1,0:T(8,128)(2,1)} %collective-permute-done.29.refs_0_), channel_id=1, source_target_pairs={{2,3},{3,2},{4,5},{5,4},{10,11},{11,10},{12,13},{13,12},{18,19},{1... | collective-permute-start | bytes 2949128 | tf_op jit(solution)/shard_map/ppermute | solution.py:466
  265.1 38.2 %collective-permute-start.32 = (bf16[640,768]{1,0:T(8,128)(2,1)}, bf16[640,768]{1,0:T(8,128)(2,1)}, u32[]{:S(2)}, u32[]{:S(2)}) collective-permute-start(bf16[640,768]{1,0:T(8,128)(2,1)} %collective-permute-done.31.refs_2_), channel_id=1, source_target_pairs={{0,1},{1,0},{6,7},{7,6},{8,9},{9,8},{14,15},{15,14},{16,17},{17,16... | collective-permute-start | bytes 2949128 | tf_op jit(solution)/shard_map/ppermute | solution.py:466
  291.2 19.1 %collective-permute-start.3 = (bf16[256,1280]{1,0:T(8,128)(2,1)}, bf16[256,1280]{1,0:T(8,128)(2,1)S(1)}, u32[]{:S(2)}, u32[]{:S(2)}) collective-permute-start(bf16[256,1280]{1,0:T(8,128)(2,1)} %collective-permute-done.1.refs_2_), channel_id=1, source_target_pairs={{0,2},{1,3},{2,4},{3,5},{4,6},{5,7},{6,0},{7,1},{8,10},{9,11},{10,... | collective-permute-start | bytes 1966088 | tf_op jit(solution)/shard_map/ppermute | solution.py:435
  291.5 36.9 %collective-permute-start.53 = (bf16[1152,512]{1,0:T(8,128)(2,1)}, bf16[1152,512]{1,0:T(8,128)(2,1)S(1)}, u32[]{:S(2)}, u32[]{:S(2)}) collective-permute-start(bf16[1152,512]{1,0:T(8,128)(2,1)} %get-tuple-element.24.refs_0_), channel_id=1, source_target_pairs={{0,1},{1,0},{2,3},{3,2},{4,5},{5,4},{6,7},{7,6},{8,9},{9,8},{10,11... | collective-permute-start | bytes 3538952 | tf_op jit(solution)/shard_map/ppermute | solution.py:481
  308.0 30.4 %collective-permute-start.33 = (bf16[1152,512]{1,0:T(8,128)(2,1)S(1)}, bf16[1152,512]{1,0:T(8,128)(2,1)S(1)}, u32[]{:S(2)}, u32[]{:S(2)}) collective-permute-start(bf16[1152,512]{1,0:T(8,128)(2,1)S(1)} %get-tuple-element.18.refs_0_), channel_id=1, source_target_pairs={{0,1},{1,0},{2,3},{3,2},{4,5},{5,4},{6,7},{7,6},{8,9},{9,8},{10,11... | collective-permute-start | bytes 3538952 | tf_op jit(solution)/shard_map/ppermute | solution.py:481
  310.4 18.1 %collective-permute-start.5 = (bf16[256,1280]{1,0:T(8,128)(2,1)S(1)}, bf16[256,1280]{1,0:T(8,128)(2,1)S(1)}, u32[]{:S(2)}, u32[]{:S(2)}) collective-permute-start(bf16[256,1280]{1,0:T(8,128)(2,1)S(1)} %collective-permute-done.3.refs_4_), channel_id=1, source_target_pairs={{0,2},{1,3},{2,4},{3,5},{4,6},{5,7},{6,0},{7,1},{8,10},{9,11},{10,... | collective-permute-start | bytes 1966088 | tf_op jit(solution)/shard_map/ppermute | solution.py:435
  310.4 31.6 %collective-permute-start = (bf16[256,1280]{1,0:T(8,128)(2,1)S(1)}, bf16[256,1280]{1,0:T(8,128)(2,1)S(1)}, u32[]{:S(2)}, u32[]{:S(2)}) collective-permute-start(bf16[256,1280]{1,0:T(8,128)(2,1)S(1)} %copy-done.15), channel_id=1, source_target_pairs={{0,1},{1,0},{2,3},{3,2},{4,5},{5,4},{6,7},{7,6},{8,9},{9,8},{10,11... | collective-permute-start | bytes 1966088 | tf_op jit(solution)/shard_map/ppermute | solution.py:439
  310.4 33.2 %collective-permute-start.2 = (bf16[256,1280]{1,0:T(8,128)(2,1)}, bf16[256,1280]{1,0:T(8,128)(2,1)S(1)}, u32[]{:S(2)}, u32[]{:S(2)}) collective-permute-start(bf16[256,1280]{1,0:T(8,128)(2,1)} %collective-permute-done.1.refs_2_), channel_id=1, source_target_pairs={{0,1},{1,0},{2,3},{3,2},{4,5},{5,4},{6,7},{7,6},{8,9},{9,8},{10,11... | collective-permute-start | bytes 1966088 | tf_op jit(solution)/shard_map/ppermute | solution.py:439
  328.4 21.7 %collective-permute-start.4 = (bf16[256,1280]{1,0:T(8,128)(2,1)S(1)}, bf16[256,1280]{1,0:T(8,128)(2,1)S(1)}, u32[]{:S(2)}, u32[]{:S(2)}) collective-permute-start(bf16[256,1280]{1,0:T(8,128)(2,1)S(1)} %collective-permute-done.3.refs_4_), channel_id=1, source_target_pairs={{0,1},{1,0},{2,3},{3,2},{4,5},{5,4},{6,7},{7,6},{8,9},{9,8},{10,11... | collective-permute-start | bytes 1966088 | tf_op jit(solution)/shard_map/ppermute | solution.py:439
  328.4 26.4 %collective-permute-start.6 = (bf16[256,1280]{1,0:T(8,128)(2,1)S(1)}, bf16[256,1280]{1,0:T(8,128)(2,1)S(1)}, u32[]{:S(2)}, u32[]{:S(2)}) collective-permute-start(bf16[256,1280]{1,0:T(8,128)(2,1)S(1)} %collective-permute-done.5.refs_6_), channel_id=1, source_target_pairs={{0,1},{1,0},{2,3},{3,2},{4,5},{5,4},{6,7},{7,6},{8,9},{9,8},{10,11... | collective-permute-start | bytes 1966088 | tf_op jit(solution)/shard_map/ppermute | solution.py:439
  338.4 16.5 %collective-permute-start.62 = (bf16[288,256]{1,0:T(8,128)(2,1)S(1)}, bf16[288,256]{1,0:T(8,128)(2,1)S(1)}, u32[]{:S(2)}, u32[]{:S(2)}) collective-permute-start(bf16[288,256]{1,0:T(8,128)(2,1)S(1)} %get-tuple-element.27), channel_id=1, source_target_pairs={{0,4},{1,5},{2,6},{3,7},{4,0},{5,1},{6,2},{7,3},{8,12},{9,13},{10,... | collective-permute-start | bytes 442376 | tf_op jit(solution)/shard_map/ppermute | solution.py:435
  341.9 15.0 %collective-permute-start.66 = (bf16[288,256]{1,0:T(8,128)(2,1)S(1)}, bf16[288,256]{1,0:T(8,128)(2,1)S(1)}, u32[]{:S(2)}, u32[]{:S(2)}) collective-permute-start(bf16[288,256]{1,0:T(8,128)(2,1)S(1)} %get-tuple-element.28.refs_28_), channel_id=1, source_target_pairs={{0,16},{8,24},{16,0},{24,8},{1,17},{9,25},{17,1},{25,9},{2,18},{10... | collective-permute-start | bytes 442376 | tf_op jit(solution)/shard_map/ppermute | solution.py:46
  343.5 9.5 %collective-permute-start.39 = (bf16[288,256]{1,0:T(8,128)(2,1)S(1)}, bf16[288,256]{1,0:T(8,128)(2,1)S(1)}, u32[]{:S(2)}, u32[]{:S(2)}) collective-permute-start(bf16[288,256]{1,0:T(8,128)(2,1)S(1)} %get-tuple-element.21), channel_id=1, source_target_pairs={{0,4},{1,5},{2,6},{3,7},{4,0},{5,1},{6,2},{7,3},{8,12},{9,13},{10,... | collective-permute-start | bytes 442376 | tf_op jit(solution)/shard_map/ppermute | solution.py:435
  354.8 13.4 %collective-permute-start.54 = (bf16[288,256]{1,0:T(8,128)(2,1)S(1)}, bf16[288,256]{1,0:T(8,128)(2,1)S(1)}, u32[]{:S(2)}, u32[]{:S(2)}) collective-permute-start(bf16[288,256]{1,0:T(8,128)(2,1)S(1)} %get-tuple-element.25), channel_id=1, source_target_pairs={{0,6},{1,7},{2,0},{3,1},{4,2},{5,3},{6,4},{7,5},{8,14},{9,15},{10,... | collective-permute-start | bytes 442376 | tf_op jit(solution)/shard_map/ppermute | solution.py:435
  354.9 14.8 %collective-permute-start.58 = (bf16[288,256]{1,0:T(8,128)(2,1)S(1)}, bf16[288,256]{1,0:T(8,128)(2,1)S(1)}, u32[]{:S(2)}, u32[]{:S(2)}) collective-permute-start(bf16[288,256]{1,0:T(8,128)(2,1)S(1)} %get-tuple-element.26), channel_id=1, source_target_pairs={{0,2},{1,3},{2,4},{3,5},{4,6},{5,7},{6,0},{7,1},{8,10},{9,11},{10,... | collective-permute-start | bytes 442376 | tf_op jit(solution)/shard_map/ppermute | solution.py:435
  356.9 13.4 %collective-permute-start.35 = (bf16[288,256]{1,0:T(8,128)(2,1)S(1)}, bf16[288,256]{1,0:T(8,128)(2,1)S(1)}, u32[]{:S(2)}, u32[]{:S(2)}) collective-permute-start(bf16[288,256]{1,0:T(8,128)(2,1)S(1)} %get-tuple-element.20), channel_id=1, source_target_pairs={{0,2},{1,3},{2,4},{3,5},{4,6},{5,7},{6,0},{7,1},{8,10},{9,11},{10,... | collective-permute-start | bytes 442376 | tf_op jit(solution)/shard_map/ppermute | solution.py:435
  357.2 14.2 %collective-permute-start.63 = (bf16[288,256]{1,0:T(8,128)(2,1)S(1)}, bf16[288,256]{1,0:T(8,128)(2,1)S(1)}, u32[]{:S(2)}, u32[]{:S(2)}) collective-permute-start(bf16[288,256]{1,0:T(8,128)(2,1)S(1)} %collective-permute-done.62.refs_24_), channel_id=1, source_target_pairs={{0,8},{8,0},{16,24},{24,16},{1,9},{9,1},{17,25},{25,17},{2,10},{10... | collective-permute-start | bytes 442376 | tf_op jit(solution)/shard_map/ppermute | solution.py:46
  359.9 12.6 %collective-permute-start.64 = (bf16[288,256]{1,0:T(8,128)(2,1)S(1)}, bf16[288,256]{1,0:T(8,128)(2,1)S(1)}, u32[]{:S(2)}, u32[]{:S(2)}) collective-permute-start(bf16[288,256]{1,0:T(8,128)(2,1)S(1)} %collective-permute-done.62.refs_24_), channel_id=1, source_target_pairs={{0,16},{8,24},{16,0},{24,8},{1,17},{9,25},{17,1},{25,9},{2,18},{10... | collective-permute-start | bytes 442376 | tf_op jit(solution)/shard_map/ppermute | solution.py:46
  369.8 8.4 %collective-permute-start.55 = (bf16[288,256]{1,0:T(8,128)(2,1)S(1)}, bf16[288,256]{1,0:T(8,128)(2,1)S(1)}, u32[]{:S(2)}, u32[]{:S(2)}) collective-permute-start(bf16[288,256]{1,0:T(8,128)(2,1)S(1)} %collective-permute-done.54.refs_16_), channel_id=1, source_target_pairs={{0,8},{8,0},{16,24},{24,16},{1,9},{9,1},{17,25},{25,17},{2,10},{10... | collective-permute-start | bytes 442376 | tf_op jit(solution)/shard_map/ppermute | solution.py:46
  370.3 9.3 %collective-permute-start.59 = (bf16[288,256]{1,0:T(8,128)(2,1)S(1)}, bf16[288,256]{1,0:T(8,128)(2,1)S(1)}, u32[]{:S(2)}, u32[]{:S(2)}) collective-permute-start(bf16[288,256]{1,0:T(8,128)(2,1)S(1)} %collective-permute-done.58.refs_20_), channel_id=1, source_target_pairs={{0,16},{8,24},{16,0},{24,8},{1,17},{9,25},{17,1},{25,9},{2,18},{10... | collective-permute-start | bytes 442376 | tf_op jit(solution)/shard_map/ppermute | solution.py:46
  371.4 17.8 %collective-permute-start.40 = (bf16[576,256]{1,0:T(8,128)(2,1)S(1)}, bf16[576,256]{1,0:T(8,128)(2,1)S(1)}, u32[]{:S(2)}, u32[]{:S(2)}) collective-permute-start(bf16[576,256]{1,0:T(8,128)(2,1)S(1)} %constant_dynamic-update-slice_fusion.2.refs_12_), channel_id=1, source_target_pairs={{0,16},{8,24},{16,0},{24,8},{1,17},{9,25},{17,1},{25,9},{2,18},{10... | collective-permute-start | bytes 884744 | tf_op jit(solution)/shard_map/ppermute | solution.py:46
  372.4 18.2 %collective-permute-start.36 = (bf16[576,256]{1,0:T(8,128)(2,1)S(1)}, bf16[576,256]{1,0:T(8,128)(2,1)S(1)}, u32[]{:S(2)}, u32[]{:S(2)}) collective-permute-start(bf16[576,256]{1,0:T(8,128)(2,1)S(1)} %constant_dynamic-update-slice_fusion.refs_8_), channel_id=1, source_target_pairs={{0,8},{8,0},{16,24},{24,16},{1,9},{9,1},{17,25},{25,17},{2,10},{10... | collective-permute-start | bytes 884744 | tf_op jit(solution)/shard_map/ppermute | solution.py:46
  375.0 9.7 %collective-permute-start.56 = (bf16[288,256]{1,0:T(8,128)(2,1)S(1)}, bf16[288,256]{1,0:T(8,128)(2,1)S(1)}, u32[]{:S(2)}, u32[]{:S(2)}) collective-permute-start(bf16[288,256]{1,0:T(8,128)(2,1)S(1)} %collective-permute-done.54.refs_16_), channel_id=1, source_target_pairs={{0,16},{8,24},{16,0},{24,8},{1,17},{9,25},{17,1},{25,9},{2,18},{10... | collective-permute-start | bytes 442376 | tf_op jit(solution)/shard_map/ppermute | solution.py:46
  378.1 8.8 %collective-permute-start.60 = (bf16[288,256]{1,0:T(8,128)(2,1)S(1)}, bf16[288,256]{1,0:T(8,128)(2,1)S(1)}, u32[]{:S(2)}, u32[]{:S(2)}) collective-permute-start(bf16[288,256]{1,0:T(8,128)(2,1)S(1)} %collective-permute-done.58.refs_20_), channel_id=1, source_target_pairs={{0,8},{8,0},{16,24},{24,16},{1,9},{9,1},{17,25},{25,17},{2,10},{10... | collective-permute-start | bytes 442376 | tf_op jit(solution)/shard_map/ppermute | solution.py:46
  379.6 8.4 %collective-permute-start.65 = (bf16[288,256]{1,0:T(8,128)(2,1)S(1)}, bf16[288,256]{1,0:T(8,128)(2,1)S(1)}, u32[]{:S(2)}, u32[]{:S(2)}) collective-permute-start(bf16[288,256]{1,0:T(8,128)(2,1)S(1)} %collective-permute-done.63.refs_25_), channel_id=1, source_target_pairs={{0,16},{8,24},{16,0},{24,8},{1,17},{9,25},{17,1},{25,9},{2,18},{10... | collective-permute-start | bytes 442376 | tf_op jit(solution)/shard_map/ppermute | solution.py:46
  384.7 14.1 %collective-permute-start.41 = (bf16[576,256]{1,0:T(8,128)(2,1)S(1)}, bf16[576,256]{1,0:T(8,128)(2,1)S(1)}, u32[]{:S(2)}, u32[]{:S(2)}) collective-permute-start(bf16[576,256]{1,0:T(8,128)(2,1)S(1)} %constant_dynamic-update-slice_fusion.2.refs_12_), channel_id=1, source_target_pairs={{0,8},{8,0},{16,24},{24,16},{1,9},{9,1},{17,25},{25,17},{2,10},{10... | collective-permute-start | bytes 884744 | tf_op jit(solution)/shard_map/ppermute | solution.py:46
  388.0 10.8 %collective-permute-start.37 = (bf16[576,256]{1,0:T(8,128)(2,1)S(1)}, bf16[576,256]{1,0:T(8,128)(2,1)S(1)}, u32[]{:S(2)}, u32[]{:S(2)}) collective-permute-start(bf16[576,256]{1,0:T(8,128)(2,1)S(1)} %constant_dynamic-update-slice_fusion.refs_8_), channel_id=1, source_target_pairs={{0,16},{8,24},{16,0},{24,8},{1,17},{9,25},{17,1},{25,9},{2,18},{10... | collective-permute-start | bytes 884744 | tf_op jit(solution)/shard_map/ppermute | solution.py:46
  389.2 9.6 %collective-permute-start.42 = (bf16[576,256]{1,0:T(8,128)(2,1)S(1)}, bf16[576,256]{1,0:T(8,128)(2,1)S(1)}, u32[]{:S(2)}, u32[]{:S(2)}) collective-permute-start(bf16[576,256]{1,0:T(8,128)(2,1)S(1)} %collective-permute-done.40.refs_13_), channel_id=1, source_target_pairs={{0,8},{8,0},{16,24},{24,16},{1,9},{9,1},{17,25},{25,17},{2,10},{10... | collective-permute-start | bytes 884744 | tf_op jit(solution)/shard_map/ppermute | solution.py:46
  390.7 9.6 %collective-permute-start.38 = (bf16[576,256]{1,0:T(8,128)(2,1)S(1)}, bf16[576,256]{1,0:T(8,128)(2,1)S(1)}, u32[]{:S(2)}, u32[]{:S(2)}) collective-permute-start(bf16[576,256]{1,0:T(8,128)(2,1)S(1)} %collective-permute-done.36.refs_9_), channel_id=1, source_target_pairs={{0,16},{8,24},{16,0},{24,8},{1,17},{9,25},{17,1},{25,9},{2,18},{10... | collective-permute-start | bytes 884744 | tf_op jit(solution)/shard_map/ppermute | solution.py:46
  (26 other events, 851.0 us)

commit v2 on v1

--- a/solution.py
+++ b/solution.py
@@ -315,28 +315,36 @@
     )(query, *pairs)
 
 
-def out_kernel(parts, turns, tags, w_tags, base_ref, *refs):
+def out_kernel(parts, turns, tags, w_tags, last, base_ref, *refs):
     w_refs, refs = refs[: len(w_tags)], refs[len(w_tags) :]
     o_refs = refs[: len(tags)]
-    out_ref, o_v, w_v, b_v, r_v, o_sem, w_sem, b_sem, r_sem = refs[len(tags) :]
+    outs = refs[len(tags) : len(tags) + (1 if last else 2)]
+    o_v, w_v, b_v, r_v, o_sem, w_sem, b_sem, r_sem, k_sem = refs[len(tags) + len(outs) :]
     me, col = lax.axis_index("row"), lax.axis_index("col")
     images, rows, columns = base_ref.shape
     image, part = col // parts, col % parts
     half = images // 2
+    deep = w_v.shape[0]
     spots = [(image + k) % images for k in turns]
     cuts = column_cuts(columns)
-    heads = [[], []]
+    heads = []
     for n, (chunk, mask, block) in enumerate(tags):
+        if last:
+            heads.append(pltpu.make_async_copy(o_refs[n], o_v, o_sem.at[n]))
+            continue
         size, width = o_refs[n].shape
-        at = pl.multiple_of(((me ^ mask) * CHUNKS + chunk) * width, 128)
+        per = parts * w_refs[0].shape[0] // (CHUNKS * width)
+        other = me ^ mask
+        slot = (image + images - other // per) % images
+        at = pl.multiple_of(((slot * per + other % per) * CHUNKS + chunk) * width, 128)
         to = o_v.at[pl.ds(block * rows, size), pl.ds(at, width)]
-        heads[block // half].append(pltpu.make_async_copy(o_refs[n], to, o_sem.at[n]))
+        heads.append(pltpu.make_async_copy(o_refs[n], to, o_sem.at[n]))
     weights = []
     for m, (begin, size) in enumerate(cuts):
         for n, (step, turn) in enumerate(w_tags):
             depth = w_refs[n].shape[0]
-            place = ((image + images - step) % images) * parts + (part + parts - turn) % parts
-            at = pl.multiple_of(place * depth, 16)
+            first = 0 if last else step * parts * depth
+            at = pl.multiple_of(first + (part + parts - turn) % parts * depth, 16)
             span = pl.ds(begin, size)
             weights.append(
                 pltpu.make_async_copy(
@@ -344,20 +352,25 @@
                 )
             )
     bases = [
-        pltpu.make_async_copy(base_ref.at[spot], b_v.at[n], b_sem.at[n])
+        pltpu.make_async_copy(base_ref.at[n if last else spot], b_v.at[n], b_sem.at[n])
         for n, spot in enumerate(spots)
     ]
     per = len(w_tags)
-    for copy in heads[0] + weights[:per] + heads[1] + bases + weights[per:]:
+    for copy in heads + weights[:per] + bases + weights[per:]:
         copy.start()
-    for copy in heads[0] + heads[1]:
+    for copy in heads:
         copy.wait()
+    keep = None
+    if not last:
+        keep = pltpu.make_async_copy(
+            o_v.at[:, pl.ds(deep, o_v.shape[1] - deep)], outs[1], k_sem.at[0]
+        )
+        keep.start()
 
     def store(m, n, spot):
         span = pl.ds(*cuts[m])
-        return pltpu.make_async_copy(
-            r_v.at[n, :, span], out_ref.at[spot, :, span], r_sem.at[m, n]
-        )
+        to = spot if last else n
+        return pltpu.make_async_copy(r_v.at[n, :, span], outs[0].at[to, :, span], r_sem.at[m, n])
 
     for m, (begin, size) in enumerate(cuts):
         for copy in weights[m * per : (m + 1) * per]:
@@ -369,7 +382,7 @@
         def body(block, carry, m=m, begin=begin, size=size):
             at = pl.ds(pl.multiple_of(block * half * rows, 16), half * rows)
             got = jnp.dot(
-                o_v[at, :], w_v[:, begin : begin + size], preferred_element_type=jnp.float32
+                o_v[at, :deep], w_v[:, begin : begin + size], preferred_element_type=jnp.float32
             )
             for k in range(half):
                 n = block * half + k
@@ -384,6 +397,8 @@
     for m in range(len(cuts)):
         for n, spot in enumerate(spots):
             store(m, n, spot).wait()
+    if keep is not None:
+        keep.wait()
 
 
 def column_cuts(columns):
@@ -391,31 +406,38 @@
     return ((0, first), (first, columns - first))
 
 
-def project_out(base, w_pieces, pieces, parts, row_count, turns):
+def project_out(base, w_pieces, pieces, parts, turns, last):
     tags = [(chunk, m, block) for chunk, m, block, _ in pieces]
     w_tags = [(s, t) for s, t, _ in w_pieces]
     images, rows, columns = base.shape
-    width = pieces[0][3].shape[1]
-    deep = len(w_pieces) * w_pieces[0][2].shape[0]
+    depth = w_pieces[0][2].shape[0]
+    deep = len(w_pieces) * depth
+    wide = deep if last else deep + parts * depth
     cuts = len(column_cuts(columns))
+    kind = jnp.bfloat16 if last else jnp.float32
+    tokens = images * rows
+    shapes = [jax.ShapeDtypeStruct(base.shape, kind)]
+    if not last:
+        shapes.append(jax.ShapeDtypeStruct((tokens, wide - deep), jnp.bfloat16))
     return pl.pallas_call(
-        functools.partial(out_kernel, parts, turns, tags, w_tags),
+        functools.partial(out_kernel, parts, turns, tags, w_tags, last),
         in_specs=[ANY] * (1 + len(w_tags) + len(tags)),
-        out_specs=ANY,
-        out_shape=jax.ShapeDtypeStruct(base.shape, jnp.bfloat16),
+        out_specs=[ANY] * len(shapes),
+        out_shape=shapes,
         scratch_shapes=[
-            pltpu.VMEM((images * rows, row_count * CHUNKS * width), jnp.bfloat16),
+            pltpu.VMEM((tokens, wide), jnp.bfloat16),
             pltpu.VMEM((deep, columns), jnp.bfloat16),
             pltpu.VMEM(base.shape, base.dtype),
-            pltpu.VMEM(base.shape, jnp.bfloat16),
+            pltpu.VMEM(base.shape, kind),
             pltpu.SemaphoreType.DMA((len(tags),)),
             pltpu.SemaphoreType.DMA((cuts, len(w_tags))),
             pltpu.SemaphoreType.DMA((images,)),
             pltpu.SemaphoreType.DMA((cuts, images)),
+            pltpu.SemaphoreType.DMA((1,)),
         ],
-        cost_estimate=cost(2 * images * rows * columns * deep, 8 * images * rows * columns),
+        cost_estimate=cost(2 * tokens * columns * deep, 8 * tokens * columns),
         name="out",
-        compiler_params=pltpu.CompilerParams(vmem_limit_bytes=30 << 20),
+        compiler_params=pltpu.CompilerParams(vmem_limit_bytes=28 << 20),
     )(base, *[w for _, _, w in w_pieces], *[o for _, _, _, o in pieces])
 
 
@@ -508,7 +530,10 @@
     pieces = [
         (j, m, n, o) for j in range(CHUNKS) for n, got in results[j] for m, o in got
     ]
-    return project_out(pixels_tokens, out_pieces, pieces, parts, row_count, shifts)
+    split = len(out_pieces) - parts
+    total, rest = project_out(pixels_tokens, out_pieces[:split], pieces, parts, shifts, False)
+    pieces = [(0, 0, 0, rest)]
+    return project_out(total, out_pieces[split:], pieces, parts, shifts, True)[0]
 
 
 def SLOTS(images):

time: 411 us -> 412 us (level)
    ppermute x12, waiting for transfers between devices: 100 us -> 83.2 us  [around(): return lax.ppermute(value, 'col', ring(images, parts, step))]
    ppermute x30, waiting for transfers between devices: 73.8 us -> 88.7 us  [spread(): pieces.append((m ^ d, lax.ppermute(b, 'row', perm)))]
    ppermute x30, starting transfers between devices: 37.6 us -> 33.1 us  [spread(): pieces.append((m ^ d, lax.ppermute(b, 'row', perm)))]
    pallas_call x1 -> x2, Pallas kernels: 10.3 us -> 13.4 us  [project_out(): pl.pallas_call(functools.partial(out_kernel, parts, turns, tags, w_tags,...]
    unnamed x44 -> x42, local copies, waits for them, and re-layouts: 11.2 us -> 11.1 us
  transfers between devices with their start and end apart: 69 -> 69, of which waited for: 25 -> 26; matrix products, arithmetic and copies ran while one was open for 1% -> 0% of each run, Pallas kernels for 16% -> 18%
where the time goes in v2:
time: 412 us
  waiting for transfers between devices  243 us (59%)
  Pallas kernels  78.1 us (19%)
  starting transfers between devices  76.1 us (18%)
  local copies, waits for them, and re-layouts  13.4 us (3%)
    ppermute x30, waiting for transfers between devices, spread(): pieces.append((m ^ d, lax.ppermute(b, 'row', perm)))  88.7 us
    ppermute x12, waiting for transfers between devices, around(): return lax.ppermute(value, 'col', ring(images, parts, step))  83.2 us
    ppermute x10, waiting for transfers between devices, arrive(): got = lax.ppermute(value, 'col', hop(parts, moves))  71.4 us
    ppermute x30, starting transfers between devices, spread(): pieces.append((m ^ d, lax.ppermute(b, 'row', perm)))  33.1 us
    pallas_call x2, Pallas kernels, project_early(): pl.pallas_call(functools.partial(early_kernel, steps, parts, tags, first)...  23.4 us
    ppermute x12, starting transfers between devices, around(): return lax.ppermute(value, 'col', ring(images, parts, step))  17.9 us
    pallas_call x4, Pallas kernels, attend(): pl.pallas_call(functools.partial(attend_kernel, first, slots, heads), in_...  16.5 us
    pallas_call x4, Pallas kernels, normalize(): pl.pallas_call(functools.partial(norm_kernel, masks, parts), grid=(rows /...  13.7 us
  transfers between devices with their start and end apart: 69, of which 26 were waited for; matrix products, arithmetic and copies ran while one was open for 0% of the time, Pallas kernels for 18%

profile of v2, /device:TPU:0, one launch (start us, length us, event | category | flops | bytes accessed | tf_op | source)
XLA Modules:
  0.0 411.6 jit_solution(1235495126806543150)
XLA Ops:
  0.0 2.1 dynamic-slice_bitcast_fusion
  2.1 3.0 collective-permute-start.17
  5.2 1.5 collective-permute-start.18
  6.7 1.6 collective-permute-start.13
  8.3 2.6 collective-permute-start.9
  11.7 9.9 %collective-permute-done.17.refs_1_ = bf16[288,1280]{1,0:T(8,128)(2,1)S(1)} collective-permute-done((bf16[288,1280]{1,0:T(8,128)(2,1)S(1)}, bf16[288,1280]{1,0:T(8,128)(2,1)S(1)}, u32[]{:S(2)}, u32[]{:S(2)}) %collective-permute-start.17) | collective-permute-done | bytes 737312 | tf_op jit(solution)/shard_map/ppermute | solution.py:46
  21.7 1.8 collective-permute-start.41
  23.5 3.2 collective-permute-start.5
  28.7 29.3 %collective-permute-done.9.refs_0_ = bf16[288,1280]{1,0:T(8,128)(2,1)S(1)} collective-permute-done((bf16[288,1280]{1,0:T(8,128)(2,1)S(1)}, bf16[288,1280]{1,0:T(8,128)(2,1)S(1)}, u32[]{:S(2)}, u32[]{:S(2)}) %collective-permute-start.9) | collective-permute-done | bytes 737312 | tf_op jit(solution)/shard_map/ppermute | solution.py:457
  58.4 20.8 %collective-permute-done.5.refs_0_ = bf16[288,1280]{1,0:T(8,128)(2,1)S(1)} collective-permute-done((bf16[288,1280]{1,0:T(8,128)(2,1)S(1)}, bf16[288,1280]{1,0:T(8,128)(2,1)S(1)}, u32[]{:S(2)}, u32[]{:S(2)}) %collective-permute-start.5) | collective-permute-done | bytes 737312 | tf_op jit(solution)/shard_map/ppermute | solution.py:457
  83.2 16.8 %collective-permute-done.21.refs_2_ = bf16[640,768]{1,0:T(8,128)(2,1)} collective-permute-done((bf16[640,768]{1,0:T(8,128)(2,1)S(1)}, bf16[640,768]{1,0:T(8,128)(2,1)}, u32[]{:S(2)}, u32[]{:S(2)}) %collective-permute-start.21) | collective-permute-done | bytes 983072 | tf_op jit(solution)/shard_map/ppermute | solution.py:481
  100.6 1.5 collective-permute-start.6
  102.1 12.2 %collective-permute-done.14.refs_1_ = bf16[288,1280]{1,0:T(8,128)(2,1)S(1)} collective-permute-done((bf16[288,1280]{1,0:T(8,128)(2,1)S(1)}, bf16[288,1280]{1,0:T(8,128)(2,1)S(1)}, u32[]{:S(2)}, u32[]{:S(2)}) %collective-permute-start.14) | collective-permute-done | bytes 737312 | tf_op jit(solution)/shard_map/ppermute | solution.py:46
  115.5 1.3 collective-permute-start.45
  116.8 13.4 %collective-permute-done.11.refs_2_ = bf16[288,1280]{1,0:T(8,128)(2,1)S(1)} collective-permute-done((bf16[288,1280]{1,0:T(8,128)(2,1)S(1)}, bf16[288,1280]{1,0:T(8,128)(2,1)S(1)}, u32[]{:S(2)}, u32[]{:S(2)}) %collective-permute-start.11) | collective-permute-done | bytes 737312 | tf_op jit(solution)/shard_map/ppermute | solution.py:46
  130.1 14.4 %collective-permute-done.6.refs_1_ = bf16[288,1280]{1,0:T(8,128)(2,1)S(1)} collective-permute-done((bf16[288,1280]{1,0:T(8,128)(2,1)S(1)}, bf16[288,1280]{1,0:T(8,128)(2,1)S(1)}, u32[]{:S(2)}, u32[]{:S(2)}) %collective-permute-start.6) | collective-permute-done | bytes 737312 | tf_op jit(solution)/shard_map/ppermute | solution.py:46
  146.0 11.1 %collective-permute-done.45.refs_6_ = bf16[640,768]{1,0:T(8,128)(2,1)S(1)} collective-permute-done((bf16[640,768]{1,0:T(8,128)(2,1)S(1)}, bf16[640,768]{1,0:T(8,128)(2,1)S(1)}, u32[]{:S(2)}, u32[]{:S(2)}) %collective-permute-start.45) | collective-permute-done | bytes 983072 | tf_op jit(solution)/shard_map/ppermute | solution.py:481
  158.4 1.6 collective-permute-start.27
  160.0 1.3 collective-permute-start.49
  162.5 26.5 %collective-permute-done.25.refs_6_ = bf16[640,768]{1,0:T(8,128)(2,1)S(1)} collective-permute-done((bf16[640,768]{1,0:T(8,128)(2,1)S(1)}, bf16[640,768]{1,0:T(8,128)(2,1)S(1)}, u32[]{:S(2)}, u32[]{:S(2)}) %collective-permute-start.25) | collective-permute-done | bytes 983072 | tf_op jit(solution)/shard_map/ppermute | solution.py:481
  189.0 1.9 collective-permute-start.46
  191.6 1.3 collective-permute-start.29
  192.9 16.9 %collective-permute-done.49.refs_2_ = bf16[640,768]{1,0:T(8,128)(2,1)S(1)} collective-permute-done((bf16[640,768]{1,0:T(8,128)(2,1)S(1)}, bf16[640,768]{1,0:T(8,128)(2,1)S(1)}, u32[]{:S(2)}, u32[]{:S(2)}) %collective-permute-start.49) | collective-permute-done | bytes 983072 | tf_op jit(solution)/shard_map/ppermute | solution.py:481
  209.8 1.9 collective-permute-start.50
  212.4 18.4 %collective-permute-done.8.refs_3_ = bf16[288,1280]{1,0:T(8,128)(2,1)S(1)} collective-permute-done((bf16[288,1280]{1,0:T(8,128)(2,1)S(1)}, bf16[288,1280]{1,0:T(8,128)(2,1)S(1)}, u32[]{:S(2)}, u32[]{:S(2)}) %collective-permute-start.8) | collective-permute-done | bytes 737312 | tf_op jit(solution)/shard_map/ppermute | solution.py:46
  230.7 1.6 collective-permute-start.24
  232.3 2.4 collective-permute-start.26
  234.8 3.4 norm.4.refs_4_
  238.2 3.4 norm.5.refs_4_
  241.6 3.4 norm.6.refs_4_
  245.1 3.4 norm.7.x_ref
  248.5 4.3 %copy-done = bf16[4,4,288,1280]{3,2,1,0:T(8,128)(2,1)} copy-done((bf16[4,4,288,1280]{3,2,1,0:T(8,128)(2,1)}, bf16[4,4,288,1280]{3,2,1,0:T(8,128)(2,1)S(1)}, u32[]{:S(2)}) %copy-start) | copy-done | bytes 11796504
  252.8 1.6 collective-permute-start.28
  255.4 1.9 collective-permute-start.30
  257.4 12.0 %early.3.acc_ref = f32[4,288,768]{2,1,0:T(8,128)S(1)} custom-call(bf16[4,4,288,1280]{3,2,1,0:T(8,128)(2,1)} %copy-done, bf16[640,1536]{1,0:T(8,128)(2,1)S(1)} %copy-done.2, bf16[640,1536]{1,0:T(8,128)(2,1)S(1)} %collective-permute-done.20.refs_1_, bf16[640,768]{1,0:T(8,128)(2,1)S(1)} %collective-permute-done.41.refs_2_, ...), custom_call_target="tpu_custom_call" | custom-call | flops 6794772480 | bytes 8847360 | tf_op jit(solution)/shard_map/early/pallas_call | solution.py:179
  269.4 1.7 copy-done.4
  271.1 2.0 copy-done.5
  274.3 6.4 %late.3 = (bf16[1152,256]{1,0:T(8,128)(2,1)S(1)}, bf16[1152,512]{1,0:T(8,128)(2,1)}) custom-call(bf16[4,4,288,1280]{3,2,1,0:T(8,128)(2,1)S(1)} %copy-done.1, f32[4,288,768]{2,1,0:T(8,128)S(1)} %copy-done.5, bf16[640,768]{1,0:T(8,128)(2,1)S(1)} %collective-permute-done.47.refs_0_, bf16[640,768]{1,0:T(8,128)(2,1)S(1)} %collective-permute-done.48.refs_1_, ...), custom_call_target="tpu_custom_call" | custom-call | flops 2264924160 | bytes 7077888 | tf_op jit(solution)/shard_map/late/pallas_call | solution.py:248
  282.2 11.4 %early.2.acc_ref = f32[4,288,768]{2,1,0:T(8,128)S(1)} custom-call(bf16[4,4,288,1280]{3,2,1,0:T(8,128)(2,1)} %copy-done, bf16[640,1536]{1,0:T(8,128)(2,1)S(1)} %copy-done.3, bf16[640,1536]{1,0:T(8,128)(2,1)S(1)} %copy-done.7, bf16[640,768]{1,0:T(8,128)(2,1)} %collective-permute-done.21.refs_2_, bf16[640,768]{1,0:T(8,128)(2,1)} %collective-permute-done.22.refs_3_, ...), custom_call_target="tpu_custom_call" | custom-call | flops 6794772480 | bytes 8847360 | tf_op jit(solution)/shard_map/early/pallas_call | solution.py:179
  293.6 4.7 %late.2 = (bf16[1152,256]{1,0:T(8,128)(2,1)S(1)}, bf16[1152,512]{1,0:T(8,128)(2,1)S(1)}) custom-call(bf16[4,4,288,1280]{3,2,1,0:T(8,128)(2,1)S(1)} %bitcast.11, f32[4,288,768]{2,1,0:T(8,128)S(1)} %early.2.acc_ref, bf16[640,768]{1,0:T(8,128)(2,1)} %collective-permute-done.27.refs_0_, bf16[640,768]{1,0:T(8,128)(2,1)} %collective-permute-done.28.refs_1_, ...), custom_call_target="tpu_custom_call" | custom-call | flops 2264924160 | bytes 7077888 | tf_op jit(solution)/shard_map/late/pallas_call | solution.py:248
  298.6 2.1 collective-permute-done.1.refs_2_
  301.2 17.6 %collective-permute-done.3.refs_4_ = bf16[256,1280]{1,0:T(8,128)(2,1)S(1)} collective-permute-done((bf16[256,1280]{1,0:T(8,128)(2,1)S(1)}, bf16[256,1280]{1,0:T(8,128)(2,1)S(1)}, u32[]{:S(2)}, u32[]{:S(2)}) %collective-permute-start.3) | collective-permute-done | bytes 655392 | tf_op jit(solution)/shard_map/ppermute | solution.py:457
  318.8 4.7 %attend.7 = (bf16[288,256]{1,0:T(8,128)(2,1)S(1)}, bf16[288,256]{1,0:T(8,128)(2,1)S(1)}) custom-call(bf16[1152,256]{1,0:T(8,128)(2,1)S(1)} %copy-done.16, bf16[1152,512]{1,0:T(8,128)(2,1)} %get-tuple-element.26.refs_0_, bf16[1152,512]{1,0:T(8,128)(2,1)S(1)} %collective-permute-done.51.refs_1_), custom_call_target="tpu_custom_call" | custom-call | flops 2717908992 | bytes 3538944 | tf_op jit(solution)/shard_map/attend/pallas_call | solution.py:303
  323.5 4.7 %attend.6 = (bf16[288,256]{1,0:T(8,128)(2,1)S(1)}, bf16[288,256]{1,0:T(8,128)(2,1)S(1)}) custom-call(bf16[1152,256]{1,0:T(8,128)(2,1)S(1)} %copy-done.16, bf16[1152,512]{1,0:T(8,128)(2,1)} %get-tuple-element.26.refs_0_, bf16[1152,512]{1,0:T(8,128)(2,1)S(1)} %collective-permute-done.51.refs_1_), custom_call_target="tpu_custom_call" | custom-call | flops 2717908992 | bytes 3538944 | tf_op jit(solution)/shard_map/attend/pallas_call | solution.py:303
  328.8 3.4 attend.5
  333.6 2.2 collective-permute-start.37
  335.8 3.7 attend.4
  339.5 3.9 collective-permute-start.52
  343.3 7.2 %collective-permute-done.37 = bf16[288,256]{1,0:T(8,128)(2,1)S(1)} collective-permute-done((bf16[288,256]{1,0:T(8,128)(2,1)S(1)}, bf16[288,256]{1,0:T(8,128)(2,1)S(1)}, u32[]{:S(2)}, u32[]{:S(2)}) %collective-permute-start.37) | collective-permute-done | bytes 147488 | tf_op jit(solution)/shard_map/ppermute | solution.py:457
  350.5 3.3 collective-permute-start.32
  355.3 1.6 collective-permute-start.62
  359.3 3.1 collective-permute-done.56.refs_18_
  366.4 1.3 collective-permute-start.38
  367.7 1.5 collective-permute-start.34
  369.7 4.5 %collective-permute-done.57.refs_19_ = bf16[288,256]{1,0:T(8,128)(2,1)S(1)} collective-permute-done((bf16[288,256]{1,0:T(8,128)(2,1)S(1)}, bf16[288,256]{1,0:T(8,128)(2,1)S(1)}, u32[]{:S(2)}, u32[]{:S(2)}) %collective-permute-start.57) | collective-permute-done | bytes 147488 | tf_op jit(solution)/shard_map/ppermute | solution.py:46
  376.2 1.8 collective-permute-done.58.refs_20_
  378.0 1.5 collective-permute-start.59
  379.5 3.7 collective-permute-done.63.refs_25_
  386.0 1.5 collective-permute-start.40
  388.0 4.7 %collective-permute-done.39.refs_12_ = bf16[576,256]{1,0:T(8,128)(2,1)S(1)} collective-permute-done((bf16[576,256]{1,0:T(8,128)(2,1)S(1)}, bf16[576,256]{1,0:T(8,128)(2,1)S(1)}, u32[]{:S(2)}, u32[]{:S(2)}) %collective-permute-start.39) | collective-permute-done | bytes 294944 | tf_op jit(solution)/shard_map/ppermute | solution.py:46
  392.7 2.0 collective-permute-done.35.refs_8_
  395.8 2.2 collective-permute-done.36.refs_9_
  398.0 8.7 %out.2 = (f32[4,288,1280]{2,1,0:T(8,128)S(1)}, bf16[1152,512]{1,0:T(8,128)(2,1)S(1)}) custom-call(bf16[4,288,1280]{2,1,0:T(8,128)(2,1)S(1)} %copy-done.8, bf16[256,1280]{1,0:T(8,128)(2,1)} %refs_0_.5, bf16[256,1280]{1,0:T(8,128)(2,1)S(1)} %collective-permute-done.refs_1_, bf16[256,1280]{1,0:T(8,128)(2,1)S(1)} %collective-permute-done.1.refs_2_, ...), custom_call_target="tpu_custom_call" | custom-call | flops 4529848320 | bytes 11796480 | tf_op jit(solution)/shard_map/out/pallas_call | solution.py:422
  406.8 4.7 %out.3 = bf16[4,288,1280]{2,1,0:T(8,128)(2,1)} custom-call(f32[4,288,1280]{2,1,0:T(8,128)S(1)} %get-tuple-element.31.base_ref, bf16[256,1280]{1,0:T(8,128)(2,1)S(1)} %collective-permute-done.67.refs_0_, bf16[256,1280]{1,0:T(8,128)(2,1)S(1)} %collective-permute-done.68.refs_1_, bf16[1152,512]{1,0:T(8,128)(2,1)S(1)} %get-tuple-element.32.refs_2_), custom_call_target="tpu_custom_call" | custom-call | flops 1509949440 | bytes 11796480 | tf_op jit(solution)/shard_map/out/pallas_call | solution.py:422
  (135 shorter events, 35.5 us)
Async XLA Ops:
  2.1 19.5 %collective-permute-start.17 = (bf16[288,1280]{1,0:T(8,128)(2,1)S(1)}, bf16[288,1280]{1,0:T(8,128)(2,1)S(1)}, u32[]{:S(2)}, u32[]{:S(2)}) collective-permute-start(bf16[288,1280]{1,0:T(8,128)(2,1)S(1)} %get-tuple-element.33.refs_0_), channel_id=1, source_target_pairs={{0,8},{8,0},{16,24},{24,16},{1,9},{9,1},{17,25},{25,17},{2,10},{10... | collective-permute-start | bytes 2211848 | tf_op jit(solution)/shard_map/ppermute | solution.py:46
  5.2 18.3 %collective-permute-start.18 = (bf16[288,1280]{1,0:T(8,128)(2,1)S(1)}, bf16[288,1280]{1,0:T(8,128)(2,1)S(1)}, u32[]{:S(2)}, u32[]{:S(2)}) collective-permute-start(bf16[288,1280]{1,0:T(8,128)(2,1)S(1)} %get-tuple-element.33.refs_0_), channel_id=1, source_target_pairs={{0,16},{8,24},{16,0},{24,8},{1,17},{9,25},{17,1},{25,9},{2,18},{10... | collective-permute-start | bytes 2211848 | tf_op jit(solution)/shard_map/ppermute | solution.py:46
  6.7 21.3 %collective-permute-start.13 = (bf16[288,1280]{1,0:T(8,128)(2,1)S(1)}, bf16[288,1280]{1,0:T(8,128)(2,1)S(1)}, u32[]{:S(2)}, u32[]{:S(2)}) collective-permute-start(bf16[288,1280]{1,0:T(8,128)(2,1)S(1)} %get-tuple-element.34), channel_id=1, source_target_pairs={{0,2},{1,3},{2,4},{3,5},{4,6},{5,7},{6,0},{7,1},{8,10},{9,11},{10,... | collective-permute-start | bytes 2211848 | tf_op jit(solution)/shard_map/ppermute | solution.py:457
  8.3 49.7 %collective-permute-start.9 = (bf16[288,1280]{1,0:T(8,128)(2,1)S(1)}, bf16[288,1280]{1,0:T(8,128)(2,1)S(1)}, u32[]{:S(2)}, u32[]{:S(2)}) collective-permute-start(bf16[288,1280]{1,0:T(8,128)(2,1)S(1)} %get-tuple-element.35), channel_id=1, source_target_pairs={{0,4},{1,5},{2,6},{3,7},{4,0},{5,1},{6,2},{7,3},{8,12},{9,13},{10,... | collective-permute-start | bytes 2211848 | tf_op jit(solution)/shard_map/ppermute | solution.py:457
  11.0 69.3 %collective-permute-start.43 = (bf16[640,768]{1,0:T(8,128)(2,1)S(1)}, bf16[640,768]{1,0:T(8,128)(2,1)S(1)}, u32[]{:S(2)}, u32[]{:S(2)}) collective-permute-start(bf16[640,768]{1,0:T(8,128)(2,1)S(1)} %get-tuple-element.37), channel_id=1, source_target_pairs={{2,4},{3,5},{4,2},{5,3},{10,12},{11,13},{12,10},{13,11},{18,20},{1... | collective-permute-start | bytes 2949128 | tf_op jit(solution)/shard_map/ppermute | solution.py:481
  21.7 59.5 %collective-permute-start.41 = (bf16[640,768]{1,0:T(8,128)(2,1)S(1)}, bf16[640,768]{1,0:T(8,128)(2,1)S(1)}, u32[]{:S(2)}, u32[]{:S(2)}) collective-permute-start(bf16[640,768]{1,0:T(8,128)(2,1)S(1)} %get-tuple-element.37), channel_id=1, source_target_pairs={{0,2},{1,3},{2,0},{3,1},{4,6},{5,7},{6,4},{7,5},{8,10},{9,11},{10,... | collective-permute-start | bytes 2949128 | tf_op jit(solution)/shard_map/ppermute | solution.py:481
  23.5 55.7 %collective-permute-start.5 = (bf16[288,1280]{1,0:T(8,128)(2,1)S(1)}, bf16[288,1280]{1,0:T(8,128)(2,1)S(1)}, u32[]{:S(2)}, u32[]{:S(2)}) collective-permute-start(bf16[288,1280]{1,0:T(8,128)(2,1)S(1)} %get-tuple-element.36), channel_id=1, source_target_pairs={{0,6},{1,7},{2,0},{3,1},{4,2},{5,3},{6,4},{7,5},{8,14},{9,15},{10,... | collective-permute-start | bytes 2211848 | tf_op jit(solution)/shard_map/ppermute | solution.py:457
  28.0 54.4 %collective-permute-start.23 = (bf16[640,768]{1,0:T(8,128)(2,1)S(1)}, bf16[640,768]{1,0:T(8,128)(2,1)S(1)}, u32[]{:S(2)}, u32[]{:S(2)}) collective-permute-start(bf16[640,768]{1,0:T(8,128)(2,1)S(1)} %get-tuple-element.38), channel_id=1, source_target_pairs={{2,4},{3,5},{4,2},{5,3},{10,12},{11,13},{12,10},{13,11},{18,20},{1... | collective-permute-start | bytes 2949128 | tf_op jit(solution)/shard_map/ppermute | solution.py:481
  58.0 42.1 %collective-permute-start.21 = (bf16[640,768]{1,0:T(8,128)(2,1)S(1)}, bf16[640,768]{1,0:T(8,128)(2,1)}, u32[]{:S(2)}, u32[]{:S(2)}) collective-permute-start(bf16[640,768]{1,0:T(8,128)(2,1)S(1)} %get-tuple-element.38), channel_id=1, source_target_pairs={{0,2},{1,3},{2,0},{3,1},{4,6},{5,7},{6,4},{7,5},{8,10},{9,11},{10,... | collective-permute-start | bytes 2949128 | tf_op jit(solution)/shard_map/ppermute | solution.py:481
  79.2 21.4 %collective-permute-start.19 = (bf16[288,1280]{1,0:T(8,128)(2,1)S(1)}, bf16[288,1280]{1,0:T(8,128)(2,1)S(1)}, u32[]{:S(2)}, u32[]{:S(2)}) collective-permute-start(bf16[288,1280]{1,0:T(8,128)(2,1)S(1)} %collective-permute-done.17.refs_1_), channel_id=1, source_target_pairs={{0,16},{8,24},{16,0},{24,8},{1,17},{9,25},{17,1},{25,9},{2,18},{10... | collective-permute-start | bytes 2211848 | tf_op jit(solution)/shard_map/ppermute | solution.py:46
  80.3 34.0 %collective-permute-start.14 = (bf16[288,1280]{1,0:T(8,128)(2,1)S(1)}, bf16[288,1280]{1,0:T(8,128)(2,1)S(1)}, u32[]{:S(2)}, u32[]{:S(2)}) collective-permute-start(bf16[288,1280]{1,0:T(8,128)(2,1)S(1)} %collective-permute-done.13.refs_0_), channel_id=1, source_target_pairs={{0,16},{8,24},{16,0},{24,8},{1,17},{9,25},{17,1},{25,9},{2,18},{10... | collective-permute-start | bytes 2211848 | tf_op jit(solution)/shard_map/ppermute | solution.py:46
  81.2 33.1 %collective-permute-start.15 = (bf16[288,1280]{1,0:T(8,128)(2,1)S(1)}, bf16[288,1280]{1,0:T(8,128)(2,1)S(1)}, u32[]{:S(2)}, u32[]{:S(2)}) collective-permute-start(bf16[288,1280]{1,0:T(8,128)(2,1)S(1)} %collective-permute-done.13.refs_0_), channel_id=1, source_target_pairs={{0,8},{8,0},{16,24},{24,16},{1,9},{9,1},{17,25},{25,17},{2,10},{10... | collective-permute-start | bytes 2211848 | tf_op jit(solution)/shard_map/ppermute | solution.py:46
  82.3 33.1 %collective-permute-start.10 = (bf16[288,1280]{1,0:T(8,128)(2,1)S(1)}, bf16[288,1280]{1,0:T(8,128)(2,1)S(1)}, u32[]{:S(2)}, u32[]{:S(2)}) collective-permute-start(bf16[288,1280]{1,0:T(8,128)(2,1)S(1)} %collective-permute-done.9.refs_0_), channel_id=1, source_target_pairs={{0,8},{8,0},{16,24},{24,16},{1,9},{9,1},{17,25},{25,17},{2,10},{10... | collective-permute-start | bytes 2211848 | tf_op jit(solution)/shard_map/ppermute | solution.py:46
  100.1 30.1 %collective-permute-start.11 = (bf16[288,1280]{1,0:T(8,128)(2,1)S(1)}, bf16[288,1280]{1,0:T(8,128)(2,1)S(1)}, u32[]{:S(2)}, u32[]{:S(2)}) collective-permute-start(bf16[288,1280]{1,0:T(8,128)(2,1)S(1)} %collective-permute-done.9.refs_0_), channel_id=1, source_target_pairs={{0,16},{8,24},{16,0},{24,8},{1,17},{9,25},{17,1},{25,9},{2,18},{10... | collective-permute-start | bytes 2211848 | tf_op jit(solution)/shard_map/ppermute | solution.py:46
  100.6 44.0 %collective-permute-start.6 = (bf16[288,1280]{1,0:T(8,128)(2,1)S(1)}, bf16[288,1280]{1,0:T(8,128)(2,1)S(1)}, u32[]{:S(2)}, u32[]{:S(2)}) collective-permute-start(bf16[288,1280]{1,0:T(8,128)(2,1)S(1)} %collective-permute-done.5.refs_0_), channel_id=1, source_target_pairs={{0,16},{8,24},{16,0},{24,8},{1,17},{9,25},{17,1},{25,9},{2,18},{10... | collective-permute-start | bytes 2211848 | tf_op jit(solution)/shard_map/ppermute | solution.py:46
  114.3 47.6 %collective-permute-start.20 = (bf16[640,1536]{1,0:T(8,128)(2,1)S(1)}, bf16[640,1536]{1,0:T(8,128)(2,1)S(1)}, u32[]{:S(2)}, u32[]{:S(2)}) collective-permute-start(bf16[640,1536]{1,0:T(8,128)(2,1)S(1)} %copy-done.2), channel_id=1, source_target_pairs={{0,1},{1,0},{2,3},{3,2},{4,5},{5,4},{6,7},{7,6},{8,9},{9,8},{10,11... | collective-permute-start | bytes 5898248 | tf_op jit(solution)/shard_map/ppermute | solution.py:461
  114.3 30.9 %collective-permute-start.7 = (bf16[288,1280]{1,0:T(8,128)(2,1)S(1)}, bf16[288,1280]{1,0:T(8,128)(2,1)S(1)}, u32[]{:S(2)}, u32[]{:S(2)}) collective-permute-start(bf16[288,1280]{1,0:T(8,128)(2,1)S(1)} %collective-permute-done.5.refs_0_), channel_id=1, source_target_pairs={{0,8},{8,0},{16,24},{24,16},{1,9},{9,1},{17,25},{25,17},{2,10},{10... | collective-permute-start | bytes 2211848 | tf_op jit(solution)/shard_map/ppermute | solution.py:46
  115.5 41.7 %collective-permute-start.45 = (bf16[640,768]{1,0:T(8,128)(2,1)S(1)}, bf16[640,768]{1,0:T(8,128)(2,1)S(1)}, u32[]{:S(2)}, u32[]{:S(2)}) collective-permute-start(bf16[640,768]{1,0:T(8,128)(2,1)S(1)} %collective-permute-done.43.refs_4_), channel_id=1, source_target_pairs={{2,0},{3,1},{4,6},{5,7},{10,8},{11,9},{12,14},{13,15},{18,16},{19,... | collective-permute-start | bytes 2949128 | tf_op jit(solution)/shard_map/ppermute | solution.py:481
  130.1 28.3 %collective-permute-start.42 = (bf16[640,768]{1,0:T(8,128)(2,1)S(1)}, bf16[640,768]{1,0:T(8,128)(2,1)S(1)}, u32[]{:S(2)}, u32[]{:S(2)}) collective-permute-start(bf16[640,768]{1,0:T(8,128)(2,1)S(1)} %collective-permute-done.41.refs_2_), channel_id=1, source_target_pairs={{0,1},{1,0},{2,3},{3,2},{4,5},{5,4},{6,7},{7,6},{8,9},{9,8},{10,11... | collective-permute-start | bytes 2949128 | tf_op jit(solution)/shard_map/ppermute | solution.py:488
  144.5 15.5 %collective-permute-start.47 = (bf16[640,768]{1,0:T(8,128)(2,1)S(1)}, bf16[640,768]{1,0:T(8,128)(2,1)S(1)}, u32[]{:S(2)}, u32[]{:S(2)}) collective-permute-start(bf16[640,768]{1,0:T(8,128)(2,1)S(1)} %collective-permute-done.41.refs_2_), channel_id=1, source_target_pairs={{2,4},{3,5},{4,2},{5,3},{10,12},{11,13},{12,10},{13,11},{18,20},{1... | collective-permute-start | bytes 2949128 | tf_op jit(solution)/shard_map/ppermute | solution.py:481
  145.3 16.1 %collective-permute-start.44 = (bf16[640,768]{1,0:T(8,128)(2,1)S(1)}, bf16[640,768]{1,0:T(8,128)(2,1)S(1)}, u32[]{:S(2)}, u32[]{:S(2)}) collective-permute-start(bf16[640,768]{1,0:T(8,128)(2,1)S(1)} %collective-permute-done.43.refs_4_), channel_id=1, source_target_pairs={{2,3},{3,2},{4,5},{5,4},{10,11},{11,10},{12,13},{13,12},{18,19},{1... | collective-permute-start | bytes 2949128 | tf_op jit(solution)/shard_map/ppermute | solution.py:488
  157.1 31.8 %collective-permute-start.25 = (bf16[640,768]{1,0:T(8,128)(2,1)S(1)}, bf16[640,768]{1,0:T(8,128)(2,1)S(1)}, u32[]{:S(2)}, u32[]{:S(2)}) collective-permute-start(bf16[640,768]{1,0:T(8,128)(2,1)S(1)} %collective-permute-done.23.refs_4_), channel_id=1, source_target_pairs={{2,0},{3,1},{4,6},{5,7},{10,8},{11,9},{12,14},{13,15},{18,16},{19,... | collective-permute-start | bytes 2949128 | tf_op jit(solution)/shard_map/ppermute | solution.py:481
  158.4 32.5 %collective-permute-start.27 = (bf16[640,768]{1,0:T(8,128)(2,1)}, bf16[640,768]{1,0:T(8,128)(2,1)}, u32[]{:S(2)}, u32[]{:S(2)}) collective-permute-start(bf16[640,768]{1,0:T(8,128)(2,1)} %collective-permute-done.21.refs_2_), channel_id=1, source_target_pairs={{2,4},{3,5},{4,2},{5,3},{10,12},{11,13},{12,10},{13,11},{18,20},{1... | collective-permute-start | bytes 2949128 | tf_op jit(solution)/shard_map/ppermute | solution.py:481
  160.0 49.8 %collective-permute-start.49 = (bf16[640,768]{1,0:T(8,128)(2,1)S(1)}, bf16[640,768]{1,0:T(8,128)(2,1)S(1)}, u32[]{:S(2)}, u32[]{:S(2)}) collective-permute-start(bf16[640,768]{1,0:T(8,128)(2,1)S(1)} %collective-permute-done.47.refs_0_), channel_id=1, source_target_pairs={{2,0},{3,1},{4,6},{5,7},{10,8},{11,9},{12,14},{13,15},{18,16},{19,... | collective-permute-start | bytes 2949128 | tf_op jit(solution)/shard_map/ppermute | solution.py:481
  161.3 30.3 %collective-permute-start.16 = (bf16[288,1280]{1,0:T(8,128)(2,1)S(1)}, bf16[288,1280]{1,0:T(8,128)(2,1)S(1)}, u32[]{:S(2)}, u32[]{:S(2)}) collective-permute-start(bf16[288,1280]{1,0:T(8,128)(2,1)S(1)} %collective-permute-done.14.refs_1_), channel_id=1, source_target_pairs={{0,8},{8,0},{16,24},{24,16},{1,9},{9,1},{17,25},{25,17},{2,10},{10... | collective-permute-start | bytes 2211848 | tf_op jit(solution)/shard_map/ppermute | solution.py:46
  162.0 49.8 %collective-permute-start.12 = (bf16[288,1280]{1,0:T(8,128)(2,1)S(1)}, bf16[288,1280]{1,0:T(8,128)(2,1)S(1)}, u32[]{:S(2)}, u32[]{:S(2)}) collective-permute-start(bf16[288,1280]{1,0:T(8,128)(2,1)S(1)} %collective-permute-done.10.refs_1_), channel_id=1, source_target_pairs={{0,16},{8,24},{16,0},{24,8},{1,17},{9,25},{17,1},{25,9},{2,18},{10... | collective-permute-start | bytes 2211848 | tf_op jit(solution)/shard_map/ppermute | solution.py:46
  189.0 41.8 %collective-permute-start.46 = (bf16[640,768]{1,0:T(8,128)(2,1)S(1)}, bf16[640,768]{1,0:T(8,128)(2,1)S(1)}, u32[]{:S(2)}, u32[]{:S(2)}) collective-permute-start(bf16[640,768]{1,0:T(8,128)(2,1)S(1)} %collective-permute-done.45.refs_6_), channel_id=1, source_target_pairs={{0,1},{1,0},{6,7},{7,6},{8,9},{9,8},{14,15},{15,14},{16,17},{17,16... | collective-permute-start | bytes 2949128 | tf_op jit(solution)/shard_map/ppermute | solution.py:488
  190.9 41.4 %collective-permute-start.48 = (bf16[640,768]{1,0:T(8,128)(2,1)S(1)}, bf16[640,768]{1,0:T(8,128)(2,1)S(1)}, u32[]{:S(2)}, u32[]{:S(2)}) collective-permute-start(bf16[640,768]{1,0:T(8,128)(2,1)S(1)} %collective-permute-done.47.refs_0_), channel_id=1, source_target_pairs={{2,3},{3,2},{4,5},{5,4},{10,11},{11,10},{12,13},{13,12},{18,19},{1... | collective-permute-start | bytes 2949128 | tf_op jit(solution)/shard_map/ppermute | solution.py:488
  191.6 61.2 %collective-permute-start.29 = (bf16[640,768]{1,0:T(8,128)(2,1)}, bf16[640,768]{1,0:T(8,128)(2,1)}, u32[]{:S(2)}, u32[]{:S(2)}) collective-permute-start(bf16[640,768]{1,0:T(8,128)(2,1)} %collective-permute-done.27.refs_0_), channel_id=1, source_target_pairs={{2,0},{3,1},{4,6},{5,7},{10,8},{11,9},{12,14},{13,15},{18,16},{19,... | collective-permute-start | bytes 2949128 | tf_op jit(solution)/shard_map/ppermute | solution.py:481
  209.8 44.6 %collective-permute-start.50 = (bf16[640,768]{1,0:T(8,128)(2,1)S(1)}, bf16[640,768]{1,0:T(8,128)(2,1)S(1)}, u32[]{:S(2)}, u32[]{:S(2)}) collective-permute-start(bf16[640,768]{1,0:T(8,128)(2,1)S(1)} %collective-permute-done.49.refs_2_), channel_id=1, source_target_pairs={{0,1},{1,0},{6,7},{7,6},{8,9},{9,8},{14,15},{15,14},{16,17},{17,16... | collective-permute-start | bytes 2949128 | tf_op jit(solution)/shard_map/ppermute | solution.py:488
  211.8 19.0 %collective-permute-start.8 = (bf16[288,1280]{1,0:T(8,128)(2,1)S(1)}, bf16[288,1280]{1,0:T(8,128)(2,1)S(1)}, u32[]{:S(2)}, u32[]{:S(2)}) collective-permute-start(bf16[288,1280]{1,0:T(8,128)(2,1)S(1)} %collective-permute-done.6.refs_1_), channel_id=1, source_target_pairs={{0,8},{8,0},{16,24},{24,16},{1,9},{9,1},{17,25},{25,17},{2,10},{10... | collective-permute-start | bytes 2211848 | tf_op jit(solution)/shard_map/ppermute | solution.py:46
  230.7 50.8 %collective-permute-start.22 = (bf16[640,768]{1,0:T(8,128)(2,1)}, bf16[640,768]{1,0:T(8,128)(2,1)}, u32[]{:S(2)}, u32[]{:S(2)}) collective-permute-start(bf16[640,768]{1,0:T(8,128)(2,1)} %collective-permute-done.21.refs_2_), channel_id=1, source_target_pairs={{0,1},{1,0},{2,3},{3,2},{4,5},{5,4},{6,7},{7,6},{8,9},{9,8},{10,11... | collective-permute-start | bytes 2949128 | tf_op jit(solution)/shard_map/ppermute | solution.py:488
  230.7 51.1 %collective-permute-start.24 = (bf16[640,768]{1,0:T(8,128)(2,1)S(1)}, bf16[640,768]{1,0:T(8,128)(2,1)}, u32[]{:S(2)}, u32[]{:S(2)}) collective-permute-start(bf16[640,768]{1,0:T(8,128)(2,1)S(1)} %collective-permute-done.23.refs_4_), channel_id=1, source_target_pairs={{2,3},{3,2},{4,5},{5,4},{10,11},{11,10},{12,13},{13,12},{18,19},{1... | collective-permute-start | bytes 2949128 | tf_op jit(solution)/shard_map/ppermute | solution.py:488
  232.3 49.8 %collective-permute-start.26 = (bf16[640,768]{1,0:T(8,128)(2,1)S(1)}, bf16[640,768]{1,0:T(8,128)(2,1)}, u32[]{:S(2)}, u32[]{:S(2)}) collective-permute-start(bf16[640,768]{1,0:T(8,128)(2,1)S(1)} %collective-permute-done.25.refs_6_), channel_id=1, source_target_pairs={{0,1},{1,0},{6,7},{7,6},{8,9},{9,8},{14,15},{15,14},{16,17},{17,16... | collective-permute-start | bytes 2949128 | tf_op jit(solution)/shard_map/ppermute | solution.py:488
  252.8 40.8 %collective-permute-start.28 = (bf16[640,768]{1,0:T(8,128)(2,1)}, bf16[640,768]{1,0:T(8,128)(2,1)}, u32[]{:S(2)}, u32[]{:S(2)}) collective-permute-start(bf16[640,768]{1,0:T(8,128)(2,1)} %collective-permute-done.27.refs_0_), channel_id=1, source_target_pairs={{2,3},{3,2},{4,5},{5,4},{10,11},{11,10},{12,13},{13,12},{18,19},{1... | collective-permute-start | bytes 2949128 | tf_op jit(solution)/shard_map/ppermute | solution.py:488
  255.4 38.2 %collective-permute-start.30 = (bf16[640,768]{1,0:T(8,128)(2,1)}, bf16[640,768]{1,0:T(8,128)(2,1)}, u32[]{:S(2)}, u32[]{:S(2)}) collective-permute-start(bf16[640,768]{1,0:T(8,128)(2,1)} %collective-permute-done.29.refs_2_), channel_id=1, source_target_pairs={{0,1},{1,0},{6,7},{7,6},{8,9},{9,8},{14,15},{15,14},{16,17},{17,16... | collective-permute-start | bytes 2949128 | tf_op jit(solution)/shard_map/ppermute | solution.py:488
  281.6 19.1 %collective-permute-start.1 = (bf16[256,1280]{1,0:T(8,128)(2,1)}, bf16[256,1280]{1,0:T(8,128)(2,1)S(1)}, u32[]{:S(2)}, u32[]{:S(2)}) collective-permute-start(bf16[256,1280]{1,0:T(8,128)(2,1)} %refs_0_.5), channel_id=1, source_target_pairs={{0,2},{1,3},{2,4},{3,5},{4,6},{5,7},{6,0},{7,1},{8,10},{9,11},{10,... | collective-permute-start | bytes 1966088 | tf_op jit(solution)/shard_map/ppermute | solution.py:457
  281.8 36.9 %collective-permute-start.51 = (bf16[1152,512]{1,0:T(8,128)(2,1)}, bf16[1152,512]{1,0:T(8,128)(2,1)S(1)}, u32[]{:S(2)}, u32[]{:S(2)}) collective-permute-start(bf16[1152,512]{1,0:T(8,128)(2,1)} %get-tuple-element.26.refs_0_), channel_id=1, source_target_pairs={{0,1},{1,0},{2,3},{3,2},{4,5},{5,4},{6,7},{7,6},{8,9},{9,8},{10,11... | collective-permute-start | bytes 3538952 | tf_op jit(solution)/shard_map/ppermute | solution.py:503
  298.3 29.9 %collective-permute-start.31 = (bf16[1152,512]{1,0:T(8,128)(2,1)S(1)}, bf16[1152,512]{1,0:T(8,128)(2,1)S(1)}, u32[]{:S(2)}, u32[]{:S(2)}) collective-permute-start(bf16[1152,512]{1,0:T(8,128)(2,1)S(1)} %get-tuple-element.20.refs_0_), channel_id=1, source_target_pairs={{0,1},{1,0},{2,3},{3,2},{4,5},{5,4},{6,7},{7,6},{8,9},{9,8},{10,11... | collective-permute-start | bytes 3538952 | tf_op jit(solution)/shard_map/ppermute | solution.py:503
  300.7 18.1 %collective-permute-start.3 = (bf16[256,1280]{1,0:T(8,128)(2,1)S(1)}, bf16[256,1280]{1,0:T(8,128)(2,1)S(1)}, u32[]{:S(2)}, u32[]{:S(2)}) collective-permute-start(bf16[256,1280]{1,0:T(8,128)(2,1)S(1)} %collective-permute-done.1.refs_2_), channel_id=1, source_target_pairs={{0,2},{1,3},{2,4},{3,5},{4,6},{5,7},{6,0},{7,1},{8,10},{9,11},{10,... | collective-permute-start | bytes 1966088 | tf_op jit(solution)/shard_map/ppermute | solution.py:457
  300.7 31.6 %collective-permute-start = (bf16[256,1280]{1,0:T(8,128)(2,1)}, bf16[256,1280]{1,0:T(8,128)(2,1)S(1)}, u32[]{:S(2)}, u32[]{:S(2)}) collective-permute-start(bf16[256,1280]{1,0:T(8,128)(2,1)} %refs_0_.5), channel_id=1, source_target_pairs={{0,1},{1,0},{2,3},{3,2},{4,5},{5,4},{6,7},{7,6},{8,9},{9,8},{10,11... | collective-permute-start | bytes 1966088 | tf_op jit(solution)/shard_map/ppermute | solution.py:461
  300.7 32.2 %collective-permute-start.2 = (bf16[256,1280]{1,0:T(8,128)(2,1)S(1)}, bf16[256,1280]{1,0:T(8,128)(2,1)S(1)}, u32[]{:S(2)}, u32[]{:S(2)}) collective-permute-start(bf16[256,1280]{1,0:T(8,128)(2,1)S(1)} %collective-permute-done.1.refs_2_), channel_id=1, source_target_pairs={{0,1},{1,0},{2,3},{3,2},{4,5},{5,4},{6,7},{7,6},{8,9},{9,8},{10,11... | collective-permute-start | bytes 1966088 | tf_op jit(solution)/shard_map/ppermute | solution.py:461
  318.8 14.9 %collective-permute-start.4 = (bf16[256,1280]{1,0:T(8,128)(2,1)S(1)}, bf16[256,1280]{1,0:T(8,128)(2,1)S(1)}, u32[]{:S(2)}, u32[]{:S(2)}) collective-permute-start(bf16[256,1280]{1,0:T(8,128)(2,1)S(1)} %collective-permute-done.3.refs_4_), channel_id=1, source_target_pairs={{0,1},{1,0},{2,3},{3,2},{4,5},{5,4},{6,7},{7,6},{8,9},{9,8},{10,11... | collective-permute-start | bytes 1966088 | tf_op jit(solution)/shard_map/ppermute | solution.py:461
  318.8 20.7 %collective-permute-start.67 = (bf16[256,1280]{1,0:T(8,128)(2,1)S(1)}, bf16[256,1280]{1,0:T(8,128)(2,1)S(1)}, u32[]{:S(2)}, u32[]{:S(2)}) collective-permute-start(bf16[256,1280]{1,0:T(8,128)(2,1)S(1)} %collective-permute-done.3.refs_4_), channel_id=1, source_target_pairs={{0,2},{1,3},{2,4},{3,5},{4,6},{5,7},{6,0},{7,1},{8,10},{9,11},{10,... | collective-permute-start | bytes 1966088 | tf_op jit(solution)/shard_map/ppermute | solution.py:457
  328.2 25.7 %collective-permute-start.64 = (bf16[288,256]{1,0:T(8,128)(2,1)S(1)}, bf16[288,256]{1,0:T(8,128)(2,1)S(1)}, u32[]{:S(2)}, u32[]{:S(2)}) collective-permute-start(bf16[288,256]{1,0:T(8,128)(2,1)S(1)} %get-tuple-element.30.refs_26_), channel_id=1, source_target_pairs={{0,16},{8,24},{16,0},{24,8},{1,17},{9,25},{17,1},{25,9},{2,18},{10... | collective-permute-start | bytes 442376 | tf_op jit(solution)/shard_map/ppermute | solution.py:46
  332.3 21.7 %collective-permute-start.65 = (bf16[288,256]{1,0:T(8,128)(2,1)S(1)}, bf16[288,256]{1,0:T(8,128)(2,1)S(1)}, u32[]{:S(2)}, u32[]{:S(2)}) collective-permute-start(bf16[288,256]{1,0:T(8,128)(2,1)S(1)} %get-tuple-element.30.refs_26_), channel_id=1, source_target_pairs={{0,8},{8,0},{16,24},{24,16},{1,9},{9,1},{17,25},{25,17},{2,10},{10... | collective-permute-start | bytes 442376 | tf_op jit(solution)/shard_map/ppermute | solution.py:46
  332.9 21.0 %collective-permute-start.60 = (bf16[288,256]{1,0:T(8,128)(2,1)S(1)}, bf16[288,256]{1,0:T(8,128)(2,1)S(1)}, u32[]{:S(2)}, u32[]{:S(2)}) collective-permute-start(bf16[288,256]{1,0:T(8,128)(2,1)S(1)} %get-tuple-element.29), channel_id=1, source_target_pairs={{0,4},{1,5},{2,6},{3,7},{4,0},{5,1},{6,2},{7,3},{8,12},{9,13},{10,... | collective-permute-start | bytes 442376 | tf_op jit(solution)/shard_map/ppermute | solution.py:457
  333.6 16.9 %collective-permute-start.37 = (bf16[288,256]{1,0:T(8,128)(2,1)S(1)}, bf16[288,256]{1,0:T(8,128)(2,1)S(1)}, u32[]{:S(2)}, u32[]{:S(2)}) collective-permute-start(bf16[288,256]{1,0:T(8,128)(2,1)S(1)} %get-tuple-element.23), channel_id=1, source_target_pairs={{0,4},{1,5},{2,6},{3,7},{4,0},{5,1},{6,2},{7,3},{8,12},{9,13},{10,... | collective-permute-start | bytes 442376 | tf_op jit(solution)/shard_map/ppermute | solution.py:457
  339.5 15.8 %collective-permute-start.52 = (bf16[288,256]{1,0:T(8,128)(2,1)S(1)}, bf16[288,256]{1,0:T(8,128)(2,1)S(1)}, u32[]{:S(2)}, u32[]{:S(2)}) collective-permute-start(bf16[288,256]{1,0:T(8,128)(2,1)S(1)} %get-tuple-element.27), channel_id=1, source_target_pairs={{0,6},{1,7},{2,0},{3,1},{4,2},{5,3},{6,4},{7,5},{8,14},{9,15},{10,... | collective-permute-start | bytes 442376 | tf_op jit(solution)/shard_map/ppermute | solution.py:457
  353.9 10.4 %collective-permute-start.33 = (bf16[288,256]{1,0:T(8,128)(2,1)S(1)}, bf16[288,256]{1,0:T(8,128)(2,1)S(1)}, u32[]{:S(2)}, u32[]{:S(2)}) collective-permute-start(bf16[288,256]{1,0:T(8,128)(2,1)S(1)} %get-tuple-element.22), channel_id=1, source_target_pairs={{0,2},{1,3},{2,4},{3,5},{4,6},{5,7},{6,0},{7,1},{8,10},{9,11},{10,... | collective-permute-start | bytes 442376 | tf_op jit(solution)/shard_map/ppermute | solution.py:457
  354.0 11.6 %collective-permute-start.61 = (bf16[288,256]{1,0:T(8,128)(2,1)S(1)}, bf16[288,256]{1,0:T(8,128)(2,1)S(1)}, u32[]{:S(2)}, u32[]{:S(2)}) collective-permute-start(bf16[288,256]{1,0:T(8,128)(2,1)S(1)} %collective-permute-done.60.refs_22_), channel_id=1, source_target_pairs={{0,8},{8,0},{16,24},{24,16},{1,9},{9,1},{17,25},{25,17},{2,10},{10... | collective-permute-start | bytes 442376 | tf_op jit(solution)/shard_map/ppermute | solution.py:46
  355.3 11.1 %collective-permute-start.62 = (bf16[288,256]{1,0:T(8,128)(2,1)S(1)}, bf16[288,256]{1,0:T(8,128)(2,1)S(1)}, u32[]{:S(2)}, u32[]{:S(2)}) collective-permute-start(bf16[288,256]{1,0:T(8,128)(2,1)S(1)} %collective-permute-done.60.refs_22_), channel_id=1, source_target_pairs={{0,16},{8,24},{16,0},{24,8},{1,17},{9,25},{17,1},{25,9},{2,18},{10... | collective-permute-start | bytes 442376 | tf_op jit(solution)/shard_map/ppermute | solution.py:46
  358.1 9.6 %collective-permute-start.66 = (bf16[288,256]{1,0:T(8,128)(2,1)S(1)}, bf16[288,256]{1,0:T(8,128)(2,1)S(1)}, u32[]{:S(2)}, u32[]{:S(2)}) collective-permute-start(bf16[288,256]{1,0:T(8,128)(2,1)S(1)} %collective-permute-done.64.refs_27_), channel_id=1, source_target_pairs={{0,8},{8,0},{16,24},{24,16},{1,9},{9,1},{17,25},{25,17},{2,10},{10... | collective-permute-start | bytes 442376 | tf_op jit(solution)/shard_map/ppermute | solution.py:46
  364.3 11.1 %collective-permute-start.54 = (bf16[288,256]{1,0:T(8,128)(2,1)S(1)}, bf16[288,256]{1,0:T(8,128)(2,1)S(1)}, u32[]{:S(2)}, u32[]{:S(2)}) collective-permute-start(bf16[288,256]{1,0:T(8,128)(2,1)S(1)} %collective-permute-done.52.refs_14_), channel_id=1, source_target_pairs={{0,16},{8,24},{16,0},{24,8},{1,17},{9,25},{17,1},{25,9},{2,18},{10... | collective-permute-start | bytes 442376 | tf_op jit(solution)/shard_map/ppermute | solution.py:46
  366.4 19.6 %collective-permute-start.38 = (bf16[576,256]{1,0:T(8,128)(2,1)S(1)}, bf16[576,256]{1,0:T(8,128)(2,1)S(1)}, u32[]{:S(2)}, u32[]{:S(2)}) collective-permute-start(bf16[576,256]{1,0:T(8,128)(2,1)S(1)} %constant_dynamic-update-slice_fusion.2.refs_10_), channel_id=1, source_target_pairs={{0,16},{8,24},{16,0},{24,8},{1,17},{9,25},{17,1},{25,9},{2,18},{10... | collective-permute-start | bytes 884744 | tf_op jit(solution)/shard_map/ppermute | solution.py:46
  367.7 19.8 %collective-permute-start.34 = (bf16[576,256]{1,0:T(8,128)(2,1)S(1)}, bf16[576,256]{1,0:T(8,128)(2,1)S(1)}, u32[]{:S(2)}, u32[]{:S(2)}) collective-permute-start(bf16[576,256]{1,0:T(8,128)(2,1)S(1)} %constant_dynamic-update-slice_fusion.refs_6_), channel_id=1, source_target_pairs={{0,8},{8,0},{16,24},{24,16},{1,9},{9,1},{17,25},{25,17},{2,10},{10... | collective-permute-start | bytes 884744 | tf_op jit(solution)/shard_map/ppermute | solution.py:46
  374.2 9.0 %collective-permute-start.63 = (bf16[288,256]{1,0:T(8,128)(2,1)S(1)}, bf16[288,256]{1,0:T(8,128)(2,1)S(1)}, u32[]{:S(2)}, u32[]{:S(2)}) collective-permute-start(bf16[288,256]{1,0:T(8,128)(2,1)S(1)} %collective-permute-done.61.refs_23_), channel_id=1, source_target_pairs={{0,16},{8,24},{16,0},{24,8},{1,17},{9,25},{17,1},{25,9},{2,18},{10... | collective-permute-start | bytes 442376 | tf_op jit(solution)/shard_map/ppermute | solution.py:46
  375.4 9.3 %collective-permute-start.55 = (bf16[288,256]{1,0:T(8,128)(2,1)S(1)}, bf16[288,256]{1,0:T(8,128)(2,1)S(1)}, u32[]{:S(2)}, u32[]{:S(2)}) collective-permute-start(bf16[288,256]{1,0:T(8,128)(2,1)S(1)} %collective-permute-done.53.refs_15_), channel_id=1, source_target_pairs={{0,16},{8,24},{16,0},{24,8},{1,17},{9,25},{17,1},{25,9},{2,18},{10... | collective-permute-start | bytes 442376 | tf_op jit(solution)/shard_map/ppermute | solution.py:46
  378.0 10.0 %collective-permute-start.59 = (bf16[288,256]{1,0:T(8,128)(2,1)S(1)}, bf16[288,256]{1,0:T(8,128)(2,1)S(1)}, u32[]{:S(2)}, u32[]{:S(2)}) collective-permute-start(bf16[288,256]{1,0:T(8,128)(2,1)S(1)} %collective-permute-done.57.refs_19_), channel_id=1, source_target_pairs={{0,8},{8,0},{16,24},{24,16},{1,9},{9,1},{17,25},{25,17},{2,10},{10... | collective-permute-start | bytes 442376 | tf_op jit(solution)/shard_map/ppermute | solution.py:46
  383.2 9.5 %collective-permute-start.39 = (bf16[576,256]{1,0:T(8,128)(2,1)S(1)}, bf16[576,256]{1,0:T(8,128)(2,1)S(1)}, u32[]{:S(2)}, u32[]{:S(2)}) collective-permute-start(bf16[576,256]{1,0:T(8,128)(2,1)S(1)} %constant_dynamic-update-slice_fusion.2.refs_10_), channel_id=1, source_target_pairs={{0,8},{8,0},{16,24},{24,16},{1,9},{9,1},{17,25},{25,17},{2,10},{10... | collective-permute-start | bytes 884744 | tf_op jit(solution)/shard_map/ppermute | solution.py:46
  384.8 9.9 %collective-permute-start.35 = (bf16[576,256]{1,0:T(8,128)(2,1)S(1)}, bf16[576,256]{1,0:T(8,128)(2,1)S(1)}, u32[]{:S(2)}, u32[]{:S(2)}) collective-permute-start(bf16[576,256]{1,0:T(8,128)(2,1)S(1)} %constant_dynamic-update-slice_fusion.refs_6_), channel_id=1, source_target_pairs={{0,16},{8,24},{16,0},{24,8},{1,17},{9,25},{17,1},{25,9},{2,18},{10... | collective-permute-start | bytes 884744 | tf_op jit(solution)/shard_map/ppermute | solution.py:46
  386.0 9.8 %collective-permute-start.40 = (bf16[576,256]{1,0:T(8,128)(2,1)S(1)}, bf16[576,256]{1,0:T(8,128)(2,1)S(1)}, u32[]{:S(2)}, u32[]{:S(2)}) collective-permute-start(bf16[576,256]{1,0:T(8,128)(2,1)S(1)} %collective-permute-done.38.refs_11_), channel_id=1, source_target_pairs={{0,8},{8,0},{16,24},{24,16},{1,9},{9,1},{17,25},{25,17},{2,10},{10... | collective-permute-start | bytes 884744 | tf_op jit(solution)/shard_map/ppermute | solution.py:46
  387.5 10.6 %collective-permute-start.36 = (bf16[576,256]{1,0:T(8,128)(2,1)S(1)}, bf16[576,256]{1,0:T(8,128)(2,1)S(1)}, u32[]{:S(2)}, u32[]{:S(2)}) collective-permute-start(bf16[576,256]{1,0:T(8,128)(2,1)S(1)} %collective-permute-done.34.refs_7_), channel_id=1, source_target_pairs={{0,16},{8,24},{16,0},{24,8},{1,17},{9,25},{17,1},{25,9},{2,18},{10... | collective-permute-start | bytes 884744 | tf_op jit(solution)/shard_map/ppermute | solution.py:46
  388.0 18.8 %collective-permute-start.68 = (bf16[256,1280]{1,0:T(8,128)(2,1)S(1)}, bf16[256,1280]{1,0:T(8,128)(2,1)S(1)}, u32[]{:S(2)}, u32[]{:S(2)}) collective-permute-start(bf16[256,1280]{1,0:T(8,128)(2,1)S(1)} %collective-permute-done.67.refs_0_), channel_id=1, source_target_pairs={{0,1},{1,0},{2,3},{3,2},{4,5},{5,4},{6,7},{7,6},{8,9},{9,8},{10,11... | collective-permute-start | bytes 1966088 | tf_op jit(solution)/shard_map/ppermute | solution.py:461
  (25 other events, 849.5 us)

commit v3 on v2

--- a/solution.py
+++ b/solution.py
@@ -330,7 +330,6 @@
     heads = []
     for n, (chunk, mask, block) in enumerate(tags):
         if last:
-            heads.append(pltpu.make_async_copy(o_refs[n], o_v, o_sem.at[n]))
             continue
         size, width = o_refs[n].shape
         per = parts * w_refs[0].shape[0] // (CHUNKS * width)
@@ -351,10 +350,13 @@
                     w_refs[n].at[:, span], w_v.at[pl.ds(at, depth), span], w_sem.at[m, n]
                 )
             )
-    bases = [
-        pltpu.make_async_copy(base_ref.at[n if last else spot], b_v.at[n], b_sem.at[n])
-        for n, spot in enumerate(spots)
-    ]
+    bases = []
+    if not last:
+        bases = [
+            pltpu.make_async_copy(base_ref.at[spot], b_v.at[n], b_sem.at[n])
+            for n, spot in enumerate(spots)
+        ]
+    held, added = (o_refs[0], base_ref) if last else (o_v, b_v)
     per = len(w_tags)
     for copy in heads + weights[:per] + bases + weights[per:]:
         copy.start()
@@ -382,13 +384,13 @@
         def body(block, carry, m=m, begin=begin, size=size):
             at = pl.ds(pl.multiple_of(block * half * rows, 16), half * rows)
             got = jnp.dot(
-                o_v[at, :deep], w_v[:, begin : begin + size], preferred_element_type=jnp.float32
+                held[at, :deep], w_v[:, begin : begin + size], preferred_element_type=jnp.float32
             )
             for k in range(half):
                 n = block * half + k
                 mine = got[k * rows : (k + 1) * rows]
                 r_v[n, :, begin : begin + size] = (
-                    b_v[n, :, begin : begin + size].astype(jnp.float32) + mine
+                    added[n, :, begin : begin + size].astype(jnp.float32) + mine
                 ).astype(r_v.dtype)
                 store(m, n, jnp.where(block == 0, spots[k], spots[half + k])).start()
             return carry
@@ -421,13 +423,15 @@
         shapes.append(jax.ShapeDtypeStruct((tokens, wide - deep), jnp.bfloat16))
     return pl.pallas_call(
         functools.partial(out_kernel, parts, turns, tags, w_tags, last),
-        in_specs=[ANY] * (1 + len(w_tags) + len(tags)),
+        in_specs=[VMEM if last else ANY]
+        + [ANY] * len(w_tags)
+        + [VMEM if last else ANY] * len(tags),
         out_specs=[ANY] * len(shapes),
         out_shape=shapes,
         scratch_shapes=[
-            pltpu.VMEM((tokens, wide), jnp.bfloat16),
+            pltpu.VMEM((16, 128) if last else (tokens, wide), jnp.bfloat16),
             pltpu.VMEM((deep, columns), jnp.bfloat16),
-            pltpu.VMEM(base.shape, base.dtype),
+            pltpu.VMEM((1, 8, 128) if last else base.shape, base.dtype),
             pltpu.VMEM(base.shape, kind),
             pltpu.SemaphoreType.DMA((len(tags),)),
             pltpu.SemaphoreType.DMA((cuts, len(w_tags))),

time: 412 us -> 411 us (level)
  no operation moved by 1% of the time
where the time goes in v3:
time: 411 us; the launch traced here: 410 us
  waiting for transfers between devices  243 us (59%)
  Pallas kernels  76.6 us (19%)
  starting transfers between devices  76.1 us (19%)
  local copies, waits for them, and re-layouts  13.4 us (3%)
    ppermute x30, waiting for transfers between devices, spread(): pieces.append((m ^ d, lax.ppermute(b, 'row', perm)))  88.7 us
    ppermute x12, waiting for transfers between devices, around(): return lax.ppermute(value, 'col', ring(images, parts, step))  83.2 us
    ppermute x10, waiting for transfers between devices, arrive(): got = lax.ppermute(value, 'col', hop(parts, moves))  71.4 us
    ppermute x30, starting transfers between devices, spread(): pieces.append((m ^ d, lax.ppermute(b, 'row', perm)))  33.1 us
    pallas_call x2, Pallas kernels, project_early(): pl.pallas_call(functools.partial(early_kernel, steps, parts, tags, first)...  23.4 us
    ppermute x12, starting transfers between devices, around(): return lax.ppermute(value, 'col', ring(images, parts, step))  17.9 us
    pallas_call x4, Pallas kernels, attend(): pl.pallas_call(functools.partial(attend_kernel, first, slots, heads), in_...  16.5 us
    pallas_call x4, Pallas kernels, normalize(): pl.pallas_call(functools.partial(norm_kernel, masks, parts), grid=(rows /...  13.7 us
  transfers between devices with their start and end apart: 69, of which 26 were waited for; matrix products, arithmetic and copies ran while one was open for 0% of the time, Pallas kernels for 18%

profile of v3, /device:TPU:0, one launch (start us, length us, event | category | flops | bytes accessed | tf_op | source)
XLA Modules:
  0.0 410.2 jit_solution(13940007905431408528)
XLA Ops:
  0.0 2.1 dynamic-slice_bitcast_fusion
  2.1 3.0 collective-permute-start.17
  5.2 1.5 collective-permute-start.18
  6.7 1.6 collective-permute-start.13
  8.3 2.6 collective-permute-start.9
  11.7 9.9 %collective-permute-done.17.refs_1_ = bf16[288,1280]{1,0:T(8,128)(2,1)S(1)} collective-permute-done((bf16[288,1280]{1,0:T(8,128)(2,1)S(1)}, bf16[288,1280]{1,0:T(8,128)(2,1)S(1)}, u32[]{:S(2)}, u32[]{:S(2)}) %collective-permute-start.17) | collective-permute-done | bytes 737312 | tf_op jit(solution)/shard_map/ppermute | solution.py:46
  21.7 1.8 collective-permute-start.41
  23.5 3.2 collective-permute-start.5
  28.7 29.3 %collective-permute-done.9.refs_0_ = bf16[288,1280]{1,0:T(8,128)(2,1)S(1)} collective-permute-done((bf16[288,1280]{1,0:T(8,128)(2,1)S(1)}, bf16[288,1280]{1,0:T(8,128)(2,1)S(1)}, u32[]{:S(2)}, u32[]{:S(2)}) %collective-permute-start.9) | collective-permute-done | bytes 737312 | tf_op jit(solution)/shard_map/ppermute | solution.py:461
  58.4 20.8 %collective-permute-done.5.refs_0_ = bf16[288,1280]{1,0:T(8,128)(2,1)S(1)} collective-permute-done((bf16[288,1280]{1,0:T(8,128)(2,1)S(1)}, bf16[288,1280]{1,0:T(8,128)(2,1)S(1)}, u32[]{:S(2)}, u32[]{:S(2)}) %collective-permute-start.5) | collective-permute-done | bytes 737312 | tf_op jit(solution)/shard_map/ppermute | solution.py:461
  83.2 16.8 %collective-permute-done.21.refs_2_ = bf16[640,768]{1,0:T(8,128)(2,1)} collective-permute-done((bf16[640,768]{1,0:T(8,128)(2,1)S(1)}, bf16[640,768]{1,0:T(8,128)(2,1)}, u32[]{:S(2)}, u32[]{:S(2)}) %collective-permute-start.21) | collective-permute-done | bytes 983072 | tf_op jit(solution)/shard_map/ppermute | solution.py:485
  100.6 1.5 collective-permute-start.6
  102.1 12.2 %collective-permute-done.14.refs_1_ = bf16[288,1280]{1,0:T(8,128)(2,1)S(1)} collective-permute-done((bf16[288,1280]{1,0:T(8,128)(2,1)S(1)}, bf16[288,1280]{1,0:T(8,128)(2,1)S(1)}, u32[]{:S(2)}, u32[]{:S(2)}) %collective-permute-start.14) | collective-permute-done | bytes 737312 | tf_op jit(solution)/shard_map/ppermute | solution.py:46
  115.5 1.3 collective-permute-start.45
  116.8 13.4 %collective-permute-done.11.refs_2_ = bf16[288,1280]{1,0:T(8,128)(2,1)S(1)} collective-permute-done((bf16[288,1280]{1,0:T(8,128)(2,1)S(1)}, bf16[288,1280]{1,0:T(8,128)(2,1)S(1)}, u32[]{:S(2)}, u32[]{:S(2)}) %collective-permute-start.11) | collective-permute-done | bytes 737312 | tf_op jit(solution)/shard_map/ppermute | solution.py:46
  130.1 14.4 %collective-permute-done.6.refs_1_ = bf16[288,1280]{1,0:T(8,128)(2,1)S(1)} collective-permute-done((bf16[288,1280]{1,0:T(8,128)(2,1)S(1)}, bf16[288,1280]{1,0:T(8,128)(2,1)S(1)}, u32[]{:S(2)}, u32[]{:S(2)}) %collective-permute-start.6) | collective-permute-done | bytes 737312 | tf_op jit(solution)/shard_map/ppermute | solution.py:46
  146.0 11.1 %collective-permute-done.45.refs_6_ = bf16[640,768]{1,0:T(8,128)(2,1)S(1)} collective-permute-done((bf16[640,768]{1,0:T(8,128)(2,1)S(1)}, bf16[640,768]{1,0:T(8,128)(2,1)S(1)}, u32[]{:S(2)}, u32[]{:S(2)}) %collective-permute-start.45) | collective-permute-done | bytes 983072 | tf_op jit(solution)/shard_map/ppermute | solution.py:485
  158.4 1.6 collective-permute-start.27
  160.0 1.3 collective-permute-start.49
  162.5 26.5 %collective-permute-done.25.refs_6_ = bf16[640,768]{1,0:T(8,128)(2,1)S(1)} collective-permute-done((bf16[640,768]{1,0:T(8,128)(2,1)S(1)}, bf16[640,768]{1,0:T(8,128)(2,1)S(1)}, u32[]{:S(2)}, u32[]{:S(2)}) %collective-permute-start.25) | collective-permute-done | bytes 983072 | tf_op jit(solution)/shard_map/ppermute | solution.py:485
  189.0 1.9 collective-permute-start.46
  191.6 1.3 collective-permute-start.29
  192.9 16.9 %collective-permute-done.49.refs_2_ = bf16[640,768]{1,0:T(8,128)(2,1)S(1)} collective-permute-done((bf16[640,768]{1,0:T(8,128)(2,1)S(1)}, bf16[640,768]{1,0:T(8,128)(2,1)S(1)}, u32[]{:S(2)}, u32[]{:S(2)}) %collective-permute-start.49) | collective-permute-done | bytes 983072 | tf_op jit(solution)/shard_map/ppermute | solution.py:485
  209.8 1.9 collective-permute-start.50
  212.4 18.4 %collective-permute-done.8.refs_3_ = bf16[288,1280]{1,0:T(8,128)(2,1)S(1)} collective-permute-done((bf16[288,1280]{1,0:T(8,128)(2,1)S(1)}, bf16[288,1280]{1,0:T(8,128)(2,1)S(1)}, u32[]{:S(2)}, u32[]{:S(2)}) %collective-permute-start.8) | collective-permute-done | bytes 737312 | tf_op jit(solution)/shard_map/ppermute | solution.py:46
  230.7 1.6 collective-permute-start.24
  232.3 2.4 collective-permute-start.26
  234.8 3.4 norm.4.refs_4_
  238.2 3.4 norm.5.refs_4_
  241.6 3.4 norm.6.refs_4_
  245.1 3.4 norm.7.x_ref
  248.5 4.3 %copy-done = bf16[4,4,288,1280]{3,2,1,0:T(8,128)(2,1)} copy-done((bf16[4,4,288,1280]{3,2,1,0:T(8,128)(2,1)}, bf16[4,4,288,1280]{3,2,1,0:T(8,128)(2,1)S(1)}, u32[]{:S(2)}) %copy-start) | copy-done | bytes 11796504
  252.8 1.6 collective-permute-start.28
  255.4 1.9 collective-permute-start.30
  257.4 12.0 %early.3.acc_ref = f32[4,288,768]{2,1,0:T(8,128)S(1)} custom-call(bf16[4,4,288,1280]{3,2,1,0:T(8,128)(2,1)} %copy-done, bf16[640,1536]{1,0:T(8,128)(2,1)S(1)} %copy-done.2, bf16[640,1536]{1,0:T(8,128)(2,1)S(1)} %collective-permute-done.20.refs_1_, bf16[640,768]{1,0:T(8,128)(2,1)S(1)} %collective-permute-done.41.refs_2_, ...), custom_call_target="tpu_custom_call" | custom-call | flops 6794772480 | bytes 8847360 | tf_op jit(solution)/shard_map/early/pallas_call | solution.py:179
  269.4 1.7 copy-done.4
  271.1 2.0 copy-done.5
  274.3 6.4 %late.3 = (bf16[1152,256]{1,0:T(8,128)(2,1)S(1)}, bf16[1152,512]{1,0:T(8,128)(2,1)}) custom-call(bf16[4,4,288,1280]{3,2,1,0:T(8,128)(2,1)S(1)} %copy-done.1, f32[4,288,768]{2,1,0:T(8,128)S(1)} %copy-done.5, bf16[640,768]{1,0:T(8,128)(2,1)S(1)} %collective-permute-done.47.refs_0_, bf16[640,768]{1,0:T(8,128)(2,1)S(1)} %collective-permute-done.48.refs_1_, ...), custom_call_target="tpu_custom_call" | custom-call | flops 2264924160 | bytes 7077888 | tf_op jit(solution)/shard_map/late/pallas_call | solution.py:248
  282.2 11.4 %early.2.acc_ref = f32[4,288,768]{2,1,0:T(8,128)S(1)} custom-call(bf16[4,4,288,1280]{3,2,1,0:T(8,128)(2,1)} %copy-done, bf16[640,1536]{1,0:T(8,128)(2,1)S(1)} %copy-done.3, bf16[640,1536]{1,0:T(8,128)(2,1)S(1)} %copy-done.7, bf16[640,768]{1,0:T(8,128)(2,1)} %collective-permute-done.21.refs_2_, bf16[640,768]{1,0:T(8,128)(2,1)} %collective-permute-done.22.refs_3_, ...), custom_call_target="tpu_custom_call" | custom-call | flops 6794772480 | bytes 8847360 | tf_op jit(solution)/shard_map/early/pallas_call | solution.py:179
  293.6 4.7 %late.2 = (bf16[1152,256]{1,0:T(8,128)(2,1)S(1)}, bf16[1152,512]{1,0:T(8,128)(2,1)S(1)}) custom-call(bf16[4,4,288,1280]{3,2,1,0:T(8,128)(2,1)S(1)} %bitcast.11, f32[4,288,768]{2,1,0:T(8,128)S(1)} %early.2.acc_ref, bf16[640,768]{1,0:T(8,128)(2,1)} %collective-permute-done.27.refs_0_, bf16[640,768]{1,0:T(8,128)(2,1)} %collective-permute-done.28.refs_1_, ...), custom_call_target="tpu_custom_call" | custom-call | flops 2264924160 | bytes 7077888 | tf_op jit(solution)/shard_map/late/pallas_call | solution.py:248
  298.6 2.1 collective-permute-done.1.refs_2_
  301.2 17.6 %collective-permute-done.3.refs_4_ = bf16[256,1280]{1,0:T(8,128)(2,1)S(1)} collective-permute-done((bf16[256,1280]{1,0:T(8,128)(2,1)S(1)}, bf16[256,1280]{1,0:T(8,128)(2,1)S(1)}, u32[]{:S(2)}, u32[]{:S(2)}) %collective-permute-start.3) | collective-permute-done | bytes 655392 | tf_op jit(solution)/shard_map/ppermute | solution.py:461
  318.8 4.7 %attend.7 = (bf16[288,256]{1,0:T(8,128)(2,1)S(1)}, bf16[288,256]{1,0:T(8,128)(2,1)S(1)}) custom-call(bf16[1152,256]{1,0:T(8,128)(2,1)S(1)} %copy-done.16, bf16[1152,512]{1,0:T(8,128)(2,1)} %get-tuple-element.26.refs_0_, bf16[1152,512]{1,0:T(8,128)(2,1)S(1)} %collective-permute-done.51.refs_1_), custom_call_target="tpu_custom_call" | custom-call | flops 2717908992 | bytes 3538944 | tf_op jit(solution)/shard_map/attend/pallas_call | solution.py:303
  323.5 4.7 %attend.6 = (bf16[288,256]{1,0:T(8,128)(2,1)S(1)}, bf16[288,256]{1,0:T(8,128)(2,1)S(1)}) custom-call(bf16[1152,256]{1,0:T(8,128)(2,1)S(1)} %copy-done.16, bf16[1152,512]{1,0:T(8,128)(2,1)} %get-tuple-element.26.refs_0_, bf16[1152,512]{1,0:T(8,128)(2,1)S(1)} %collective-permute-done.51.refs_1_), custom_call_target="tpu_custom_call" | custom-call | flops 2717908992 | bytes 3538944 | tf_op jit(solution)/shard_map/attend/pallas_call | solution.py:303
  328.8 3.4 attend.5
  333.6 2.2 collective-permute-start.37
  335.8 3.7 attend.4
  339.5 3.9 collective-permute-start.52
  343.3 7.2 %collective-permute-done.37 = bf16[288,256]{1,0:T(8,128)(2,1)S(1)} collective-permute-done((bf16[288,256]{1,0:T(8,128)(2,1)S(1)}, bf16[288,256]{1,0:T(8,128)(2,1)S(1)}, u32[]{:S(2)}, u32[]{:S(2)}) %collective-permute-start.37) | collective-permute-done | bytes 147488 | tf_op jit(solution)/shard_map/ppermute | solution.py:461
  350.5 3.3 collective-permute-start.32
  355.3 1.6 collective-permute-start.62
  359.3 3.1 collective-permute-done.56.refs_18_
  366.4 1.3 collective-permute-start.38
  367.7 1.5 collective-permute-start.34
  369.7 4.5 %collective-permute-done.57.refs_19_ = bf16[288,256]{1,0:T(8,128)(2,1)S(1)} collective-permute-done((bf16[288,256]{1,0:T(8,128)(2,1)S(1)}, bf16[288,256]{1,0:T(8,128)(2,1)S(1)}, u32[]{:S(2)}, u32[]{:S(2)}) %collective-permute-start.57) | collective-permute-done | bytes 147488 | tf_op jit(solution)/shard_map/ppermute | solution.py:46
  376.2 1.8 collective-permute-done.58.refs_20_
  378.0 1.5 collective-permute-start.59
  379.5 3.7 collective-permute-done.63.refs_25_
  386.0 1.5 collective-permute-start.40
  388.0 4.7 %collective-permute-done.39.refs_12_ = bf16[576,256]{1,0:T(8,128)(2,1)S(1)} collective-permute-done((bf16[576,256]{1,0:T(8,128)(2,1)S(1)}, bf16[576,256]{1,0:T(8,128)(2,1)S(1)}, u32[]{:S(2)}, u32[]{:S(2)}) %collective-permute-start.39) | collective-permute-done | bytes 294944 | tf_op jit(solution)/shard_map/ppermute | solution.py:46
  392.7 2.0 collective-permute-done.35.refs_8_
  395.8 2.2 collective-permute-done.36.refs_9_
  398.0 8.7 %out.2 = (f32[4,288,1280]{2,1,0:T(8,128)S(1)}, bf16[1152,512]{1,0:T(8,128)(2,1)S(1)}) custom-call(bf16[4,288,1280]{2,1,0:T(8,128)(2,1)S(1)} %copy-done.8, bf16[256,1280]{1,0:T(8,128)(2,1)} %refs_0_.5, bf16[256,1280]{1,0:T(8,128)(2,1)S(1)} %collective-permute-done.refs_1_, bf16[256,1280]{1,0:T(8,128)(2,1)S(1)} %collective-permute-done.1.refs_2_, ...), custom_call_target="tpu_custom_call" | custom-call | flops 4529848320 | bytes 11796480 | tf_op jit(solution)/shard_map/out/pallas_call | solution.py:424
  406.8 3.2 out.3
  (135 shorter events, 35.5 us)
Async XLA Ops:
  2.1 19.5 %collective-permute-start.17 = (bf16[288,1280]{1,0:T(8,128)(2,1)S(1)}, bf16[288,1280]{1,0:T(8,128)(2,1)S(1)}, u32[]{:S(2)}, u32[]{:S(2)}) collective-permute-start(bf16[288,1280]{1,0:T(8,128)(2,1)S(1)} %get-tuple-element.33.refs_0_), channel_id=1, source_target_pairs={{0,8},{8,0},{16,24},{24,16},{1,9},{9,1},{17,25},{25,17},{2,10},{10... | collective-permute-start | bytes 2211848 | tf_op jit(solution)/shard_map/ppermute | solution.py:46
  5.2 18.3 %collective-permute-start.18 = (bf16[288,1280]{1,0:T(8,128)(2,1)S(1)}, bf16[288,1280]{1,0:T(8,128)(2,1)S(1)}, u32[]{:S(2)}, u32[]{:S(2)}) collective-permute-start(bf16[288,1280]{1,0:T(8,128)(2,1)S(1)} %get-tuple-element.33.refs_0_), channel_id=1, source_target_pairs={{0,16},{8,24},{16,0},{24,8},{1,17},{9,25},{17,1},{25,9},{2,18},{10... | collective-permute-start | bytes 2211848 | tf_op jit(solution)/shard_map/ppermute | solution.py:46
  6.7 21.3 %collective-permute-start.13 = (bf16[288,1280]{1,0:T(8,128)(2,1)S(1)}, bf16[288,1280]{1,0:T(8,128)(2,1)S(1)}, u32[]{:S(2)}, u32[]{:S(2)}) collective-permute-start(bf16[288,1280]{1,0:T(8,128)(2,1)S(1)} %get-tuple-element.34), channel_id=1, source_target_pairs={{0,2},{1,3},{2,4},{3,5},{4,6},{5,7},{6,0},{7,1},{8,10},{9,11},{10,... | collective-permute-start | bytes 2211848 | tf_op jit(solution)/shard_map/ppermute | solution.py:461
  8.3 49.7 %collective-permute-start.9 = (bf16[288,1280]{1,0:T(8,128)(2,1)S(1)}, bf16[288,1280]{1,0:T(8,128)(2,1)S(1)}, u32[]{:S(2)}, u32[]{:S(2)}) collective-permute-start(bf16[288,1280]{1,0:T(8,128)(2,1)S(1)} %get-tuple-element.35), channel_id=1, source_target_pairs={{0,4},{1,5},{2,6},{3,7},{4,0},{5,1},{6,2},{7,3},{8,12},{9,13},{10,... | collective-permute-start | bytes 2211848 | tf_op jit(solution)/shard_map/ppermute | solution.py:461
  11.0 69.3 %collective-permute-start.43 = (bf16[640,768]{1,0:T(8,128)(2,1)S(1)}, bf16[640,768]{1,0:T(8,128)(2,1)S(1)}, u32[]{:S(2)}, u32[]{:S(2)}) collective-permute-start(bf16[640,768]{1,0:T(8,128)(2,1)S(1)} %get-tuple-element.37), channel_id=1, source_target_pairs={{2,4},{3,5},{4,2},{5,3},{10,12},{11,13},{12,10},{13,11},{18,20},{1... | collective-permute-start | bytes 2949128 | tf_op jit(solution)/shard_map/ppermute | solution.py:485
  21.7 59.5 %collective-permute-start.41 = (bf16[640,768]{1,0:T(8,128)(2,1)S(1)}, bf16[640,768]{1,0:T(8,128)(2,1)S(1)}, u32[]{:S(2)}, u32[]{:S(2)}) collective-permute-start(bf16[640,768]{1,0:T(8,128)(2,1)S(1)} %get-tuple-element.37), channel_id=1, source_target_pairs={{0,2},{1,3},{2,0},{3,1},{4,6},{5,7},{6,4},{7,5},{8,10},{9,11},{10,... | collective-permute-start | bytes 2949128 | tf_op jit(solution)/shard_map/ppermute | solution.py:485
  23.5 55.7 %collective-permute-start.5 = (bf16[288,1280]{1,0:T(8,128)(2,1)S(1)}, bf16[288,1280]{1,0:T(8,128)(2,1)S(1)}, u32[]{:S(2)}, u32[]{:S(2)}) collective-permute-start(bf16[288,1280]{1,0:T(8,128)(2,1)S(1)} %get-tuple-element.36), channel_id=1, source_target_pairs={{0,6},{1,7},{2,0},{3,1},{4,2},{5,3},{6,4},{7,5},{8,14},{9,15},{10,... | collective-permute-start | bytes 2211848 | tf_op jit(solution)/shard_map/ppermute | solution.py:461
  28.0 54.4 %collective-permute-start.23 = (bf16[640,768]{1,0:T(8,128)(2,1)S(1)}, bf16[640,768]{1,0:T(8,128)(2,1)S(1)}, u32[]{:S(2)}, u32[]{:S(2)}) collective-permute-start(bf16[640,768]{1,0:T(8,128)(2,1)S(1)} %get-tuple-element.38), channel_id=1, source_target_pairs={{2,4},{3,5},{4,2},{5,3},{10,12},{11,13},{12,10},{13,11},{18,20},{1... | collective-permute-start | bytes 2949128 | tf_op jit(solution)/shard_map/ppermute | solution.py:485
  58.0 42.1 %collective-permute-start.21 = (bf16[640,768]{1,0:T(8,128)(2,1)S(1)}, bf16[640,768]{1,0:T(8,128)(2,1)}, u32[]{:S(2)}, u32[]{:S(2)}) collective-permute-start(bf16[640,768]{1,0:T(8,128)(2,1)S(1)} %get-tuple-element.38), channel_id=1, source_target_pairs={{0,2},{1,3},{2,0},{3,1},{4,6},{5,7},{6,4},{7,5},{8,10},{9,11},{10,... | collective-permute-start | bytes 2949128 | tf_op jit(solution)/shard_map/ppermute | solution.py:485
  79.2 21.4 %collective-permute-start.19 = (bf16[288,1280]{1,0:T(8,128)(2,1)S(1)}, bf16[288,1280]{1,0:T(8,128)(2,1)S(1)}, u32[]{:S(2)}, u32[]{:S(2)}) collective-permute-start(bf16[288,1280]{1,0:T(8,128)(2,1)S(1)} %collective-permute-done.17.refs_1_), channel_id=1, source_target_pairs={{0,16},{8,24},{16,0},{24,8},{1,17},{9,25},{17,1},{25,9},{2,18},{10... | collective-permute-start | bytes 2211848 | tf_op jit(solution)/shard_map/ppermute | solution.py:46
  80.3 34.0 %collective-permute-start.14 = (bf16[288,1280]{1,0:T(8,128)(2,1)S(1)}, bf16[288,1280]{1,0:T(8,128)(2,1)S(1)}, u32[]{:S(2)}, u32[]{:S(2)}) collective-permute-start(bf16[288,1280]{1,0:T(8,128)(2,1)S(1)} %collective-permute-done.13.refs_0_), channel_id=1, source_target_pairs={{0,16},{8,24},{16,0},{24,8},{1,17},{9,25},{17,1},{25,9},{2,18},{10... | collective-permute-start | bytes 2211848 | tf_op jit(solution)/shard_map/ppermute | solution.py:46
  81.2 33.1 %collective-permute-start.15 = (bf16[288,1280]{1,0:T(8,128)(2,1)S(1)}, bf16[288,1280]{1,0:T(8,128)(2,1)S(1)}, u32[]{:S(2)}, u32[]{:S(2)}) collective-permute-start(bf16[288,1280]{1,0:T(8,128)(2,1)S(1)} %collective-permute-done.13.refs_0_), channel_id=1, source_target_pairs={{0,8},{8,0},{16,24},{24,16},{1,9},{9,1},{17,25},{25,17},{2,10},{10... | collective-permute-start | bytes 2211848 | tf_op jit(solution)/shard_map/ppermute | solution.py:46
  82.3 33.1 %collective-permute-start.10 = (bf16[288,1280]{1,0:T(8,128)(2,1)S(1)}, bf16[288,1280]{1,0:T(8,128)(2,1)S(1)}, u32[]{:S(2)}, u32[]{:S(2)}) collective-permute-start(bf16[288,1280]{1,0:T(8,128)(2,1)S(1)} %collective-permute-done.9.refs_0_), channel_id=1, source_target_pairs={{0,8},{8,0},{16,24},{24,16},{1,9},{9,1},{17,25},{25,17},{2,10},{10... | collective-permute-start | bytes 2211848 | tf_op jit(solution)/shard_map/ppermute | solution.py:46
  100.1 30.1 %collective-permute-start.11 = (bf16[288,1280]{1,0:T(8,128)(2,1)S(1)}, bf16[288,1280]{1,0:T(8,128)(2,1)S(1)}, u32[]{:S(2)}, u32[]{:S(2)}) collective-permute-start(bf16[288,1280]{1,0:T(8,128)(2,1)S(1)} %collective-permute-done.9.refs_0_), channel_id=1, source_target_pairs={{0,16},{8,24},{16,0},{24,8},{1,17},{9,25},{17,1},{25,9},{2,18},{10... | collective-permute-start | bytes 2211848 | tf_op jit(solution)/shard_map/ppermute | solution.py:46
  100.6 44.0 %collective-permute-start.6 = (bf16[288,1280]{1,0:T(8,128)(2,1)S(1)}, bf16[288,1280]{1,0:T(8,128)(2,1)S(1)}, u32[]{:S(2)}, u32[]{:S(2)}) collective-permute-start(bf16[288,1280]{1,0:T(8,128)(2,1)S(1)} %collective-permute-done.5.refs_0_), channel_id=1, source_target_pairs={{0,16},{8,24},{16,0},{24,8},{1,17},{9,25},{17,1},{25,9},{2,18},{10... | collective-permute-start | bytes 2211848 | tf_op jit(solution)/shard_map/ppermute | solution.py:46
  114.3 47.6 %collective-permute-start.20 = (bf16[640,1536]{1,0:T(8,128)(2,1)S(1)}, bf16[640,1536]{1,0:T(8,128)(2,1)S(1)}, u32[]{:S(2)}, u32[]{:S(2)}) collective-permute-start(bf16[640,1536]{1,0:T(8,128)(2,1)S(1)} %copy-done.2), channel_id=1, source_target_pairs={{0,1},{1,0},{2,3},{3,2},{4,5},{5,4},{6,7},{7,6},{8,9},{9,8},{10,11... | collective-permute-start | bytes 5898248 | tf_op jit(solution)/shard_map/ppermute | solution.py:465
  114.3 30.9 %collective-permute-start.7 = (bf16[288,1280]{1,0:T(8,128)(2,1)S(1)}, bf16[288,1280]{1,0:T(8,128)(2,1)S(1)}, u32[]{:S(2)}, u32[]{:S(2)}) collective-permute-start(bf16[288,1280]{1,0:T(8,128)(2,1)S(1)} %collective-permute-done.5.refs_0_), channel_id=1, source_target_pairs={{0,8},{8,0},{16,24},{24,16},{1,9},{9,1},{17,25},{25,17},{2,10},{10... | collective-permute-start | bytes 2211848 | tf_op jit(solution)/shard_map/ppermute | solution.py:46
  115.5 41.7 %collective-permute-start.45 = (bf16[640,768]{1,0:T(8,128)(2,1)S(1)}, bf16[640,768]{1,0:T(8,128)(2,1)S(1)}, u32[]{:S(2)}, u32[]{:S(2)}) collective-permute-start(bf16[640,768]{1,0:T(8,128)(2,1)S(1)} %collective-permute-done.43.refs_4_), channel_id=1, source_target_pairs={{2,0},{3,1},{4,6},{5,7},{10,8},{11,9},{12,14},{13,15},{18,16},{19,... | collective-permute-start | bytes 2949128 | tf_op jit(solution)/shard_map/ppermute | solution.py:485
  130.1 28.3 %collective-permute-start.42 = (bf16[640,768]{1,0:T(8,128)(2,1)S(1)}, bf16[640,768]{1,0:T(8,128)(2,1)S(1)}, u32[]{:S(2)}, u32[]{:S(2)}) collective-permute-start(bf16[640,768]{1,0:T(8,128)(2,1)S(1)} %collective-permute-done.41.refs_2_), channel_id=1, source_target_pairs={{0,1},{1,0},{2,3},{3,2},{4,5},{5,4},{6,7},{7,6},{8,9},{9,8},{10,11... | collective-permute-start | bytes 2949128 | tf_op jit(solution)/shard_map/ppermute | solution.py:492
  144.5 15.5 %collective-permute-start.47 = (bf16[640,768]{1,0:T(8,128)(2,1)S(1)}, bf16[640,768]{1,0:T(8,128)(2,1)S(1)}, u32[]{:S(2)}, u32[]{:S(2)}) collective-permute-start(bf16[640,768]{1,0:T(8,128)(2,1)S(1)} %collective-permute-done.41.refs_2_), channel_id=1, source_target_pairs={{2,4},{3,5},{4,2},{5,3},{10,12},{11,13},{12,10},{13,11},{18,20},{1... | collective-permute-start | bytes 2949128 | tf_op jit(solution)/shard_map/ppermute | solution.py:485
  145.3 16.1 %collective-permute-start.44 = (bf16[640,768]{1,0:T(8,128)(2,1)S(1)}, bf16[640,768]{1,0:T(8,128)(2,1)S(1)}, u32[]{:S(2)}, u32[]{:S(2)}) collective-permute-start(bf16[640,768]{1,0:T(8,128)(2,1)S(1)} %collective-permute-done.43.refs_4_), channel_id=1, source_target_pairs={{2,3},{3,2},{4,5},{5,4},{10,11},{11,10},{12,13},{13,12},{18,19},{1... | collective-permute-start | bytes 2949128 | tf_op jit(solution)/shard_map/ppermute | solution.py:492
  157.1 31.8 %collective-permute-start.25 = (bf16[640,768]{1,0:T(8,128)(2,1)S(1)}, bf16[640,768]{1,0:T(8,128)(2,1)S(1)}, u32[]{:S(2)}, u32[]{:S(2)}) collective-permute-start(bf16[640,768]{1,0:T(8,128)(2,1)S(1)} %collective-permute-done.23.refs_4_), channel_id=1, source_target_pairs={{2,0},{3,1},{4,6},{5,7},{10,8},{11,9},{12,14},{13,15},{18,16},{19,... | collective-permute-start | bytes 2949128 | tf_op jit(solution)/shard_map/ppermute | solution.py:485
  158.4 32.5 %collective-permute-start.27 = (bf16[640,768]{1,0:T(8,128)(2,1)}, bf16[640,768]{1,0:T(8,128)(2,1)}, u32[]{:S(2)}, u32[]{:S(2)}) collective-permute-start(bf16[640,768]{1,0:T(8,128)(2,1)} %collective-permute-done.21.refs_2_), channel_id=1, source_target_pairs={{2,4},{3,5},{4,2},{5,3},{10,12},{11,13},{12,10},{13,11},{18,20},{1... | collective-permute-start | bytes 2949128 | tf_op jit(solution)/shard_map/ppermute | solution.py:485
  160.0 49.8 %collective-permute-start.49 = (bf16[640,768]{1,0:T(8,128)(2,1)S(1)}, bf16[640,768]{1,0:T(8,128)(2,1)S(1)}, u32[]{:S(2)}, u32[]{:S(2)}) collective-permute-start(bf16[640,768]{1,0:T(8,128)(2,1)S(1)} %collective-permute-done.47.refs_0_), channel_id=1, source_target_pairs={{2,0},{3,1},{4,6},{5,7},{10,8},{11,9},{12,14},{13,15},{18,16},{19,... | collective-permute-start | bytes 2949128 | tf_op jit(solution)/shard_map/ppermute | solution.py:485
  161.3 30.3 %collective-permute-start.16 = (bf16[288,1280]{1,0:T(8,128)(2,1)S(1)}, bf16[288,1280]{1,0:T(8,128)(2,1)S(1)}, u32[]{:S(2)}, u32[]{:S(2)}) collective-permute-start(bf16[288,1280]{1,0:T(8,128)(2,1)S(1)} %collective-permute-done.14.refs_1_), channel_id=1, source_target_pairs={{0,8},{8,0},{16,24},{24,16},{1,9},{9,1},{17,25},{25,17},{2,10},{10... | collective-permute-start | bytes 2211848 | tf_op jit(solution)/shard_map/ppermute | solution.py:46
  162.0 49.8 %collective-permute-start.12 = (bf16[288,1280]{1,0:T(8,128)(2,1)S(1)}, bf16[288,1280]{1,0:T(8,128)(2,1)S(1)}, u32[]{:S(2)}, u32[]{:S(2)}) collective-permute-start(bf16[288,1280]{1,0:T(8,128)(2,1)S(1)} %collective-permute-done.10.refs_1_), channel_id=1, source_target_pairs={{0,16},{8,24},{16,0},{24,8},{1,17},{9,25},{17,1},{25,9},{2,18},{10... | collective-permute-start | bytes 2211848 | tf_op jit(solution)/shard_map/ppermute | solution.py:46
  189.0 41.8 %collective-permute-start.46 = (bf16[640,768]{1,0:T(8,128)(2,1)S(1)}, bf16[640,768]{1,0:T(8,128)(2,1)S(1)}, u32[]{:S(2)}, u32[]{:S(2)}) collective-permute-start(bf16[640,768]{1,0:T(8,128)(2,1)S(1)} %collective-permute-done.45.refs_6_), channel_id=1, source_target_pairs={{0,1},{1,0},{6,7},{7,6},{8,9},{9,8},{14,15},{15,14},{16,17},{17,16... | collective-permute-start | bytes 2949128 | tf_op jit(solution)/shard_map/ppermute | solution.py:492
  190.9 41.4 %collective-permute-start.48 = (bf16[640,768]{1,0:T(8,128)(2,1)S(1)}, bf16[640,768]{1,0:T(8,128)(2,1)S(1)}, u32[]{:S(2)}, u32[]{:S(2)}) collective-permute-start(bf16[640,768]{1,0:T(8,128)(2,1)S(1)} %collective-permute-done.47.refs_0_), channel_id=1, source_target_pairs={{2,3},{3,2},{4,5},{5,4},{10,11},{11,10},{12,13},{13,12},{18,19},{1... | collective-permute-start | bytes 2949128 | tf_op jit(solution)/shard_map/ppermute | solution.py:492
  191.6 61.2 %collective-permute-start.29 = (bf16[640,768]{1,0:T(8,128)(2,1)}, bf16[640,768]{1,0:T(8,128)(2,1)}, u32[]{:S(2)}, u32[]{:S(2)}) collective-permute-start(bf16[640,768]{1,0:T(8,128)(2,1)} %collective-permute-done.27.refs_0_), channel_id=1, source_target_pairs={{2,0},{3,1},{4,6},{5,7},{10,8},{11,9},{12,14},{13,15},{18,16},{19,... | collective-permute-start | bytes 2949128 | tf_op jit(solution)/shard_map/ppermute | solution.py:485
  209.8 44.6 %collective-permute-start.50 = (bf16[640,768]{1,0:T(8,128)(2,1)S(1)}, bf16[640,768]{1,0:T(8,128)(2,1)S(1)}, u32[]{:S(2)}, u32[]{:S(2)}) collective-permute-start(bf16[640,768]{1,0:T(8,128)(2,1)S(1)} %collective-permute-done.49.refs_2_), channel_id=1, source_target_pairs={{0,1},{1,0},{6,7},{7,6},{8,9},{9,8},{14,15},{15,14},{16,17},{17,16... | collective-permute-start | bytes 2949128 | tf_op jit(solution)/shard_map/ppermute | solution.py:492
  211.8 19.0 %collective-permute-start.8 = (bf16[288,1280]{1,0:T(8,128)(2,1)S(1)}, bf16[288,1280]{1,0:T(8,128)(2,1)S(1)}, u32[]{:S(2)}, u32[]{:S(2)}) collective-permute-start(bf16[288,1280]{1,0:T(8,128)(2,1)S(1)} %collective-permute-done.6.refs_1_), channel_id=1, source_target_pairs={{0,8},{8,0},{16,24},{24,16},{1,9},{9,1},{17,25},{25,17},{2,10},{10... | collective-permute-start | bytes 2211848 | tf_op jit(solution)/shard_map/ppermute | solution.py:46
  230.7 50.8 %collective-permute-start.22 = (bf16[640,768]{1,0:T(8,128)(2,1)}, bf16[640,768]{1,0:T(8,128)(2,1)}, u32[]{:S(2)}, u32[]{:S(2)}) collective-permute-start(bf16[640,768]{1,0:T(8,128)(2,1)} %collective-permute-done.21.refs_2_), channel_id=1, source_target_pairs={{0,1},{1,0},{2,3},{3,2},{4,5},{5,4},{6,7},{7,6},{8,9},{9,8},{10,11... | collective-permute-start | bytes 2949128 | tf_op jit(solution)/shard_map/ppermute | solution.py:492
  230.7 51.1 %collective-permute-start.24 = (bf16[640,768]{1,0:T(8,128)(2,1)S(1)}, bf16[640,768]{1,0:T(8,128)(2,1)}, u32[]{:S(2)}, u32[]{:S(2)}) collective-permute-start(bf16[640,768]{1,0:T(8,128)(2,1)S(1)} %collective-permute-done.23.refs_4_), channel_id=1, source_target_pairs={{2,3},{3,2},{4,5},{5,4},{10,11},{11,10},{12,13},{13,12},{18,19},{1... | collective-permute-start | bytes 2949128 | tf_op jit(solution)/shard_map/ppermute | solution.py:492
  232.3 49.8 %collective-permute-start.26 = (bf16[640,768]{1,0:T(8,128)(2,1)S(1)}, bf16[640,768]{1,0:T(8,128)(2,1)}, u32[]{:S(2)}, u32[]{:S(2)}) collective-permute-start(bf16[640,768]{1,0:T(8,128)(2,1)S(1)} %collective-permute-done.25.refs_6_), channel_id=1, source_target_pairs={{0,1},{1,0},{6,7},{7,6},{8,9},{9,8},{14,15},{15,14},{16,17},{17,16... | collective-permute-start | bytes 2949128 | tf_op jit(solution)/shard_map/ppermute | solution.py:492
  252.8 40.8 %collective-permute-start.28 = (bf16[640,768]{1,0:T(8,128)(2,1)}, bf16[640,768]{1,0:T(8,128)(2,1)}, u32[]{:S(2)}, u32[]{:S(2)}) collective-permute-start(bf16[640,768]{1,0:T(8,128)(2,1)} %collective-permute-done.27.refs_0_), channel_id=1, source_target_pairs={{2,3},{3,2},{4,5},{5,4},{10,11},{11,10},{12,13},{13,12},{18,19},{1... | collective-permute-start | bytes 2949128 | tf_op jit(solution)/shard_map/ppermute | solution.py:492
  255.4 38.2 %collective-permute-start.30 = (bf16[640,768]{1,0:T(8,128)(2,1)}, bf16[640,768]{1,0:T(8,128)(2,1)}, u32[]{:S(2)}, u32[]{:S(2)}) collective-permute-start(bf16[640,768]{1,0:T(8,128)(2,1)} %collective-permute-done.29.refs_2_), channel_id=1, source_target_pairs={{0,1},{1,0},{6,7},{7,6},{8,9},{9,8},{14,15},{15,14},{16,17},{17,16... | collective-permute-start | bytes 2949128 | tf_op jit(solution)/shard_map/ppermute | solution.py:492
  281.6 19.1 %collective-permute-start.1 = (bf16[256,1280]{1,0:T(8,128)(2,1)}, bf16[256,1280]{1,0:T(8,128)(2,1)S(1)}, u32[]{:S(2)}, u32[]{:S(2)}) collective-permute-start(bf16[256,1280]{1,0:T(8,128)(2,1)} %refs_0_.5), channel_id=1, source_target_pairs={{0,2},{1,3},{2,4},{3,5},{4,6},{5,7},{6,0},{7,1},{8,10},{9,11},{10,... | collective-permute-start | bytes 1966088 | tf_op jit(solution)/shard_map/ppermute | solution.py:461
  281.8 36.9 %collective-permute-start.51 = (bf16[1152,512]{1,0:T(8,128)(2,1)}, bf16[1152,512]{1,0:T(8,128)(2,1)S(1)}, u32[]{:S(2)}, u32[]{:S(2)}) collective-permute-start(bf16[1152,512]{1,0:T(8,128)(2,1)} %get-tuple-element.26.refs_0_), channel_id=1, source_target_pairs={{0,1},{1,0},{2,3},{3,2},{4,5},{5,4},{6,7},{7,6},{8,9},{9,8},{10,11... | collective-permute-start | bytes 3538952 | tf_op jit(solution)/shard_map/ppermute | solution.py:507
  298.3 29.9 %collective-permute-start.31 = (bf16[1152,512]{1,0:T(8,128)(2,1)S(1)}, bf16[1152,512]{1,0:T(8,128)(2,1)S(1)}, u32[]{:S(2)}, u32[]{:S(2)}) collective-permute-start(bf16[1152,512]{1,0:T(8,128)(2,1)S(1)} %get-tuple-element.20.refs_0_), channel_id=1, source_target_pairs={{0,1},{1,0},{2,3},{3,2},{4,5},{5,4},{6,7},{7,6},{8,9},{9,8},{10,11... | collective-permute-start | bytes 3538952 | tf_op jit(solution)/shard_map/ppermute | solution.py:507
  300.7 18.1 %collective-permute-start.3 = (bf16[256,1280]{1,0:T(8,128)(2,1)S(1)}, bf16[256,1280]{1,0:T(8,128)(2,1)S(1)}, u32[]{:S(2)}, u32[]{:S(2)}) collective-permute-start(bf16[256,1280]{1,0:T(8,128)(2,1)S(1)} %collective-permute-done.1.refs_2_), channel_id=1, source_target_pairs={{0,2},{1,3},{2,4},{3,5},{4,6},{5,7},{6,0},{7,1},{8,10},{9,11},{10,... | collective-permute-start | bytes 1966088 | tf_op jit(solution)/shard_map/ppermute | solution.py:461
  300.7 31.6 %collective-permute-start = (bf16[256,1280]{1,0:T(8,128)(2,1)}, bf16[256,1280]{1,0:T(8,128)(2,1)S(1)}, u32[]{:S(2)}, u32[]{:S(2)}) collective-permute-start(bf16[256,1280]{1,0:T(8,128)(2,1)} %refs_0_.5), channel_id=1, source_target_pairs={{0,1},{1,0},{2,3},{3,2},{4,5},{5,4},{6,7},{7,6},{8,9},{9,8},{10,11... | collective-permute-start | bytes 1966088 | tf_op jit(solution)/shard_map/ppermute | solution.py:465
  300.7 32.2 %collective-permute-start.2 = (bf16[256,1280]{1,0:T(8,128)(2,1)S(1)}, bf16[256,1280]{1,0:T(8,128)(2,1)S(1)}, u32[]{:S(2)}, u32[]{:S(2)}) collective-permute-start(bf16[256,1280]{1,0:T(8,128)(2,1)S(1)} %collective-permute-done.1.refs_2_), channel_id=1, source_target_pairs={{0,1},{1,0},{2,3},{3,2},{4,5},{5,4},{6,7},{7,6},{8,9},{9,8},{10,11... | collective-permute-start | bytes 1966088 | tf_op jit(solution)/shard_map/ppermute | solution.py:465
  318.8 14.9 %collective-permute-start.4 = (bf16[256,1280]{1,0:T(8,128)(2,1)S(1)}, bf16[256,1280]{1,0:T(8,128)(2,1)S(1)}, u32[]{:S(2)}, u32[]{:S(2)}) collective-permute-start(bf16[256,1280]{1,0:T(8,128)(2,1)S(1)} %collective-permute-done.3.refs_4_), channel_id=1, source_target_pairs={{0,1},{1,0},{2,3},{3,2},{4,5},{5,4},{6,7},{7,6},{8,9},{9,8},{10,11... | collective-permute-start | bytes 1966088 | tf_op jit(solution)/shard_map/ppermute | solution.py:465
  318.8 20.7 %collective-permute-start.67 = (bf16[256,1280]{1,0:T(8,128)(2,1)S(1)}, bf16[256,1280]{1,0:T(8,128)(2,1)S(1)}, u32[]{:S(2)}, u32[]{:S(2)}) collective-permute-start(bf16[256,1280]{1,0:T(8,128)(2,1)S(1)} %collective-permute-done.3.refs_4_), channel_id=1, source_target_pairs={{0,2},{1,3},{2,4},{3,5},{4,6},{5,7},{6,0},{7,1},{8,10},{9,11},{10,... | collective-permute-start | bytes 1966088 | tf_op jit(solution)/shard_map/ppermute | solution.py:461
  328.2 25.7 %collective-permute-start.64 = (bf16[288,256]{1,0:T(8,128)(2,1)S(1)}, bf16[288,256]{1,0:T(8,128)(2,1)S(1)}, u32[]{:S(2)}, u32[]{:S(2)}) collective-permute-start(bf16[288,256]{1,0:T(8,128)(2,1)S(1)} %get-tuple-element.30.refs_26_), channel_id=1, source_target_pairs={{0,16},{8,24},{16,0},{24,8},{1,17},{9,25},{17,1},{25,9},{2,18},{10... | collective-permute-start | bytes 442376 | tf_op jit(solution)/shard_map/ppermute | solution.py:46
  332.3 21.7 %collective-permute-start.65 = (bf16[288,256]{1,0:T(8,128)(2,1)S(1)}, bf16[288,256]{1,0:T(8,128)(2,1)S(1)}, u32[]{:S(2)}, u32[]{:S(2)}) collective-permute-start(bf16[288,256]{1,0:T(8,128)(2,1)S(1)} %get-tuple-element.30.refs_26_), channel_id=1, source_target_pairs={{0,8},{8,0},{16,24},{24,16},{1,9},{9,1},{17,25},{25,17},{2,10},{10... | collective-permute-start | bytes 442376 | tf_op jit(solution)/shard_map/ppermute | solution.py:46
  332.9 21.0 %collective-permute-start.60 = (bf16[288,256]{1,0:T(8,128)(2,1)S(1)}, bf16[288,256]{1,0:T(8,128)(2,1)S(1)}, u32[]{:S(2)}, u32[]{:S(2)}) collective-permute-start(bf16[288,256]{1,0:T(8,128)(2,1)S(1)} %get-tuple-element.29), channel_id=1, source_target_pairs={{0,4},{1,5},{2,6},{3,7},{4,0},{5,1},{6,2},{7,3},{8,12},{9,13},{10,... | collective-permute-start | bytes 442376 | tf_op jit(solution)/shard_map/ppermute | solution.py:461
  333.6 16.9 %collective-permute-start.37 = (bf16[288,256]{1,0:T(8,128)(2,1)S(1)}, bf16[288,256]{1,0:T(8,128)(2,1)S(1)}, u32[]{:S(2)}, u32[]{:S(2)}) collective-permute-start(bf16[288,256]{1,0:T(8,128)(2,1)S(1)} %get-tuple-element.23), channel_id=1, source_target_pairs={{0,4},{1,5},{2,6},{3,7},{4,0},{5,1},{6,2},{7,3},{8,12},{9,13},{10,... | collective-permute-start | bytes 442376 | tf_op jit(solution)/shard_map/ppermute | solution.py:461
  339.5 15.8 %collective-permute-start.52 = (bf16[288,256]{1,0:T(8,128)(2,1)S(1)}, bf16[288,256]{1,0:T(8,128)(2,1)S(1)}, u32[]{:S(2)}, u32[]{:S(2)}) collective-permute-start(bf16[288,256]{1,0:T(8,128)(2,1)S(1)} %get-tuple-element.27), channel_id=1, source_target_pairs={{0,6},{1,7},{2,0},{3,1},{4,2},{5,3},{6,4},{7,5},{8,14},{9,15},{10,... | collective-permute-start | bytes 442376 | tf_op jit(solution)/shard_map/ppermute | solution.py:461
  353.9 10.4 %collective-permute-start.33 = (bf16[288,256]{1,0:T(8,128)(2,1)S(1)}, bf16[288,256]{1,0:T(8,128)(2,1)S(1)}, u32[]{:S(2)}, u32[]{:S(2)}) collective-permute-start(bf16[288,256]{1,0:T(8,128)(2,1)S(1)} %get-tuple-element.22), channel_id=1, source_target_pairs={{0,2},{1,3},{2,4},{3,5},{4,6},{5,7},{6,0},{7,1},{8,10},{9,11},{10,... | collective-permute-start | bytes 442376 | tf_op jit(solution)/shard_map/ppermute | solution.py:461
  354.0 11.6 %collective-permute-start.61 = (bf16[288,256]{1,0:T(8,128)(2,1)S(1)}, bf16[288,256]{1,0:T(8,128)(2,1)S(1)}, u32[]{:S(2)}, u32[]{:S(2)}) collective-permute-start(bf16[288,256]{1,0:T(8,128)(2,1)S(1)} %collective-permute-done.60.refs_22_), channel_id=1, source_target_pairs={{0,8},{8,0},{16,24},{24,16},{1,9},{9,1},{17,25},{25,17},{2,10},{10... | collective-permute-start | bytes 442376 | tf_op jit(solution)/shard_map/ppermute | solution.py:46
  355.3 11.1 %collective-permute-start.62 = (bf16[288,256]{1,0:T(8,128)(2,1)S(1)}, bf16[288,256]{1,0:T(8,128)(2,1)S(1)}, u32[]{:S(2)}, u32[]{:S(2)}) collective-permute-start(bf16[288,256]{1,0:T(8,128)(2,1)S(1)} %collective-permute-done.60.refs_22_), channel_id=1, source_target_pairs={{0,16},{8,24},{16,0},{24,8},{1,17},{9,25},{17,1},{25,9},{2,18},{10... | collective-permute-start | bytes 442376 | tf_op jit(solution)/shard_map/ppermute | solution.py:46
  358.1 9.6 %collective-permute-start.66 = (bf16[288,256]{1,0:T(8,128)(2,1)S(1)}, bf16[288,256]{1,0:T(8,128)(2,1)S(1)}, u32[]{:S(2)}, u32[]{:S(2)}) collective-permute-start(bf16[288,256]{1,0:T(8,128)(2,1)S(1)} %collective-permute-done.64.refs_27_), channel_id=1, source_target_pairs={{0,8},{8,0},{16,24},{24,16},{1,9},{9,1},{17,25},{25,17},{2,10},{10... | collective-permute-start | bytes 442376 | tf_op jit(solution)/shard_map/ppermute | solution.py:46
  364.3 11.1 %collective-permute-start.54 = (bf16[288,256]{1,0:T(8,128)(2,1)S(1)}, bf16[288,256]{1,0:T(8,128)(2,1)S(1)}, u32[]{:S(2)}, u32[]{:S(2)}) collective-permute-start(bf16[288,256]{1,0:T(8,128)(2,1)S(1)} %collective-permute-done.52.refs_14_), channel_id=1, source_target_pairs={{0,16},{8,24},{16,0},{24,8},{1,17},{9,25},{17,1},{25,9},{2,18},{10... | collective-permute-start | bytes 442376 | tf_op jit(solution)/shard_map/ppermute | solution.py:46
  366.4 19.6 %collective-permute-start.38 = (bf16[576,256]{1,0:T(8,128)(2,1)S(1)}, bf16[576,256]{1,0:T(8,128)(2,1)S(1)}, u32[]{:S(2)}, u32[]{:S(2)}) collective-permute-start(bf16[576,256]{1,0:T(8,128)(2,1)S(1)} %constant_dynamic-update-slice_fusion.2.refs_10_), channel_id=1, source_target_pairs={{0,16},{8,24},{16,0},{24,8},{1,17},{9,25},{17,1},{25,9},{2,18},{10... | collective-permute-start | bytes 884744 | tf_op jit(solution)/shard_map/ppermute | solution.py:46
  367.7 19.8 %collective-permute-start.34 = (bf16[576,256]{1,0:T(8,128)(2,1)S(1)}, bf16[576,256]{1,0:T(8,128)(2,1)S(1)}, u32[]{:S(2)}, u32[]{:S(2)}) collective-permute-start(bf16[576,256]{1,0:T(8,128)(2,1)S(1)} %constant_dynamic-update-slice_fusion.refs_6_), channel_id=1, source_target_pairs={{0,8},{8,0},{16,24},{24,16},{1,9},{9,1},{17,25},{25,17},{2,10},{10... | collective-permute-start | bytes 884744 | tf_op jit(solution)/shard_map/ppermute | solution.py:46
  374.2 9.0 %collective-permute-start.63 = (bf16[288,256]{1,0:T(8,128)(2,1)S(1)}, bf16[288,256]{1,0:T(8,128)(2,1)S(1)}, u32[]{:S(2)}, u32[]{:S(2)}) collective-permute-start(bf16[288,256]{1,0:T(8,128)(2,1)S(1)} %collective-permute-done.61.refs_23_), channel_id=1, source_target_pairs={{0,16},{8,24},{16,0},{24,8},{1,17},{9,25},{17,1},{25,9},{2,18},{10... | collective-permute-start | bytes 442376 | tf_op jit(solution)/shard_map/ppermute | solution.py:46
  375.4 9.3 %collective-permute-start.55 = (bf16[288,256]{1,0:T(8,128)(2,1)S(1)}, bf16[288,256]{1,0:T(8,128)(2,1)S(1)}, u32[]{:S(2)}, u32[]{:S(2)}) collective-permute-start(bf16[288,256]{1,0:T(8,128)(2,1)S(1)} %collective-permute-done.53.refs_15_), channel_id=1, source_target_pairs={{0,16},{8,24},{16,0},{24,8},{1,17},{9,25},{17,1},{25,9},{2,18},{10... | collective-permute-start | bytes 442376 | tf_op jit(solution)/shard_map/ppermute | solution.py:46
  378.0 10.0 %collective-permute-start.59 = (bf16[288,256]{1,0:T(8,128)(2,1)S(1)}, bf16[288,256]{1,0:T(8,128)(2,1)S(1)}, u32[]{:S(2)}, u32[]{:S(2)}) collective-permute-start(bf16[288,256]{1,0:T(8,128)(2,1)S(1)} %collective-permute-done.57.refs_19_), channel_id=1, source_target_pairs={{0,8},{8,0},{16,24},{24,16},{1,9},{9,1},{17,25},{25,17},{2,10},{10... | collective-permute-start | bytes 442376 | tf_op jit(solution)/shard_map/ppermute | solution.py:46
  383.2 9.5 %collective-permute-start.39 = (bf16[576,256]{1,0:T(8,128)(2,1)S(1)}, bf16[576,256]{1,0:T(8,128)(2,1)S(1)}, u32[]{:S(2)}, u32[]{:S(2)}) collective-permute-start(bf16[576,256]{1,0:T(8,128)(2,1)S(1)} %constant_dynamic-update-slice_fusion.2.refs_10_), channel_id=1, source_target_pairs={{0,8},{8,0},{16,24},{24,16},{1,9},{9,1},{17,25},{25,17},{2,10},{10... | collective-permute-start | bytes 884744 | tf_op jit(solution)/shard_map/ppermute | solution.py:46
  384.8 9.9 %collective-permute-start.35 = (bf16[576,256]{1,0:T(8,128)(2,1)S(1)}, bf16[576,256]{1,0:T(8,128)(2,1)S(1)}, u32[]{:S(2)}, u32[]{:S(2)}) collective-permute-start(bf16[576,256]{1,0:T(8,128)(2,1)S(1)} %constant_dynamic-update-slice_fusion.refs_6_), channel_id=1, source_target_pairs={{0,16},{8,24},{16,0},{24,8},{1,17},{9,25},{17,1},{25,9},{2,18},{10... | collective-permute-start | bytes 884744 | tf_op jit(solution)/shard_map/ppermute | solution.py:46
  386.0 9.8 %collective-permute-start.40 = (bf16[576,256]{1,0:T(8,128)(2,1)S(1)}, bf16[576,256]{1,0:T(8,128)(2,1)S(1)}, u32[]{:S(2)}, u32[]{:S(2)}) collective-permute-start(bf16[576,256]{1,0:T(8,128)(2,1)S(1)} %collective-permute-done.38.refs_11_), channel_id=1, source_target_pairs={{0,8},{8,0},{16,24},{24,16},{1,9},{9,1},{17,25},{25,17},{2,10},{10... | collective-permute-start | bytes 884744 | tf_op jit(solution)/shard_map/ppermute | solution.py:46
  387.5 10.6 %collective-permute-start.36 = (bf16[576,256]{1,0:T(8,128)(2,1)S(1)}, bf16[576,256]{1,0:T(8,128)(2,1)S(1)}, u32[]{:S(2)}, u32[]{:S(2)}) collective-permute-start(bf16[576,256]{1,0:T(8,128)(2,1)S(1)} %collective-permute-done.34.refs_7_), channel_id=1, source_target_pairs={{0,16},{8,24},{16,0},{24,8},{1,17},{9,25},{17,1},{25,9},{2,18},{10... | collective-permute-start | bytes 884744 | tf_op jit(solution)/shard_map/ppermute | solution.py:46
  388.0 18.8 %collective-permute-start.68 = (bf16[256,1280]{1,0:T(8,128)(2,1)S(1)}, bf16[256,1280]{1,0:T(8,128)(2,1)S(1)}, u32[]{:S(2)}, u32[]{:S(2)}) collective-permute-start(bf16[256,1280]{1,0:T(8,128)(2,1)S(1)} %collective-permute-done.67.refs_0_), channel_id=1, source_target_pairs={{0,1},{1,0},{2,3},{3,2},{4,5},{5,4},{6,7},{7,6},{8,9},{9,8},{10,11... | collective-permute-start | bytes 1966088 | tf_op jit(solution)/shard_map/ppermute | solution.py:465
  (25 other events, 849.5 us)

commit v4 on v3

--- a/solution.py
+++ b/solution.py
@@ -389,16 +389,19 @@
             for k in range(half):
                 n = block * half + k
                 mine = got[k * rows : (k + 1) * rows]
-                r_v[n, :, begin : begin + size] = (
+                target = r_v if last else outs[0]
+                target[n, :, begin : begin + size] = (
                     added[n, :, begin : begin + size].astype(jnp.float32) + mine
-                ).astype(r_v.dtype)
-                store(m, n, jnp.where(block == 0, spots[k], spots[half + k])).start()
+                ).astype(target.dtype)
+                if last:
+                    store(m, n, jnp.where(block == 0, spots[k], spots[half + k])).start()
             return carry
 
         lax.fori_loop(0, 2, body, 0)
-    for m in range(len(cuts)):
-        for n, spot in enumerate(spots):
-            store(m, n, spot).wait()
+    if last:
+        for m in range(len(cuts)):
+            for n, spot in enumerate(spots):
+                store(m, n, spot).wait()
     if keep is not None:
         keep.wait()
 
@@ -426,13 +429,13 @@
         in_specs=[VMEM if last else ANY]
         + [ANY] * len(w_tags)
         + [VMEM if last else ANY] * len(tags),
-        out_specs=[ANY] * len(shapes),
+        out_specs=[ANY] if last else [VMEM, ANY],
         out_shape=shapes,
         scratch_shapes=[
             pltpu.VMEM((16, 128) if last else (tokens, wide), jnp.bfloat16),
             pltpu.VMEM((deep, columns), jnp.bfloat16),
             pltpu.VMEM((1, 8, 128) if last else base.shape, base.dtype),
-            pltpu.VMEM(base.shape, kind),
+            pltpu.VMEM(base.shape if last else (1, 8, 128), kind),
             pltpu.SemaphoreType.DMA((len(tags),)),
             pltpu.SemaphoreType.DMA((cuts, len(w_tags))),
             pltpu.SemaphoreType.DMA((images,)),

time: 411 us -> 410 us (level)
  no operation moved by 1% of the time
where the time goes in v4:
time: 410 us
  waiting for transfers between devices  243 us (59%)
  starting transfers between devices  76.1 us (19%)
  Pallas kernels  76 us (19%)
  local copies, waits for them, and re-layouts  13.4 us (3%)
    ppermute x30, waiting for transfers between devices, spread(): pieces.append((m ^ d, lax.ppermute(b, 'row', perm)))  88.7 us
    ppermute x12, waiting for transfers between devices, around(): return lax.ppermute(value, 'col', ring(images, parts, step))  83.2 us
    ppermute x10, waiting for transfers between devices, arrive(): got = lax.ppermute(value, 'col', hop(parts, moves))  71.4 us
    ppermute x30, starting transfers between devices, spread(): pieces.append((m ^ d, lax.ppermute(b, 'row', perm)))  33.1 us
    pallas_call x2, Pallas kernels, project_early(): pl.pallas_call(functools.partial(early_kernel, steps, parts, tags, first)...  23.4 us
    ppermute x12, starting transfers between devices, around(): return lax.ppermute(value, 'col', ring(images, parts, step))  17.9 us
    pallas_call x4, Pallas kernels, attend(): pl.pallas_call(functools.partial(attend_kernel, first, slots, heads), in_...  16.5 us
    pallas_call x4, Pallas kernels, normalize(): pl.pallas_call(functools.partial(norm_kernel, masks, parts), grid=(rows /...  13.7 us
  transfers between devices with their start and end apart: 69, of which 26 were waited for; matrix products, arithmetic and copies ran while one was open for 0% of the time, Pallas kernels for 18%

profile of v4, /device:TPU:0, one launch (start us, length us, event | category | flops | bytes accessed | tf_op | source)
XLA Modules:
  0.0 409.5 jit_solution(8322297457311994375)
XLA Ops:
  0.0 2.1 dynamic-slice_bitcast_fusion
  2.1 3.0 collective-permute-start.17
  5.2 1.5 collective-permute-start.18
  6.7 1.6 collective-permute-start.13
  8.3 2.6 collective-permute-start.9
  11.7 9.9 %collective-permute-done.17.refs_1_ = bf16[288,1280]{1,0:T(8,128)(2,1)S(1)} collective-permute-done((bf16[288,1280]{1,0:T(8,128)(2,1)S(1)}, bf16[288,1280]{1,0:T(8,128)(2,1)S(1)}, u32[]{:S(2)}, u32[]{:S(2)}) %collective-permute-start.17) | collective-permute-done | bytes 737312 | tf_op jit(solution)/shard_map/ppermute | solution.py:46
  21.7 1.8 collective-permute-start.41
  23.5 3.2 collective-permute-start.5
  28.7 29.3 %collective-permute-done.9.refs_0_ = bf16[288,1280]{1,0:T(8,128)(2,1)S(1)} collective-permute-done((bf16[288,1280]{1,0:T(8,128)(2,1)S(1)}, bf16[288,1280]{1,0:T(8,128)(2,1)S(1)}, u32[]{:S(2)}, u32[]{:S(2)}) %collective-permute-start.9) | collective-permute-done | bytes 737312 | tf_op jit(solution)/shard_map/ppermute | solution.py:464
  58.4 20.8 %collective-permute-done.5.refs_0_ = bf16[288,1280]{1,0:T(8,128)(2,1)S(1)} collective-permute-done((bf16[288,1280]{1,0:T(8,128)(2,1)S(1)}, bf16[288,1280]{1,0:T(8,128)(2,1)S(1)}, u32[]{:S(2)}, u32[]{:S(2)}) %collective-permute-start.5) | collective-permute-done | bytes 737312 | tf_op jit(solution)/shard_map/ppermute | solution.py:464
  83.2 16.8 %collective-permute-done.21.refs_2_ = bf16[640,768]{1,0:T(8,128)(2,1)} collective-permute-done((bf16[640,768]{1,0:T(8,128)(2,1)S(1)}, bf16[640,768]{1,0:T(8,128)(2,1)}, u32[]{:S(2)}, u32[]{:S(2)}) %collective-permute-start.21) | collective-permute-done | bytes 983072 | tf_op jit(solution)/shard_map/ppermute | solution.py:488
  100.6 1.5 collective-permute-start.6
  102.1 12.2 %collective-permute-done.14.refs_1_ = bf16[288,1280]{1,0:T(8,128)(2,1)S(1)} collective-permute-done((bf16[288,1280]{1,0:T(8,128)(2,1)S(1)}, bf16[288,1280]{1,0:T(8,128)(2,1)S(1)}, u32[]{:S(2)}, u32[]{:S(2)}) %collective-permute-start.14) | collective-permute-done | bytes 737312 | tf_op jit(solution)/shard_map/ppermute | solution.py:46
  115.5 1.3 collective-permute-start.45
  116.8 13.4 %collective-permute-done.11.refs_2_ = bf16[288,1280]{1,0:T(8,128)(2,1)S(1)} collective-permute-done((bf16[288,1280]{1,0:T(8,128)(2,1)S(1)}, bf16[288,1280]{1,0:T(8,128)(2,1)S(1)}, u32[]{:S(2)}, u32[]{:S(2)}) %collective-permute-start.11) | collective-permute-done | bytes 737312 | tf_op jit(solution)/shard_map/ppermute | solution.py:46
  130.1 14.4 %collective-permute-done.6.refs_1_ = bf16[288,1280]{1,0:T(8,128)(2,1)S(1)} collective-permute-done((bf16[288,1280]{1,0:T(8,128)(2,1)S(1)}, bf16[288,1280]{1,0:T(8,128)(2,1)S(1)}, u32[]{:S(2)}, u32[]{:S(2)}) %collective-permute-start.6) | collective-permute-done | bytes 737312 | tf_op jit(solution)/shard_map/ppermute | solution.py:46
  146.0 11.1 %collective-permute-done.45.refs_6_ = bf16[640,768]{1,0:T(8,128)(2,1)S(1)} collective-permute-done((bf16[640,768]{1,0:T(8,128)(2,1)S(1)}, bf16[640,768]{1,0:T(8,128)(2,1)S(1)}, u32[]{:S(2)}, u32[]{:S(2)}) %collective-permute-start.45) | collective-permute-done | bytes 983072 | tf_op jit(solution)/shard_map/ppermute | solution.py:488
  158.4 1.6 collective-permute-start.27
  160.0 1.3 collective-permute-start.49
  162.5 26.5 %collective-permute-done.25.refs_6_ = bf16[640,768]{1,0:T(8,128)(2,1)S(1)} collective-permute-done((bf16[640,768]{1,0:T(8,128)(2,1)S(1)}, bf16[640,768]{1,0:T(8,128)(2,1)S(1)}, u32[]{:S(2)}, u32[]{:S(2)}) %collective-permute-start.25) | collective-permute-done | bytes 983072 | tf_op jit(solution)/shard_map/ppermute | solution.py:488
  189.0 1.9 collective-permute-start.46
  191.6 1.3 collective-permute-start.29
  192.9 16.9 %collective-permute-done.49.refs_2_ = bf16[640,768]{1,0:T(8,128)(2,1)S(1)} collective-permute-done((bf16[640,768]{1,0:T(8,128)(2,1)S(1)}, bf16[640,768]{1,0:T(8,128)(2,1)S(1)}, u32[]{:S(2)}, u32[]{:S(2)}) %collective-permute-start.49) | collective-permute-done | bytes 983072 | tf_op jit(solution)/shard_map/ppermute | solution.py:488
  209.8 1.9 collective-permute-start.50
  212.4 18.4 %collective-permute-done.8.refs_3_ = bf16[288,1280]{1,0:T(8,128)(2,1)S(1)} collective-permute-done((bf16[288,1280]{1,0:T(8,128)(2,1)S(1)}, bf16[288,1280]{1,0:T(8,128)(2,1)S(1)}, u32[]{:S(2)}, u32[]{:S(2)}) %collective-permute-start.8) | collective-permute-done | bytes 737312 | tf_op jit(solution)/shard_map/ppermute | solution.py:46
  230.7 1.6 collective-permute-start.24
  232.3 2.4 collective-permute-start.26
  234.8 3.4 norm.4.refs_4_
  238.2 3.4 norm.5.refs_4_
  241.6 3.4 norm.6.refs_4_
  245.1 3.4 norm.7.x_ref
  248.5 4.3 %copy-done = bf16[4,4,288,1280]{3,2,1,0:T(8,128)(2,1)} copy-done((bf16[4,4,288,1280]{3,2,1,0:T(8,128)(2,1)}, bf16[4,4,288,1280]{3,2,1,0:T(8,128)(2,1)S(1)}, u32[]{:S(2)}) %copy-start) | copy-done | bytes 11796504
  252.8 1.6 collective-permute-start.28
  255.4 1.9 collective-permute-start.30
  257.4 12.0 %early.3.acc_ref = f32[4,288,768]{2,1,0:T(8,128)S(1)} custom-call(bf16[4,4,288,1280]{3,2,1,0:T(8,128)(2,1)} %copy-done, bf16[640,1536]{1,0:T(8,128)(2,1)S(1)} %copy-done.2, bf16[640,1536]{1,0:T(8,128)(2,1)S(1)} %collective-permute-done.20.refs_1_, bf16[640,768]{1,0:T(8,128)(2,1)S(1)} %collective-permute-done.41.refs_2_, ...), custom_call_target="tpu_custom_call" | custom-call | flops 6794772480 | bytes 8847360 | tf_op jit(solution)/shard_map/early/pallas_call | solution.py:179
  269.4 1.7 copy-done.4
  271.1 2.0 copy-done.5
  274.3 6.4 %late.3 = (bf16[1152,256]{1,0:T(8,128)(2,1)S(1)}, bf16[1152,512]{1,0:T(8,128)(2,1)}) custom-call(bf16[4,4,288,1280]{3,2,1,0:T(8,128)(2,1)S(1)} %copy-done.1, f32[4,288,768]{2,1,0:T(8,128)S(1)} %copy-done.5, bf16[640,768]{1,0:T(8,128)(2,1)S(1)} %collective-permute-done.47.refs_0_, bf16[640,768]{1,0:T(8,128)(2,1)S(1)} %collective-permute-done.48.refs_1_, ...), custom_call_target="tpu_custom_call" | custom-call | flops 2264924160 | bytes 7077888 | tf_op jit(solution)/shard_map/late/pallas_call | solution.py:248
  282.2 11.4 %early.2.acc_ref = f32[4,288,768]{2,1,0:T(8,128)S(1)} custom-call(bf16[4,4,288,1280]{3,2,1,0:T(8,128)(2,1)} %copy-done, bf16[640,1536]{1,0:T(8,128)(2,1)S(1)} %copy-done.3, bf16[640,1536]{1,0:T(8,128)(2,1)S(1)} %copy-done.7, bf16[640,768]{1,0:T(8,128)(2,1)} %collective-permute-done.21.refs_2_, bf16[640,768]{1,0:T(8,128)(2,1)} %collective-permute-done.22.refs_3_, ...), custom_call_target="tpu_custom_call" | custom-call | flops 6794772480 | bytes 8847360 | tf_op jit(solution)/shard_map/early/pallas_call | solution.py:179
  293.6 4.7 %late.2 = (bf16[1152,256]{1,0:T(8,128)(2,1)S(1)}, bf16[1152,512]{1,0:T(8,128)(2,1)S(1)}) custom-call(bf16[4,4,288,1280]{3,2,1,0:T(8,128)(2,1)S(1)} %bitcast.11, f32[4,288,768]{2,1,0:T(8,128)S(1)} %early.2.acc_ref, bf16[640,768]{1,0:T(8,128)(2,1)} %collective-permute-done.27.refs_0_, bf16[640,768]{1,0:T(8,128)(2,1)} %collective-permute-done.28.refs_1_, ...), custom_call_target="tpu_custom_call" | custom-call | flops 2264924160 | bytes 7077888 | tf_op jit(solution)/shard_map/late/pallas_call | solution.py:248
  298.6 2.1 collective-permute-done.1.refs_2_
  301.2 17.6 %collective-permute-done.3.refs_4_ = bf16[256,1280]{1,0:T(8,128)(2,1)S(1)} collective-permute-done((bf16[256,1280]{1,0:T(8,128)(2,1)S(1)}, bf16[256,1280]{1,0:T(8,128)(2,1)S(1)}, u32[]{:S(2)}, u32[]{:S(2)}) %collective-permute-start.3) | collective-permute-done | bytes 655392 | tf_op jit(solution)/shard_map/ppermute | solution.py:464
  318.8 4.7 %attend.7 = (bf16[288,256]{1,0:T(8,128)(2,1)S(1)}, bf16[288,256]{1,0:T(8,128)(2,1)S(1)}) custom-call(bf16[1152,256]{1,0:T(8,128)(2,1)S(1)} %copy-done.16, bf16[1152,512]{1,0:T(8,128)(2,1)} %get-tuple-element.26.refs_0_, bf16[1152,512]{1,0:T(8,128)(2,1)S(1)} %collective-permute-done.51.refs_1_), custom_call_target="tpu_custom_call" | custom-call | flops 2717908992 | bytes 3538944 | tf_op jit(solution)/shard_map/attend/pallas_call | solution.py:303
  323.5 4.7 %attend.6 = (bf16[288,256]{1,0:T(8,128)(2,1)S(1)}, bf16[288,256]{1,0:T(8,128)(2,1)S(1)}) custom-call(bf16[1152,256]{1,0:T(8,128)(2,1)S(1)} %copy-done.16, bf16[1152,512]{1,0:T(8,128)(2,1)} %get-tuple-element.26.refs_0_, bf16[1152,512]{1,0:T(8,128)(2,1)S(1)} %collective-permute-done.51.refs_1_), custom_call_target="tpu_custom_call" | custom-call | flops 2717908992 | bytes 3538944 | tf_op jit(solution)/shard_map/attend/pallas_call | solution.py:303
  328.8 3.4 attend.5
  333.6 2.2 collective-permute-start.37
  335.8 3.7 attend.4
  339.5 3.9 collective-permute-start.52
  343.3 7.2 %collective-permute-done.37 = bf16[288,256]{1,0:T(8,128)(2,1)S(1)} collective-permute-done((bf16[288,256]{1,0:T(8,128)(2,1)S(1)}, bf16[288,256]{1,0:T(8,128)(2,1)S(1)}, u32[]{:S(2)}, u32[]{:S(2)}) %collective-permute-start.37) | collective-permute-done | bytes 147488 | tf_op jit(solution)/shard_map/ppermute | solution.py:464
  350.5 3.3 collective-permute-start.32
  355.3 1.6 collective-permute-start.62
  359.3 3.1 collective-permute-done.56.refs_18_
  366.4 1.3 collective-permute-start.38
  367.7 1.5 collective-permute-start.34
  369.7 4.5 %collective-permute-done.57.refs_19_ = bf16[288,256]{1,0:T(8,128)(2,1)S(1)} collective-permute-done((bf16[288,256]{1,0:T(8,128)(2,1)S(1)}, bf16[288,256]{1,0:T(8,128)(2,1)S(1)}, u32[]{:S(2)}, u32[]{:S(2)}) %collective-permute-start.57) | collective-permute-done | bytes 147488 | tf_op jit(solution)/shard_map/ppermute | solution.py:46
  376.2 1.8 collective-permute-done.58.refs_20_
  378.0 1.5 collective-permute-start.59
  379.5 3.7 collective-permute-done.63.refs_25_
  386.0 1.5 collective-permute-start.40
  388.0 4.7 %collective-permute-done.39.refs_12_ = bf16[576,256]{1,0:T(8,128)(2,1)S(1)} collective-permute-done((bf16[576,256]{1,0:T(8,128)(2,1)S(1)}, bf16[576,256]{1,0:T(8,128)(2,1)S(1)}, u32[]{:S(2)}, u32[]{:S(2)}) %collective-permute-start.39) | collective-permute-done | bytes 294944 | tf_op jit(solution)/shard_map/ppermute | solution.py:46
  392.7 2.0 collective-permute-done.35.refs_8_
  395.8 2.2 collective-permute-done.36.refs_9_
  398.0 8.1 %out.2 = (f32[4,288,1280]{2,1,0:T(8,128)S(1)}, bf16[1152,512]{1,0:T(8,128)(2,1)S(1)}) custom-call(bf16[4,288,1280]{2,1,0:T(8,128)(2,1)S(1)} %copy-done.8, bf16[256,1280]{1,0:T(8,128)(2,1)} %refs_0_.5, bf16[256,1280]{1,0:T(8,128)(2,1)S(1)} %collective-permute-done.refs_1_, bf16[256,1280]{1,0:T(8,128)(2,1)S(1)} %collective-permute-done.1.refs_2_, ...), custom_call_target="tpu_custom_call" | custom-call | flops 4529848320 | bytes 11796480 | tf_op jit(solution)/shard_map/out/pallas_call | solution.py:427
  406.1 3.2 out.3
  (135 shorter events, 35.5 us)
Async XLA Ops:
  2.1 19.5 %collective-permute-start.17 = (bf16[288,1280]{1,0:T(8,128)(2,1)S(1)}, bf16[288,1280]{1,0:T(8,128)(2,1)S(1)}, u32[]{:S(2)}, u32[]{:S(2)}) collective-permute-start(bf16[288,1280]{1,0:T(8,128)(2,1)S(1)} %get-tuple-element.33.refs_0_), channel_id=1, source_target_pairs={{0,8},{8,0},{16,24},{24,16},{1,9},{9,1},{17,25},{25,17},{2,10},{10... | collective-permute-start | bytes 2211848 | tf_op jit(solution)/shard_map/ppermute | solution.py:46
  5.2 18.3 %collective-permute-start.18 = (bf16[288,1280]{1,0:T(8,128)(2,1)S(1)}, bf16[288,1280]{1,0:T(8,128)(2,1)S(1)}, u32[]{:S(2)}, u32[]{:S(2)}) collective-permute-start(bf16[288,1280]{1,0:T(8,128)(2,1)S(1)} %get-tuple-element.33.refs_0_), channel_id=1, source_target_pairs={{0,16},{8,24},{16,0},{24,8},{1,17},{9,25},{17,1},{25,9},{2,18},{10... | collective-permute-start | bytes 2211848 | tf_op jit(solution)/shard_map/ppermute | solution.py:46
  6.7 21.3 %collective-permute-start.13 = (bf16[288,1280]{1,0:T(8,128)(2,1)S(1)}, bf16[288,1280]{1,0:T(8,128)(2,1)S(1)}, u32[]{:S(2)}, u32[]{:S(2)}) collective-permute-start(bf16[288,1280]{1,0:T(8,128)(2,1)S(1)} %get-tuple-element.34), channel_id=1, source_target_pairs={{0,2},{1,3},{2,4},{3,5},{4,6},{5,7},{6,0},{7,1},{8,10},{9,11},{10,... | collective-permute-start | bytes 2211848 | tf_op jit(solution)/shard_map/ppermute | solution.py:464
  8.3 49.7 %collective-permute-start.9 = (bf16[288,1280]{1,0:T(8,128)(2,1)S(1)}, bf16[288,1280]{1,0:T(8,128)(2,1)S(1)}, u32[]{:S(2)}, u32[]{:S(2)}) collective-permute-start(bf16[288,1280]{1,0:T(8,128)(2,1)S(1)} %get-tuple-element.35), channel_id=1, source_target_pairs={{0,4},{1,5},{2,6},{3,7},{4,0},{5,1},{6,2},{7,3},{8,12},{9,13},{10,... | collective-permute-start | bytes 2211848 | tf_op jit(solution)/shard_map/ppermute | solution.py:464
  11.0 69.3 %collective-permute-start.43 = (bf16[640,768]{1,0:T(8,128)(2,1)S(1)}, bf16[640,768]{1,0:T(8,128)(2,1)S(1)}, u32[]{:S(2)}, u32[]{:S(2)}) collective-permute-start(bf16[640,768]{1,0:T(8,128)(2,1)S(1)} %get-tuple-element.37), channel_id=1, source_target_pairs={{2,4},{3,5},{4,2},{5,3},{10,12},{11,13},{12,10},{13,11},{18,20},{1... | collective-permute-start | bytes 2949128 | tf_op jit(solution)/shard_map/ppermute | solution.py:488
  21.7 59.5 %collective-permute-start.41 = (bf16[640,768]{1,0:T(8,128)(2,1)S(1)}, bf16[640,768]{1,0:T(8,128)(2,1)S(1)}, u32[]{:S(2)}, u32[]{:S(2)}) collective-permute-start(bf16[640,768]{1,0:T(8,128)(2,1)S(1)} %get-tuple-element.37), channel_id=1, source_target_pairs={{0,2},{1,3},{2,0},{3,1},{4,6},{5,7},{6,4},{7,5},{8,10},{9,11},{10,... | collective-permute-start | bytes 2949128 | tf_op jit(solution)/shard_map/ppermute | solution.py:488
  23.5 55.7 %collective-permute-start.5 = (bf16[288,1280]{1,0:T(8,128)(2,1)S(1)}, bf16[288,1280]{1,0:T(8,128)(2,1)S(1)}, u32[]{:S(2)}, u32[]{:S(2)}) collective-permute-start(bf16[288,1280]{1,0:T(8,128)(2,1)S(1)} %get-tuple-element.36), channel_id=1, source_target_pairs={{0,6},{1,7},{2,0},{3,1},{4,2},{5,3},{6,4},{7,5},{8,14},{9,15},{10,... | collective-permute-start | bytes 2211848 | tf_op jit(solution)/shard_map/ppermute | solution.py:464
  28.0 54.4 %collective-permute-start.23 = (bf16[640,768]{1,0:T(8,128)(2,1)S(1)}, bf16[640,768]{1,0:T(8,128)(2,1)S(1)}, u32[]{:S(2)}, u32[]{:S(2)}) collective-permute-start(bf16[640,768]{1,0:T(8,128)(2,1)S(1)} %get-tuple-element.38), channel_id=1, source_target_pairs={{2,4},{3,5},{4,2},{5,3},{10,12},{11,13},{12,10},{13,11},{18,20},{1... | collective-permute-start | bytes 2949128 | tf_op jit(solution)/shard_map/ppermute | solution.py:488
  58.0 42.1 %collective-permute-start.21 = (bf16[640,768]{1,0:T(8,128)(2,1)S(1)}, bf16[640,768]{1,0:T(8,128)(2,1)}, u32[]{:S(2)}, u32[]{:S(2)}) collective-permute-start(bf16[640,768]{1,0:T(8,128)(2,1)S(1)} %get-tuple-element.38), channel_id=1, source_target_pairs={{0,2},{1,3},{2,0},{3,1},{4,6},{5,7},{6,4},{7,5},{8,10},{9,11},{10,... | collective-permute-start | bytes 2949128 | tf_op jit(solution)/shard_map/ppermute | solution.py:488
  79.2 21.4 %collective-permute-start.19 = (bf16[288,1280]{1,0:T(8,128)(2,1)S(1)}, bf16[288,1280]{1,0:T(8,128)(2,1)S(1)}, u32[]{:S(2)}, u32[]{:S(2)}) collective-permute-start(bf16[288,1280]{1,0:T(8,128)(2,1)S(1)} %collective-permute-done.17.refs_1_), channel_id=1, source_target_pairs={{0,16},{8,24},{16,0},{24,8},{1,17},{9,25},{17,1},{25,9},{2,18},{10... | collective-permute-start | bytes 2211848 | tf_op jit(solution)/shard_map/ppermute | solution.py:46
  80.3 34.0 %collective-permute-start.14 = (bf16[288,1280]{1,0:T(8,128)(2,1)S(1)}, bf16[288,1280]{1,0:T(8,128)(2,1)S(1)}, u32[]{:S(2)}, u32[]{:S(2)}) collective-permute-start(bf16[288,1280]{1,0:T(8,128)(2,1)S(1)} %collective-permute-done.13.refs_0_), channel_id=1, source_target_pairs={{0,16},{8,24},{16,0},{24,8},{1,17},{9,25},{17,1},{25,9},{2,18},{10... | collective-permute-start | bytes 2211848 | tf_op jit(solution)/shard_map/ppermute | solution.py:46
  81.2 33.1 %collective-permute-start.15 = (bf16[288,1280]{1,0:T(8,128)(2,1)S(1)}, bf16[288,1280]{1,0:T(8,128)(2,1)S(1)}, u32[]{:S(2)}, u32[]{:S(2)}) collective-permute-start(bf16[288,1280]{1,0:T(8,128)(2,1)S(1)} %collective-permute-done.13.refs_0_), channel_id=1, source_target_pairs={{0,8},{8,0},{16,24},{24,16},{1,9},{9,1},{17,25},{25,17},{2,10},{10... | collective-permute-start | bytes 2211848 | tf_op jit(solution)/shard_map/ppermute | solution.py:46
  82.3 33.1 %collective-permute-start.10 = (bf16[288,1280]{1,0:T(8,128)(2,1)S(1)}, bf16[288,1280]{1,0:T(8,128)(2,1)S(1)}, u32[]{:S(2)}, u32[]{:S(2)}) collective-permute-start(bf16[288,1280]{1,0:T(8,128)(2,1)S(1)} %collective-permute-done.9.refs_0_), channel_id=1, source_target_pairs={{0,8},{8,0},{16,24},{24,16},{1,9},{9,1},{17,25},{25,17},{2,10},{10... | collective-permute-start | bytes 2211848 | tf_op jit(solution)/shard_map/ppermute | solution.py:46
  100.1 30.1 %collective-permute-start.11 = (bf16[288,1280]{1,0:T(8,128)(2,1)S(1)}, bf16[288,1280]{1,0:T(8,128)(2,1)S(1)}, u32[]{:S(2)}, u32[]{:S(2)}) collective-permute-start(bf16[288,1280]{1,0:T(8,128)(2,1)S(1)} %collective-permute-done.9.refs_0_), channel_id=1, source_target_pairs={{0,16},{8,24},{16,0},{24,8},{1,17},{9,25},{17,1},{25,9},{2,18},{10... | collective-permute-start | bytes 2211848 | tf_op jit(solution)/shard_map/ppermute | solution.py:46
  100.6 44.0 %collective-permute-start.6 = (bf16[288,1280]{1,0:T(8,128)(2,1)S(1)}, bf16[288,1280]{1,0:T(8,128)(2,1)S(1)}, u32[]{:S(2)}, u32[]{:S(2)}) collective-permute-start(bf16[288,1280]{1,0:T(8,128)(2,1)S(1)} %collective-permute-done.5.refs_0_), channel_id=1, source_target_pairs={{0,16},{8,24},{16,0},{24,8},{1,17},{9,25},{17,1},{25,9},{2,18},{10... | collective-permute-start | bytes 2211848 | tf_op jit(solution)/shard_map/ppermute | solution.py:46
  114.3 47.6 %collective-permute-start.20 = (bf16[640,1536]{1,0:T(8,128)(2,1)S(1)}, bf16[640,1536]{1,0:T(8,128)(2,1)S(1)}, u32[]{:S(2)}, u32[]{:S(2)}) collective-permute-start(bf16[640,1536]{1,0:T(8,128)(2,1)S(1)} %copy-done.2), channel_id=1, source_target_pairs={{0,1},{1,0},{2,3},{3,2},{4,5},{5,4},{6,7},{7,6},{8,9},{9,8},{10,11... | collective-permute-start | bytes 5898248 | tf_op jit(solution)/shard_map/ppermute | solution.py:468
  114.3 30.9 %collective-permute-start.7 = (bf16[288,1280]{1,0:T(8,128)(2,1)S(1)}, bf16[288,1280]{1,0:T(8,128)(2,1)S(1)}, u32[]{:S(2)}, u32[]{:S(2)}) collective-permute-start(bf16[288,1280]{1,0:T(8,128)(2,1)S(1)} %collective-permute-done.5.refs_0_), channel_id=1, source_target_pairs={{0,8},{8,0},{16,24},{24,16},{1,9},{9,1},{17,25},{25,17},{2,10},{10... | collective-permute-start | bytes 2211848 | tf_op jit(solution)/shard_map/ppermute | solution.py:46
  115.5 41.7 %collective-permute-start.45 = (bf16[640,768]{1,0:T(8,128)(2,1)S(1)}, bf16[640,768]{1,0:T(8,128)(2,1)S(1)}, u32[]{:S(2)}, u32[]{:S(2)}) collective-permute-start(bf16[640,768]{1,0:T(8,128)(2,1)S(1)} %collective-permute-done.43.refs_4_), channel_id=1, source_target_pairs={{2,0},{3,1},{4,6},{5,7},{10,8},{11,9},{12,14},{13,15},{18,16},{19,... | collective-permute-start | bytes 2949128 | tf_op jit(solution)/shard_map/ppermute | solution.py:488
  130.1 28.3 %collective-permute-start.42 = (bf16[640,768]{1,0:T(8,128)(2,1)S(1)}, bf16[640,768]{1,0:T(8,128)(2,1)S(1)}, u32[]{:S(2)}, u32[]{:S(2)}) collective-permute-start(bf16[640,768]{1,0:T(8,128)(2,1)S(1)} %collective-permute-done.41.refs_2_), channel_id=1, source_target_pairs={{0,1},{1,0},{2,3},{3,2},{4,5},{5,4},{6,7},{7,6},{8,9},{9,8},{10,11... | collective-permute-start | bytes 2949128 | tf_op jit(solution)/shard_map/ppermute | solution.py:495
  144.5 15.5 %collective-permute-start.47 = (bf16[640,768]{1,0:T(8,128)(2,1)S(1)}, bf16[640,768]{1,0:T(8,128)(2,1)S(1)}, u32[]{:S(2)}, u32[]{:S(2)}) collective-permute-start(bf16[640,768]{1,0:T(8,128)(2,1)S(1)} %collective-permute-done.41.refs_2_), channel_id=1, source_target_pairs={{2,4},{3,5},{4,2},{5,3},{10,12},{11,13},{12,10},{13,11},{18,20},{1... | collective-permute-start | bytes 2949128 | tf_op jit(solution)/shard_map/ppermute | solution.py:488
  145.3 16.1 %collective-permute-start.44 = (bf16[640,768]{1,0:T(8,128)(2,1)S(1)}, bf16[640,768]{1,0:T(8,128)(2,1)S(1)}, u32[]{:S(2)}, u32[]{:S(2)}) collective-permute-start(bf16[640,768]{1,0:T(8,128)(2,1)S(1)} %collective-permute-done.43.refs_4_), channel_id=1, source_target_pairs={{2,3},{3,2},{4,5},{5,4},{10,11},{11,10},{12,13},{13,12},{18,19},{1... | collective-permute-start | bytes 2949128 | tf_op jit(solution)/shard_map/ppermute | solution.py:495
  157.1 31.8 %collective-permute-start.25 = (bf16[640,768]{1,0:T(8,128)(2,1)S(1)}, bf16[640,768]{1,0:T(8,128)(2,1)S(1)}, u32[]{:S(2)}, u32[]{:S(2)}) collective-permute-start(bf16[640,768]{1,0:T(8,128)(2,1)S(1)} %collective-permute-done.23.refs_4_), channel_id=1, source_target_pairs={{2,0},{3,1},{4,6},{5,7},{10,8},{11,9},{12,14},{13,15},{18,16},{19,... | collective-permute-start | bytes 2949128 | tf_op jit(solution)/shard_map/ppermute | solution.py:488
  158.4 32.5 %collective-permute-start.27 = (bf16[640,768]{1,0:T(8,128)(2,1)}, bf16[640,768]{1,0:T(8,128)(2,1)}, u32[]{:S(2)}, u32[]{:S(2)}) collective-permute-start(bf16[640,768]{1,0:T(8,128)(2,1)} %collective-permute-done.21.refs_2_), channel_id=1, source_target_pairs={{2,4},{3,5},{4,2},{5,3},{10,12},{11,13},{12,10},{13,11},{18,20},{1... | collective-permute-start | bytes 2949128 | tf_op jit(solution)/shard_map/ppermute | solution.py:488
  160.0 49.8 %collective-permute-start.49 = (bf16[640,768]{1,0:T(8,128)(2,1)S(1)}, bf16[640,768]{1,0:T(8,128)(2,1)S(1)}, u32[]{:S(2)}, u32[]{:S(2)}) collective-permute-start(bf16[640,768]{1,0:T(8,128)(2,1)S(1)} %collective-permute-done.47.refs_0_), channel_id=1, source_target_pairs={{2,0},{3,1},{4,6},{5,7},{10,8},{11,9},{12,14},{13,15},{18,16},{19,... | collective-permute-start | bytes 2949128 | tf_op jit(solution)/shard_map/ppermute | solution.py:488
  161.3 30.3 %collective-permute-start.16 = (bf16[288,1280]{1,0:T(8,128)(2,1)S(1)}, bf16[288,1280]{1,0:T(8,128)(2,1)S(1)}, u32[]{:S(2)}, u32[]{:S(2)}) collective-permute-start(bf16[288,1280]{1,0:T(8,128)(2,1)S(1)} %collective-permute-done.14.refs_1_), channel_id=1, source_target_pairs={{0,8},{8,0},{16,24},{24,16},{1,9},{9,1},{17,25},{25,17},{2,10},{10... | collective-permute-start | bytes 2211848 | tf_op jit(solution)/shard_map/ppermute | solution.py:46
  162.0 49.8 %collective-permute-start.12 = (bf16[288,1280]{1,0:T(8,128)(2,1)S(1)}, bf16[288,1280]{1,0:T(8,128)(2,1)S(1)}, u32[]{:S(2)}, u32[]{:S(2)}) collective-permute-start(bf16[288,1280]{1,0:T(8,128)(2,1)S(1)} %collective-permute-done.10.refs_1_), channel_id=1, source_target_pairs={{0,16},{8,24},{16,0},{24,8},{1,17},{9,25},{17,1},{25,9},{2,18},{10... | collective-permute-start | bytes 2211848 | tf_op jit(solution)/shard_map/ppermute | solution.py:46
  189.0 41.8 %collective-permute-start.46 = (bf16[640,768]{1,0:T(8,128)(2,1)S(1)}, bf16[640,768]{1,0:T(8,128)(2,1)S(1)}, u32[]{:S(2)}, u32[]{:S(2)}) collective-permute-start(bf16[640,768]{1,0:T(8,128)(2,1)S(1)} %collective-permute-done.45.refs_6_), channel_id=1, source_target_pairs={{0,1},{1,0},{6,7},{7,6},{8,9},{9,8},{14,15},{15,14},{16,17},{17,16... | collective-permute-start | bytes 2949128 | tf_op jit(solution)/shard_map/ppermute | solution.py:495
  190.9 41.4 %collective-permute-start.48 = (bf16[640,768]{1,0:T(8,128)(2,1)S(1)}, bf16[640,768]{1,0:T(8,128)(2,1)S(1)}, u32[]{:S(2)}, u32[]{:S(2)}) collective-permute-start(bf16[640,768]{1,0:T(8,128)(2,1)S(1)} %collective-permute-done.47.refs_0_), channel_id=1, source_target_pairs={{2,3},{3,2},{4,5},{5,4},{10,11},{11,10},{12,13},{13,12},{18,19},{1... | collective-permute-start | bytes 2949128 | tf_op jit(solution)/shard_map/ppermute | solution.py:495
  191.6 61.2 %collective-permute-start.29 = (bf16[640,768]{1,0:T(8,128)(2,1)}, bf16[640,768]{1,0:T(8,128)(2,1)}, u32[]{:S(2)}, u32[]{:S(2)}) collective-permute-start(bf16[640,768]{1,0:T(8,128)(2,1)} %collective-permute-done.27.refs_0_), channel_id=1, source_target_pairs={{2,0},{3,1},{4,6},{5,7},{10,8},{11,9},{12,14},{13,15},{18,16},{19,... | collective-permute-start | bytes 2949128 | tf_op jit(solution)/shard_map/ppermute | solution.py:488
  209.8 44.6 %collective-permute-start.50 = (bf16[640,768]{1,0:T(8,128)(2,1)S(1)}, bf16[640,768]{1,0:T(8,128)(2,1)S(1)}, u32[]{:S(2)}, u32[]{:S(2)}) collective-permute-start(bf16[640,768]{1,0:T(8,128)(2,1)S(1)} %collective-permute-done.49.refs_2_), channel_id=1, source_target_pairs={{0,1},{1,0},{6,7},{7,6},{8,9},{9,8},{14,15},{15,14},{16,17},{17,16... | collective-permute-start | bytes 2949128 | tf_op jit(solution)/shard_map/ppermute | solution.py:495
  211.8 19.0 %collective-permute-start.8 = (bf16[288,1280]{1,0:T(8,128)(2,1)S(1)}, bf16[288,1280]{1,0:T(8,128)(2,1)S(1)}, u32[]{:S(2)}, u32[]{:S(2)}) collective-permute-start(bf16[288,1280]{1,0:T(8,128)(2,1)S(1)} %collective-permute-done.6.refs_1_), channel_id=1, source_target_pairs={{0,8},{8,0},{16,24},{24,16},{1,9},{9,1},{17,25},{25,17},{2,10},{10... | collective-permute-start | bytes 2211848 | tf_op jit(solution)/shard_map/ppermute | solution.py:46
  230.7 50.8 %collective-permute-start.22 = (bf16[640,768]{1,0:T(8,128)(2,1)}, bf16[640,768]{1,0:T(8,128)(2,1)}, u32[]{:S(2)}, u32[]{:S(2)}) collective-permute-start(bf16[640,768]{1,0:T(8,128)(2,1)} %collective-permute-done.21.refs_2_), channel_id=1, source_target_pairs={{0,1},{1,0},{2,3},{3,2},{4,5},{5,4},{6,7},{7,6},{8,9},{9,8},{10,11... | collective-permute-start | bytes 2949128 | tf_op jit(solution)/shard_map/ppermute | solution.py:495
  230.7 51.1 %collective-permute-start.24 = (bf16[640,768]{1,0:T(8,128)(2,1)S(1)}, bf16[640,768]{1,0:T(8,128)(2,1)}, u32[]{:S(2)}, u32[]{:S(2)}) collective-permute-start(bf16[640,768]{1,0:T(8,128)(2,1)S(1)} %collective-permute-done.23.refs_4_), channel_id=1, source_target_pairs={{2,3},{3,2},{4,5},{5,4},{10,11},{11,10},{12,13},{13,12},{18,19},{1... | collective-permute-start | bytes 2949128 | tf_op jit(solution)/shard_map/ppermute | solution.py:495
  232.3 49.8 %collective-permute-start.26 = (bf16[640,768]{1,0:T(8,128)(2,1)S(1)}, bf16[640,768]{1,0:T(8,128)(2,1)}, u32[]{:S(2)}, u32[]{:S(2)}) collective-permute-start(bf16[640,768]{1,0:T(8,128)(2,1)S(1)} %collective-permute-done.25.refs_6_), channel_id=1, source_target_pairs={{0,1},{1,0},{6,7},{7,6},{8,9},{9,8},{14,15},{15,14},{16,17},{17,16... | collective-permute-start | bytes 2949128 | tf_op jit(solution)/shard_map/ppermute | solution.py:495
  252.8 40.8 %collective-permute-start.28 = (bf16[640,768]{1,0:T(8,128)(2,1)}, bf16[640,768]{1,0:T(8,128)(2,1)}, u32[]{:S(2)}, u32[]{:S(2)}) collective-permute-start(bf16[640,768]{1,0:T(8,128)(2,1)} %collective-permute-done.27.refs_0_), channel_id=1, source_target_pairs={{2,3},{3,2},{4,5},{5,4},{10,11},{11,10},{12,13},{13,12},{18,19},{1... | collective-permute-start | bytes 2949128 | tf_op jit(solution)/shard_map/ppermute | solution.py:495
  255.4 38.2 %collective-permute-start.30 = (bf16[640,768]{1,0:T(8,128)(2,1)}, bf16[640,768]{1,0:T(8,128)(2,1)}, u32[]{:S(2)}, u32[]{:S(2)}) collective-permute-start(bf16[640,768]{1,0:T(8,128)(2,1)} %collective-permute-done.29.refs_2_), channel_id=1, source_target_pairs={{0,1},{1,0},{6,7},{7,6},{8,9},{9,8},{14,15},{15,14},{16,17},{17,16... | collective-permute-start | bytes 2949128 | tf_op jit(solution)/shard_map/ppermute | solution.py:495
  281.6 19.1 %collective-permute-start.1 = (bf16[256,1280]{1,0:T(8,128)(2,1)}, bf16[256,1280]{1,0:T(8,128)(2,1)S(1)}, u32[]{:S(2)}, u32[]{:S(2)}) collective-permute-start(bf16[256,1280]{1,0:T(8,128)(2,1)} %refs_0_.5), channel_id=1, source_target_pairs={{0,2},{1,3},{2,4},{3,5},{4,6},{5,7},{6,0},{7,1},{8,10},{9,11},{10,... | collective-permute-start | bytes 1966088 | tf_op jit(solution)/shard_map/ppermute | solution.py:464
  281.8 36.9 %collective-permute-start.51 = (bf16[1152,512]{1,0:T(8,128)(2,1)}, bf16[1152,512]{1,0:T(8,128)(2,1)S(1)}, u32[]{:S(2)}, u32[]{:S(2)}) collective-permute-start(bf16[1152,512]{1,0:T(8,128)(2,1)} %get-tuple-element.26.refs_0_), channel_id=1, source_target_pairs={{0,1},{1,0},{2,3},{3,2},{4,5},{5,4},{6,7},{7,6},{8,9},{9,8},{10,11... | collective-permute-start | bytes 3538952 | tf_op jit(solution)/shard_map/ppermute | solution.py:510
  298.3 29.9 %collective-permute-start.31 = (bf16[1152,512]{1,0:T(8,128)(2,1)S(1)}, bf16[1152,512]{1,0:T(8,128)(2,1)S(1)}, u32[]{:S(2)}, u32[]{:S(2)}) collective-permute-start(bf16[1152,512]{1,0:T(8,128)(2,1)S(1)} %get-tuple-element.20.refs_0_), channel_id=1, source_target_pairs={{0,1},{1,0},{2,3},{3,2},{4,5},{5,4},{6,7},{7,6},{8,9},{9,8},{10,11... | collective-permute-start | bytes 3538952 | tf_op jit(solution)/shard_map/ppermute | solution.py:510
  300.7 18.1 %collective-permute-start.3 = (bf16[256,1280]{1,0:T(8,128)(2,1)S(1)}, bf16[256,1280]{1,0:T(8,128)(2,1)S(1)}, u32[]{:S(2)}, u32[]{:S(2)}) collective-permute-start(bf16[256,1280]{1,0:T(8,128)(2,1)S(1)} %collective-permute-done.1.refs_2_), channel_id=1, source_target_pairs={{0,2},{1,3},{2,4},{3,5},{4,6},{5,7},{6,0},{7,1},{8,10},{9,11},{10,... | collective-permute-start | bytes 1966088 | tf_op jit(solution)/shard_map/ppermute | solution.py:464
  300.7 31.6 %collective-permute-start = (bf16[256,1280]{1,0:T(8,128)(2,1)}, bf16[256,1280]{1,0:T(8,128)(2,1)S(1)}, u32[]{:S(2)}, u32[]{:S(2)}) collective-permute-start(bf16[256,1280]{1,0:T(8,128)(2,1)} %refs_0_.5), channel_id=1, source_target_pairs={{0,1},{1,0},{2,3},{3,2},{4,5},{5,4},{6,7},{7,6},{8,9},{9,8},{10,11... | collective-permute-start | bytes 1966088 | tf_op jit(solution)/shard_map/ppermute | solution.py:468
  300.7 32.2 %collective-permute-start.2 = (bf16[256,1280]{1,0:T(8,128)(2,1)S(1)}, bf16[256,1280]{1,0:T(8,128)(2,1)S(1)}, u32[]{:S(2)}, u32[]{:S(2)}) collective-permute-start(bf16[256,1280]{1,0:T(8,128)(2,1)S(1)} %collective-permute-done.1.refs_2_), channel_id=1, source_target_pairs={{0,1},{1,0},{2,3},{3,2},{4,5},{5,4},{6,7},{7,6},{8,9},{9,8},{10,11... | collective-permute-start | bytes 1966088 | tf_op jit(solution)/shard_map/ppermute | solution.py:468
  318.8 14.9 %collective-permute-start.4 = (bf16[256,1280]{1,0:T(8,128)(2,1)S(1)}, bf16[256,1280]{1,0:T(8,128)(2,1)S(1)}, u32[]{:S(2)}, u32[]{:S(2)}) collective-permute-start(bf16[256,1280]{1,0:T(8,128)(2,1)S(1)} %collective-permute-done.3.refs_4_), channel_id=1, source_target_pairs={{0,1},{1,0},{2,3},{3,2},{4,5},{5,4},{6,7},{7,6},{8,9},{9,8},{10,11... | collective-permute-start | bytes 1966088 | tf_op jit(solution)/shard_map/ppermute | solution.py:468
  318.8 20.7 %collective-permute-start.67 = (bf16[256,1280]{1,0:T(8,128)(2,1)S(1)}, bf16[256,1280]{1,0:T(8,128)(2,1)S(1)}, u32[]{:S(2)}, u32[]{:S(2)}) collective-permute-start(bf16[256,1280]{1,0:T(8,128)(2,1)S(1)} %collective-permute-done.3.refs_4_), channel_id=1, source_target_pairs={{0,2},{1,3},{2,4},{3,5},{4,6},{5,7},{6,0},{7,1},{8,10},{9,11},{10,... | collective-permute-start | bytes 1966088 | tf_op jit(solution)/shard_map/ppermute | solution.py:464
  328.2 25.7 %collective-permute-start.64 = (bf16[288,256]{1,0:T(8,128)(2,1)S(1)}, bf16[288,256]{1,0:T(8,128)(2,1)S(1)}, u32[]{:S(2)}, u32[]{:S(2)}) collective-permute-start(bf16[288,256]{1,0:T(8,128)(2,1)S(1)} %get-tuple-element.30.refs_26_), channel_id=1, source_target_pairs={{0,16},{8,24},{16,0},{24,8},{1,17},{9,25},{17,1},{25,9},{2,18},{10... | collective-permute-start | bytes 442376 | tf_op jit(solution)/shard_map/ppermute | solution.py:46
  332.3 21.7 %collective-permute-start.65 = (bf16[288,256]{1,0:T(8,128)(2,1)S(1)}, bf16[288,256]{1,0:T(8,128)(2,1)S(1)}, u32[]{:S(2)}, u32[]{:S(2)}) collective-permute-start(bf16[288,256]{1,0:T(8,128)(2,1)S(1)} %get-tuple-element.30.refs_26_), channel_id=1, source_target_pairs={{0,8},{8,0},{16,24},{24,16},{1,9},{9,1},{17,25},{25,17},{2,10},{10... | collective-permute-start | bytes 442376 | tf_op jit(solution)/shard_map/ppermute | solution.py:46
  332.9 21.0 %collective-permute-start.60 = (bf16[288,256]{1,0:T(8,128)(2,1)S(1)}, bf16[288,256]{1,0:T(8,128)(2,1)S(1)}, u32[]{:S(2)}, u32[]{:S(2)}) collective-permute-start(bf16[288,256]{1,0:T(8,128)(2,1)S(1)} %get-tuple-element.29), channel_id=1, source_target_pairs={{0,4},{1,5},{2,6},{3,7},{4,0},{5,1},{6,2},{7,3},{8,12},{9,13},{10,... | collective-permute-start | bytes 442376 | tf_op jit(solution)/shard_map/ppermute | solution.py:464
  333.6 16.9 %collective-permute-start.37 = (bf16[288,256]{1,0:T(8,128)(2,1)S(1)}, bf16[288,256]{1,0:T(8,128)(2,1)S(1)}, u32[]{:S(2)}, u32[]{:S(2)}) collective-permute-start(bf16[288,256]{1,0:T(8,128)(2,1)S(1)} %get-tuple-element.23), channel_id=1, source_target_pairs={{0,4},{1,5},{2,6},{3,7},{4,0},{5,1},{6,2},{7,3},{8,12},{9,13},{10,... | collective-permute-start | bytes 442376 | tf_op jit(solution)/shard_map/ppermute | solution.py:464
  339.5 15.8 %collective-permute-start.52 = (bf16[288,256]{1,0:T(8,128)(2,1)S(1)}, bf16[288,256]{1,0:T(8,128)(2,1)S(1)}, u32[]{:S(2)}, u32[]{:S(2)}) collective-permute-start(bf16[288,256]{1,0:T(8,128)(2,1)S(1)} %get-tuple-element.27), channel_id=1, source_target_pairs={{0,6},{1,7},{2,0},{3,1},{4,2},{5,3},{6,4},{7,5},{8,14},{9,15},{10,... | collective-permute-start | bytes 442376 | tf_op jit(solution)/shard_map/ppermute | solution.py:464
  353.9 10.4 %collective-permute-start.33 = (bf16[288,256]{1,0:T(8,128)(2,1)S(1)}, bf16[288,256]{1,0:T(8,128)(2,1)S(1)}, u32[]{:S(2)}, u32[]{:S(2)}) collective-permute-start(bf16[288,256]{1,0:T(8,128)(2,1)S(1)} %get-tuple-element.22), channel_id=1, source_target_pairs={{0,2},{1,3},{2,4},{3,5},{4,6},{5,7},{6,0},{7,1},{8,10},{9,11},{10,... | collective-permute-start | bytes 442376 | tf_op jit(solution)/shard_map/ppermute | solution.py:464
  354.0 11.6 %collective-permute-start.61 = (bf16[288,256]{1,0:T(8,128)(2,1)S(1)}, bf16[288,256]{1,0:T(8,128)(2,1)S(1)}, u32[]{:S(2)}, u32[]{:S(2)}) collective-permute-start(bf16[288,256]{1,0:T(8,128)(2,1)S(1)} %collective-permute-done.60.refs_22_), channel_id=1, source_target_pairs={{0,8},{8,0},{16,24},{24,16},{1,9},{9,1},{17,25},{25,17},{2,10},{10... | collective-permute-start | bytes 442376 | tf_op jit(solution)/shard_map/ppermute | solution.py:46
  355.3 11.1 %collective-permute-start.62 = (bf16[288,256]{1,0:T(8,128)(2,1)S(1)}, bf16[288,256]{1,0:T(8,128)(2,1)S(1)}, u32[]{:S(2)}, u32[]{:S(2)}) collective-permute-start(bf16[288,256]{1,0:T(8,128)(2,1)S(1)} %collective-permute-done.60.refs_22_), channel_id=1, source_target_pairs={{0,16},{8,24},{16,0},{24,8},{1,17},{9,25},{17,1},{25,9},{2,18},{10... | collective-permute-start | bytes 442376 | tf_op jit(solution)/shard_map/ppermute | solution.py:46
  358.1 9.6 %collective-permute-start.66 = (bf16[288,256]{1,0:T(8,128)(2,1)S(1)}, bf16[288,256]{1,0:T(8,128)(2,1)S(1)}, u32[]{:S(2)}, u32[]{:S(2)}) collective-permute-start(bf16[288,256]{1,0:T(8,128)(2,1)S(1)} %collective-permute-done.64.refs_27_), channel_id=1, source_target_pairs={{0,8},{8,0},{16,24},{24,16},{1,9},{9,1},{17,25},{25,17},{2,10},{10... | collective-permute-start | bytes 442376 | tf_op jit(solution)/shard_map/ppermute | solution.py:46
  364.3 11.1 %collective-permute-start.54 = (bf16[288,256]{1,0:T(8,128)(2,1)S(1)}, bf16[288,256]{1,0:T(8,128)(2,1)S(1)}, u32[]{:S(2)}, u32[]{:S(2)}) collective-permute-start(bf16[288,256]{1,0:T(8,128)(2,1)S(1)} %collective-permute-done.52.refs_14_), channel_id=1, source_target_pairs={{0,16},{8,24},{16,0},{24,8},{1,17},{9,25},{17,1},{25,9},{2,18},{10... | collective-permute-start | bytes 442376 | tf_op jit(solution)/shard_map/ppermute | solution.py:46
  366.4 19.6 %collective-permute-start.38 = (bf16[576,256]{1,0:T(8,128)(2,1)S(1)}, bf16[576,256]{1,0:T(8,128)(2,1)S(1)}, u32[]{:S(2)}, u32[]{:S(2)}) collective-permute-start(bf16[576,256]{1,0:T(8,128)(2,1)S(1)} %constant_dynamic-update-slice_fusion.2.refs_10_), channel_id=1, source_target_pairs={{0,16},{8,24},{16,0},{24,8},{1,17},{9,25},{17,1},{25,9},{2,18},{10... | collective-permute-start | bytes 884744 | tf_op jit(solution)/shard_map/ppermute | solution.py:46
  367.7 19.8 %collective-permute-start.34 = (bf16[576,256]{1,0:T(8,128)(2,1)S(1)}, bf16[576,256]{1,0:T(8,128)(2,1)S(1)}, u32[]{:S(2)}, u32[]{:S(2)}) collective-permute-start(bf16[576,256]{1,0:T(8,128)(2,1)S(1)} %constant_dynamic-update-slice_fusion.refs_6_), channel_id=1, source_target_pairs={{0,8},{8,0},{16,24},{24,16},{1,9},{9,1},{17,25},{25,17},{2,10},{10... | collective-permute-start | bytes 884744 | tf_op jit(solution)/shard_map/ppermute | solution.py:46
  374.2 9.0 %collective-permute-start.63 = (bf16[288,256]{1,0:T(8,128)(2,1)S(1)}, bf16[288,256]{1,0:T(8,128)(2,1)S(1)}, u32[]{:S(2)}, u32[]{:S(2)}) collective-permute-start(bf16[288,256]{1,0:T(8,128)(2,1)S(1)} %collective-permute-done.61.refs_23_), channel_id=1, source_target_pairs={{0,16},{8,24},{16,0},{24,8},{1,17},{9,25},{17,1},{25,9},{2,18},{10... | collective-permute-start | bytes 442376 | tf_op jit(solution)/shard_map/ppermute | solution.py:46
  375.4 9.3 %collective-permute-start.55 = (bf16[288,256]{1,0:T(8,128)(2,1)S(1)}, bf16[288,256]{1,0:T(8,128)(2,1)S(1)}, u32[]{:S(2)}, u32[]{:S(2)}) collective-permute-start(bf16[288,256]{1,0:T(8,128)(2,1)S(1)} %collective-permute-done.53.refs_15_), channel_id=1, source_target_pairs={{0,16},{8,24},{16,0},{24,8},{1,17},{9,25},{17,1},{25,9},{2,18},{10... | collective-permute-start | bytes 442376 | tf_op jit(solution)/shard_map/ppermute | solution.py:46
  378.0 10.0 %collective-permute-start.59 = (bf16[288,256]{1,0:T(8,128)(2,1)S(1)}, bf16[288,256]{1,0:T(8,128)(2,1)S(1)}, u32[]{:S(2)}, u32[]{:S(2)}) collective-permute-start(bf16[288,256]{1,0:T(8,128)(2,1)S(1)} %collective-permute-done.57.refs_19_), channel_id=1, source_target_pairs={{0,8},{8,0},{16,24},{24,16},{1,9},{9,1},{17,25},{25,17},{2,10},{10... | collective-permute-start | bytes 442376 | tf_op jit(solution)/shard_map/ppermute | solution.py:46
  383.2 9.5 %collective-permute-start.39 = (bf16[576,256]{1,0:T(8,128)(2,1)S(1)}, bf16[576,256]{1,0:T(8,128)(2,1)S(1)}, u32[]{:S(2)}, u32[]{:S(2)}) collective-permute-start(bf16[576,256]{1,0:T(8,128)(2,1)S(1)} %constant_dynamic-update-slice_fusion.2.refs_10_), channel_id=1, source_target_pairs={{0,8},{8,0},{16,24},{24,16},{1,9},{9,1},{17,25},{25,17},{2,10},{10... | collective-permute-start | bytes 884744 | tf_op jit(solution)/shard_map/ppermute | solution.py:46
  384.8 9.9 %collective-permute-start.35 = (bf16[576,256]{1,0:T(8,128)(2,1)S(1)}, bf16[576,256]{1,0:T(8,128)(2,1)S(1)}, u32[]{:S(2)}, u32[]{:S(2)}) collective-permute-start(bf16[576,256]{1,0:T(8,128)(2,1)S(1)} %constant_dynamic-update-slice_fusion.refs_6_), channel_id=1, source_target_pairs={{0,16},{8,24},{16,0},{24,8},{1,17},{9,25},{17,1},{25,9},{2,18},{10... | collective-permute-start | bytes 884744 | tf_op jit(solution)/shard_map/ppermute | solution.py:46
  386.0 9.8 %collective-permute-start.40 = (bf16[576,256]{1,0:T(8,128)(2,1)S(1)}, bf16[576,256]{1,0:T(8,128)(2,1)S(1)}, u32[]{:S(2)}, u32[]{:S(2)}) collective-permute-start(bf16[576,256]{1,0:T(8,128)(2,1)S(1)} %collective-permute-done.38.refs_11_), channel_id=1, source_target_pairs={{0,8},{8,0},{16,24},{24,16},{1,9},{9,1},{17,25},{25,17},{2,10},{10... | collective-permute-start | bytes 884744 | tf_op jit(solution)/shard_map/ppermute | solution.py:46
  387.5 10.6 %collective-permute-start.36 = (bf16[576,256]{1,0:T(8,128)(2,1)S(1)}, bf16[576,256]{1,0:T(8,128)(2,1)S(1)}, u32[]{:S(2)}, u32[]{:S(2)}) collective-permute-start(bf16[576,256]{1,0:T(8,128)(2,1)S(1)} %collective-permute-done.34.refs_7_), channel_id=1, source_target_pairs={{0,16},{8,24},{16,0},{24,8},{1,17},{9,25},{17,1},{25,9},{2,18},{10... | collective-permute-start | bytes 884744 | tf_op jit(solution)/shard_map/ppermute | solution.py:46
  388.0 18.1 %collective-permute-start.68 = (bf16[256,1280]{1,0:T(8,128)(2,1)S(1)}, bf16[256,1280]{1,0:T(8,128)(2,1)S(1)}, u32[]{:S(2)}, u32[]{:S(2)}) collective-permute-start(bf16[256,1280]{1,0:T(8,128)(2,1)S(1)} %collective-permute-done.67.refs_0_), channel_id=1, source_target_pairs={{0,1},{1,0},{2,3},{3,2},{4,5},{5,4},{6,7},{7,6},{8,9},{9,8},{10,11... | collective-permute-start | bytes 1966088 | tf_op jit(solution)/shard_map/ppermute | solution.py:468
  (25 other events, 849.5 us)
